TPU v7x, 512 devices: a whole 4x4x16 slice. The times are simulated.
512 devices in a mesh: guide: 2 (over x_lo), seq: 32 (over x_hi, z), blk: 8 (over y, core).
Axes of the slice: x: 4 (x_hi: 2, x_lo: 2; x = x_hi * 2 + x_lo), y: 4, z: 16, core: 2. Of those that a mesh axis runs over, the one named last changes fastest.
Arguments:
- img_hidden: bfloat16 [2, 2, 2048, 3072], P('guide', None, 'seq', 'blk'), may hold values from -6 to 6
- img_query: bfloat16 [2, 2, 2048, 3072], P('guide', None, 'seq', 'blk')
- img_key: bfloat16 [2, 2, 2048, 3072], P('guide', None, 'seq', 'blk')
- img_value: bfloat16 [2, 2, 2048, 3072], P('guide', None, 'seq', 'blk'), may hold values from -6 to 6
- txt_key: bfloat16 [2, 2, 512, 3072], P('guide', None, 'seq', 'blk'), may hold values from -6 to 6
- txt_value: bfloat16 [2, 2, 512, 3072], P('guide', None, 'seq', 'blk'), may hold values from -6 to 6
- query_gain: float32 [128], replicated
- key_gain: float32 [2, 128], replicated
- gate: float32 [2, 2, 3072], P('guide', None, 'blk'), may hold values from -4 to 4
- proj_weight: bfloat16 [3072, 3072], P('blk'), may hold values from -0.15625 to 0.15625
- proj_bias: float32 [3072], P('blk'), may hold values from -3 to 3
- guidance: float32 [2], replicated, may hold values from 1.5 to 5
- text_len: int32 [2], replicated, may hold values from 1 to 512, as said below
- step_index: int32 [1], replicated, may hold values from 0 to 7
- latent: bfloat16 [2, 2048, 3072], P('guide', 'seq', 'blk'), may hold values from -6 to 6
Outputs:
- guided: bfloat16 [2, 2048, 3072], P('guide', 'seq', 'blk')
- next_state: bfloat16 [2, 2048, 3072], P('guide', 'seq', 'blk')
Inputs may be any that keep to these rules, and one draw needn't show every extreme that they name: `text_len`: some prompt has all 512 text slots live.
All inputs are finite; a program needn't handle non-finite values.
Results may differ from a plain program's by a relative error of at most 0.0095.
Values may be sent and summed in bfloat16 or wider, within the bound.
No kernel may reach another device: no remote copies, remote signals or barrier semaphores. Data moves between devices by JAX's collectives and lax.ppermute only.
A program may use at most 64 MiB of HBM per device.

v0:
```python
import jax
import jax.numpy as jnp
from jax import lax
from jax.sharding import PartitionSpec as P

HD = 128
GRID = 64
STEPS = 8


def rope_angles(positions):
    first = HD // 8
    second = (HD - first) // 2
    freqs = 10000.0 ** (-jnp.arange(0, second, 2).astype(jnp.float32) / second)
    rows = (positions // GRID).astype(jnp.float32)
    cols = (positions % GRID).astype(jnp.float32)
    zeros = jnp.zeros((positions.shape[0], first // 2), jnp.float32)
    return jnp.concatenate([zeros, rows[:, None] * freqs, cols[:, None] * freqs], -1)


def rotate(values, angles):
    pairs = values.reshape(values.shape[:-1] + (HD // 2, 2))
    cosine = jnp.cos(angles)[None, :, None, :]
    sine = jnp.sin(angles)[None, :, None, :]
    first = pairs[..., 0] * cosine - pairs[..., 1] * sine
    second = pairs[..., 0] * sine + pairs[..., 1] * cosine
    return jnp.stack([first, second], -1).reshape(values.shape)


def normed(values, gain_row):
    heads = values.astype(jnp.float32).reshape(
        values.shape[0], values.shape[1], values.shape[2] // HD, HD
    )
    return heads / jnp.sqrt(jnp.mean(heads * heads, -1, keepdims=True) + 1e-06) * gain_row


def shards(
    img_hidden,
    img_query,
    img_key,
    img_value,
    txt_key,
    txt_value,
    query_gain,
    key_gain,
    gate,
    proj_weight,
    proj_bias,
    guidance,
    text_len,
    step_index,
    latent,
):
    prompts = img_query.shape[1]
    img_here = img_query.shape[2]
    txt_here = txt_key.shape[2]
    width_here = img_query.shape[3]
    heads_here = width_here // HD
    slot_here = img_here + txt_here
    positions = lax.axis_index("seq") * img_here + jnp.arange(img_here)
    angles = rope_angles(positions)
    queries = rotate(normed(img_query[0], query_gain), angles).astype(jnp.bfloat16)
    keys_img = rotate(normed(img_key[0], key_gain[0]), angles).astype(jnp.bfloat16)
    keys_txt = normed(txt_key[0], key_gain[1]).astype(jnp.bfloat16)
    keys_local = jnp.concatenate([keys_txt, keys_img], 1).reshape(prompts, slot_here, width_here)
    values_local = jnp.concatenate([txt_value[0], img_value[0]], 1)
    running = jnp.full((prompts, img_here, heads_here), -1e30, jnp.float32)
    key_piece = lax.all_gather(keys_local, "seq", axis=1, tiled=True)
    value_piece = lax.all_gather(values_local, "seq", axis=1, tiled=True)
    count = key_piece.shape[1]
    index = jnp.arange(count)
    device = index // slot_here
    within = index % slot_here
    text_pos = device * txt_here + within
    live = (within >= txt_here)[None, :] | (text_pos[None, :] < text_len[:, None])
    key_heads = key_piece.reshape(prompts, count, heads_here, HD)
    value_heads = value_piece.reshape(prompts, count, heads_here, HD)
    scores = jnp.einsum(
        "pqhd,pkhd->pqhk", queries, key_heads, preferred_element_type=jnp.float32
    ) * HD ** (-0.5)
    mask = live[:, None, None, :]
    scores = jnp.where(mask, scores, -1e30)
    newest = jnp.maximum(running, jnp.max(scores, -1))
    expo = jnp.where(mask, jnp.exp(scores - newest[..., None]), 0.0)
    total = jnp.sum(expo, -1)
    accum = jnp.einsum(
        "pqhk,pkhd->pqhd",
        expo.astype(jnp.bfloat16),
        value_heads,
        preferred_element_type=jnp.float32,
    )
    running, total, accum = (newest, total, accum)
    attn = (accum / total[..., None]).astype(jnp.bfloat16).reshape(prompts * img_here, width_here)
    partial_value = jnp.dot(attn, proj_weight, preferred_element_type=jnp.float32)
    proj = lax.psum_scatter(
        partial_value.astype(jnp.bfloat16), "blk", scatter_dimension=1, tiled=True
    ).astype(jnp.float32)
    proj = (proj + proj_bias).reshape(prompts, img_here, width_here)
    layer_out = (img_hidden[0].astype(jnp.float32) + gate[0][:, None, :] * proj).astype(
        jnp.bfloat16
    )
    both_halves = lax.all_to_all(layer_out[None], "guide", split_axis=1, concat_axis=0, tiled=True)
    cond = both_halves[0].astype(jnp.float32)
    uncond = both_halves[1].astype(jnp.float32)
    own_prompts = cond.shape[0]
    scale_here = lax.dynamic_slice_in_dim(
        guidance, lax.axis_index("guide") * own_prompts, own_prompts, 0
    )
    guided_f = uncond + scale_here[:, None, None] * (cond - uncond)
    index = step_index[0]
    u_now = 1.0 - index.astype(jnp.float32) / STEPS
    u_next = 1.0 - (index + 1).astype(jnp.float32) / STEPS
    step_size = 3.0 * u_next / (1.0 + 2.0 * u_next) - 3.0 * u_now / (1.0 + 2.0 * u_now)
    next_state = (latent.astype(jnp.float32) + step_size * guided_f).astype(jnp.bfloat16)
    return (guided_f.astype(jnp.bfloat16), next_state)


def solution(mesh):
    return jax.shard_map(
        shards,
        mesh=mesh,
        in_specs=(
            P("guide", None, "seq", "blk"),
            P("guide", None, "seq", "blk"),
            P("guide", None, "seq", "blk"),
            P("guide", None, "seq", "blk"),
            P("guide", None, "seq", "blk"),
            P("guide", None, "seq", "blk"),
            P(),
            P(),
            P("guide", None, "blk"),
            P("blk", None),
            P("blk"),
            P(),
            P(),
            P(),
            P("guide", "seq", "blk"),
        ),
        out_specs=(P("guide", "seq", "blk"), P("guide", "seq", "blk")),
        check_vma=False,
    )
```

profile of v0, /device:TPU:1, one launch (start us, length us, event | category | flops | bytes accessed | tf_op | source)
XLA Modules:
  0.0 418.7 jit_solution(10959240967538015908)
XLA Ops:
  7.8 1.6 convert_multiply_fusion.1
  9.5 1.0 copy.58
  10.5 1.6 convert_multiply_fusion.2
  12.1 1.0 copy.52
  13.7 0.8 slice_bitcast_fusion.2
  14.6 1.0 mul.267
  15.9 0.7 copy.54
  16.6 1.0 mul.285
  17.8 0.7 copy.60
  18.5 0.8 mul.286
  19.3 0.7 convert_multiply_fusion
  20.6 0.8 broadcast_multiply_fusion.1
  21.5 1.1 divide_multiply_fusion
  22.7 1.0 subtract_convert_fusion
  24.4 0.8 copy.56
  25.4 0.8 copy.83
  26.1 0.8 pad_maximum_fusion.3
  27.6 0.7 compare_or_fusion
  28.3 156.8 %all-gather.5.cloned.1.call-done = bf16[2,2560,384]{2,0,1:T(2,128)(2,1)} async-done(((bf16[2,80,384]{2,0,1:T(2,128)(2,1)}), bf16[2,2560,384]{2,0,1:T(2,128)(2,1)}) %all-gather.5.cloned.1.call-update) | async-done | bytes 3932176 | tf_op jit(solution)/shard_map/all_gather | solution.py:68
  185.1 10.5 %copy.57 = bf16[2,2560,384]{1,2,0:T(8,128)(2,1)} copy(bf16[2,2560,384]{2,0,1:T(2,128)(2,1)} %all-gather.5.cloned.1.call-done) | data formatting | bytes 7864320 | tf_op jit(solution)/shard_map/all_gather | solution.py:68
  195.7 3.2 fusion.38
  198.9 1.9 copy-done.1
  200.8 0.9 fusion.2
  201.7 143.6 %all-gather.3.cloned.1.call-done = bf16[2,2560,384]{2,0,1:T(2,128)(2,1)} async-done(((bf16[2,80,384]{2,0,1:T(2,128)(2,1)}), bf16[2,2560,384]{2,0,1:T(2,128)(2,1)}) %all-gather.3.cloned.1.call-update) | async-done | bytes 3932176 | tf_op jit(solution)/shard_map/all_gather | solution.py:69
  345.3 10.5 %copy.51 = bf16[2,2560,384]{1,2,0:T(8,128)(2,1)} copy(bf16[2,2560,384]{2,0,1:T(2,128)(2,1)} %all-gather.3.cloned.1.call-done) | data formatting | bytes 7864320 | tf_op jit(solution)/shard_map/all_gather | solution.py:69
  355.9 4.8 %fusion.15 = bf16[2,64,3,128]{3,1,2,0:T(8,128)(2,1)S(1)} fusion(bf16[2,2560,3,128]{1,3,2,0:T(8,128)(2,1)} %bitcast.73, f32[2,64,3,2560]{3,1,2,0:T(8,128)} %copy-done.1, f32[2,64,3]{1,2,0:T(4,128)S(1)} %broadcast_maximum_fusion, pred[2,2560]{1,0:T(4,128)(4,1)S(1)} %compare_or_fusion, f32[2,64,3]{1,2,0:T(4,128)S(1)} %fusion.2), kind=kOutput, calls=%fused_computation.13 | convolution fusion | flops 254705664 | bytes 7970816 | tf_op jit(solution)/shard_map/pqhk,pkhd->pqhd/dot_general | solution.py:86
  361.4 1.2 copy.69
  362.6 40.1 %reduce-scatter.4.cloned.1.call-done = bf16[384,128]{1,0:T(8,128)(2,1)} async-done(((bf16[3072,128]{1,0:T(8,128)(2,1)}), bf16[384,128]{1,0:T(8,128)(2,1)}) %reduce-scatter.4.cloned.1.call-update) | async-done | bytes 98320
  402.7 1.0 copy.70
  404.4 3.3 all-to-all-start
  409.1 1.7 all-to-all-done
  410.9 1.3 add_convert_fusion.3
  (53 shorter events, 5.9 us)
Async XLA Ops:
  7.2 353.7 %copy-start = (bf16[384,3072]{1,0:T(8,128)(2,1)S(1)}, bf16[384,3072]{1,0:T(8,128)(2,1)}, u32[]{:S(2)}) copy-start(bf16[384,3072]{1,0:T(8,128)(2,1)} %param.24) | copy-start | bytes 7077892
  7.2 13.2 %copy-start.4 = (bf16[1,2,16,384]{3,2,1,0:T(8,128)(2,1)S(1)}, bf16[1,2,16,384]{3,2,1,0:T(8,128)(2,1)}, u32[]{:S(2)}) copy-start(bf16[1,2,16,384]{3,2,1,0:T(8,128)(2,1)} %param.19) | copy-start | bytes 73732
  7.2 177.9 %all-gather.5.cloned.1.call-start = ((), (), s32[]{:S(2)}) async-start(), calls=%async_computation.3 | async-start | bytes 4055040 | tf_op jit(solution)/shard_map/all_gather | solution.py:68
  17.8 7.4 %copy-start.2 = (bf16[1,2,64,384]{3,2,1,0:T(8,128)(2,1)S(1)}, bf16[1,2,64,384]{3,2,1,0:T(8,128)(2,1)}, u32[]{:S(2)}) copy-start(bf16[1,2,64,384]{3,2,1,0:T(8,128)(2,1)} %param.18) | copy-start | bytes 294916
  25.2 320.1 %all-gather.3.cloned.1.call-start = ((), (), s32[]{:S(2)}) async-start(), calls=%async_computation.2 | async-start | bytes 4055040 | tf_op jit(solution)/shard_map/all_gather | solution.py:69
  27.0 375.7 %reduce-scatter.4.cloned.1.call-start = ((), (), s32[]{:S(2)}) async-start(), calls=%async_computation.4 | async-start | bytes 884736
  198.9 1.9 copy-start.1
  360.7 43.0 %copy-start.7 = (f32[384]{0:T(512)S(1)}, f32[384]{0:T(512)}, u32[]{:S(2)}) copy-start(f32[384]{0:T(512)} %param.25) | copy-start | bytes 4612
  360.7 43.0 %copy-start.3 = (bf16[1,2,64,384]{3,2,1,0:T(8,128)(2,1)S(1)}, bf16[1,2,64,384]{3,2,1,0:T(8,128)(2,1)}, u32[]{:S(2)}) copy-start(bf16[1,2,64,384]{3,2,1,0:T(8,128)(2,1)} %param.15) | copy-start | bytes 294916
  360.7 43.0 %copy-start.6 = (f32[1,2,384]{2,1,0:T(2,128)S(1)}, f32[1,2,384]{2,1,0:T(2,128)}, u32[]{:S(2)}) copy-start(f32[1,2,384]{2,1,0:T(2,128)} %param.23) | copy-start | bytes 9220
  360.7 47.7 %copy-start.8 = (f32[2]{0:T(128)S(1)}, f32[2]{0:T(128)}, u32[]{:S(2)}) copy-start(f32[2]{0:T(128)} %param.26) | copy-start | bytes 28
  360.7 50.1 %copy-start.5 = (bf16[1,64,384]{2,1,0:T(8,128)(2,1)S(1)}, bf16[1,64,384]{2,1,0:T(8,128)(2,1)}, u32[]{:S(2)}) copy-start(bf16[1,64,384]{2,1,0:T(8,128)(2,1)} %param.29) | copy-start | bytes 147460
  404.4 6.5 %all-to-all-start = ((bf16[1,2,64,384]{3,2,0,1:T(8,128)(2,1)}), bf16[1,2,64,384]{3,2,0,1:T(8,128)(2,1)S(1)}, u32[]{:S(2)}, u32[]{:S(2)}) async-start(bf16[1,2,64,384]{3,2,0,1:T(8,128)(2,1)} %add_convert_fusion), calls=%async_computation | async-start | bytes 196608 | tf_op jit(solution)/shard_map/all_to_all | solution.py:102
Sparse Core Ops, SparseCore 0:
  25.3 159.7 all-gather.4
  188.2 157.0 all-gather.2
  362.7 39.8 reduce-scatter.3
where the time goes:
time: 422 us; the launch traced here: 419 us
  waiting for transfers between devices  342 us (81%)
  local copies, waits for them, and re-layouts  35 us (8%)
  between operations  14.9 us (4%)
  other arithmetic  14.5 us (3%)
  matrix products  8.62 us (2%)
    all_gather x1, waiting for transfers between devices, shards(): key_piece = lax.all_gather(keys_local, 'seq', axis=1, tiled=True)  157 us
    all_gather x1, waiting for transfers between devices, shards(): value_piece = lax.all_gather(values_local, 'seq', axis=1, tiled=True)  144 us
    unnamed x4, waiting for transfers between devices  40.1 us
    all_gather x1, local copies, waits for them, and re-layouts, shards(): key_piece = lax.all_gather(keys_local, 'seq', axis=1, tiled=True)  10.5 us
    all_gather x1, local copies, waits for them, and re-layouts, shards(): value_piece = lax.all_gather(values_local, 'seq', axis=1, tiled=True)  10.5 us
  transfers between devices with their start and end apart: 4, of which 4 were waited for; matrix products, arithmetic and copies ran while one was open for 4% of the time, Pallas kernels for 0%

commit v1 on v0

v1 whole, which is shorter than its diff:
```python
import functools

import jax
import jax.numpy as jnp
import numpy as np
from jax import lax
from jax.experimental import pallas as pl
from jax.experimental.pallas import tpu as pltpu
from jax.sharding import Mesh, PartitionSpec as P

HD = 128
GRID = 64
STEPS = 8
HPD = 3
W = HPD * HD
TQ = 64
TT = 16
TK = TQ + TT
NZ = 4
NS = 8
STAT = 8
BF = jnp.bfloat16
F32 = jnp.float32
VMEM_LIMIT = 48 * 1024 * 1024


def rope_tables():
    first = HD // 8
    second = (HD - first) // 2
    freqs = 10000.0 ** (-np.arange(0, second, 2).astype(np.float64) / second)
    n = freqs.shape[0]
    lane = np.arange(HD)
    pair = lane // 2
    sign = np.where(lane % 2 == 0, -1.0, 1.0)
    row_f = np.where((pair >= first // 2) & (pair < first // 2 + n), freqs[np.clip(pair - first // 2, 0, n - 1)], 0.0)
    col_f = np.where(pair >= first // 2 + n, freqs[np.clip(pair - first // 2 - n, 0, n - 1)], 0.0)
    rows = np.arange(32)[:, None] * row_f[None]
    cols = np.arange(GRID)[:, None] * col_f[None]
    return (
        np.stack([np.cos(rows), np.sin(rows) * sign]).astype(np.float32),
        np.stack([np.cos(cols), np.sin(cols) * sign]).astype(np.float32),
    )


def split3(x):
    hi = x.astype(BF)
    rest = x - hi.astype(F32)
    mid = rest.astype(BF)
    lo = (rest - mid.astype(F32)).astype(BF)
    return hi, mid, lo


def prepare_kernel(
    ids, q_ref, k_ref, v_ref, tk_ref, tv_ref, qg_ref, kg_ref, row_ref, col_ref, hid_ref, gate_ref, kv_out, q_out, side_out
):
    seq = ids[0]
    other = ids[1]
    lane = lax.broadcasted_iota(jnp.int32, (TQ, HD), 1)
    even = lane % 2 == 0
    in_row = lane < 72
    cos_t = jnp.where(in_row, row_ref[0, pl.ds(seq, 1), :], col_ref[0])
    sin_t = jnp.where(in_row, row_ref[1, pl.ds(seq, 1), :], col_ref[1])

    def normed(x, gain):
        x = x.astype(F32)
        return x * lax.rsqrt(jnp.mean(x * x, -1, keepdims=True) + 1e-06) * gain

    def rotated(x):
        swapped = jnp.where(even, pltpu.roll(x, HD - 1, 1), pltpu.roll(x, 1, 1))
        return x * cos_t + swapped * sin_t

    for p in range(2):
        for h in range(HPD):
            hs = slice(h * HD, (h + 1) * HD)
            q = rotated(normed(q_ref[p, :, hs], qg_ref[...])).astype(BF)
            k = rotated(normed(k_ref[p, :, hs], kg_ref[0:1])).astype(BF)
            t = normed(tk_ref[p, :, hs], kg_ref[1:2]).astype(BF)
            for z in range(NZ):
                q_out[p * NZ + z, :, hs] = q
                kv_out[p * NZ + z, 0, 0:TT, hs] = t
                kv_out[p * NZ + z, 0, TT:TK, hs] = k
        for z in range(NZ):
            kv_out[p * NZ + z, 1, 0:TT, :] = tv_ref[p]
            kv_out[p * NZ + z, 1, TT:TK, :] = v_ref[p]
    side_out[0:TQ, :] = hid_ref[other]
    hi, mid, lo = split3(gate_ref[pl.ds(other, 1), :])
    rows = lax.broadcasted_iota(jnp.int32, (8, W), 0)
    packed = jnp.where(rows == 0, hi.astype(F32), jnp.where(rows == 1, mid.astype(F32), lo.astype(F32)))
    side_out[TQ : TQ + 8, :] = packed.astype(BF)


def attend_kernel(q_ref, kv_ref, bias_ref, out_ref):
    scale = HD ** (-0.5) * 1.4426950408889634
    lane = lax.broadcasted_iota(jnp.int32, (NS * TQ, HD), 1)
    stats = jnp.zeros((NS * TQ, HD), F32)
    for h in range(HPD):
        hs = slice(h * HD, (h + 1) * HD)
        q = q_ref[:, :, hs].reshape(NS * TQ, HD)
        k = kv_ref[:, 0, :, hs].reshape(NS * TK, HD)
        v = kv_ref[:, 1, :, hs].reshape(NS * TK, HD)
        s = lax.dot_general(q, k, (((1,), (1,)), ((), ())), preferred_element_type=F32)
        s = s * scale + bias_ref[...]
        top = jnp.max(s, -1, keepdims=True)
        e = jnp.exp2(s - top)
        total = jnp.sum(e, -1, keepdims=True)
        o = jnp.dot(e.astype(BF), v, preferred_element_type=F32) / total
        out_ref[:, 0:TQ, hs] = o.astype(BF).reshape(NS, TQ, HD)
        lse = top + jnp.log2(total)
        hi = lse.astype(BF).astype(F32)
        stats = jnp.where(lane == h, hi, jnp.where(lane == HPD + h, lse - hi, stats))
    rows = jnp.transpose(stats)[0:STAT, :].astype(BF)
    for d in range(NS):
        a = (d // 2) * HD
        out_ref[d, TQ : TQ + STAT, 0:HD] = rows[:, a : a + HD]
        out_ref[d, TQ : TQ + STAT, HD:W] = jnp.zeros((STAT, W - HD), BF)


def project_kernel(ids, o_ref, w_ref, out_ref, attn_ref):
    odd = ids[0]
    stats = o_ref[:, TQ : TQ + STAT, 0:HD].astype(F32).reshape(NS * STAT, HD)
    cols = jnp.transpose(jnp.concatenate([stats, stats], 0))
    cols = jnp.where(odd == 0, cols[0:TQ], cols[TQ : 2 * TQ])
    for p in range(2):
        for h in range(HPD):
            hs = slice(h * HD, (h + 1) * HD)
            lses = []
            for z in range(NZ):
                at = (p * NZ + z) * STAT + h
                lses.append(cols[:, at : at + 1] + cols[:, at + HPD : at + HPD + 1])
            top = functools.reduce(jnp.maximum, lses)
            ws = [jnp.exp2(x - top) for x in lses]
            total = functools.reduce(jnp.add, ws)
            acc = jnp.zeros((TQ, HD), F32)
            for z in range(NZ):
                acc = acc + ws[z] * o_ref[p * NZ + z, 0:TQ, hs].astype(F32)
            attn_ref[p * TQ : (p + 1) * TQ, hs] = (acc / total).astype(BF)
    attn = attn_ref[...]
    for b in range(8):
        part = jnp.dot(attn, w_ref[:, b * W : (b + 1) * W], preferred_element_type=F32).astype(BF)
        out_ref[b] = part[0:TQ]
        out_ref[8 + b] = part[TQ : 2 * TQ]


def finish_kernel(ids, scal, part_ref, hid_ref, gate_ref, side_ref, bias_ref, lat_ref, guided_ref, next_ref):
    mine = ids[0]
    mine_f = mine.astype(F32)
    outs = []
    other_gate = (
        side_ref[TQ : TQ + 1, :].astype(F32) + side_ref[TQ + 1 : TQ + 2, :].astype(F32)
    ) + side_ref[TQ + 2 : TQ + 3, :].astype(F32)
    for g in range(2):
        acc = part_ref[g * 8].astype(F32)
        for b in range(1, 8):
            acc = acc + part_ref[g * 8 + b].astype(F32)
        own = mine == g
        hidden = jnp.where(own, hid_ref[mine].astype(F32), side_ref[0:TQ, :].astype(F32))
        gate = jnp.where(own, gate_ref[pl.ds(mine, 1), :], other_gate)
        outs.append((hidden + gate * (acc + bias_ref[...])).astype(BF).astype(F32))
    cond, uncond = outs
    guided = uncond + scal[0] * (cond - uncond)
    guided_ref[0] = guided.astype(BF)
    next_ref[0] = (lat_ref[0].astype(F32) + scal[1] * guided).astype(BF)


SMEM = functools.partial(pl.BlockSpec, memory_space=pltpu.SMEM)
VMEM = functools.partial(pl.BlockSpec, memory_space=pltpu.VMEM)


def call(kernel, outs, n_smem, n_vmem, name, scratch=()):
    return pl.pallas_call(
        kernel,
        out_shape=outs,
        in_specs=[SMEM()] * n_smem + [VMEM()] * n_vmem,
        out_specs=jax.tree.map(lambda _: VMEM(), outs),
        scratch_shapes=list(scratch),
        compiler_params=pltpu.CompilerParams(vmem_limit_bytes=VMEM_LIMIT),
        name=name,
    )


def shards(
    img_hidden,
    img_query,
    img_key,
    img_value,
    txt_key,
    txt_value,
    query_gain,
    key_gain,
    gate,
    proj_weight,
    proj_bias,
    guidance,
    text_len,
    step_index,
    latent,
):
    guide = lax.axis_index("g")
    xh = lax.axis_index("xh")
    z1 = lax.axis_index("z1")
    z0 = lax.axis_index("z0")
    seq = (xh * NZ + z1) * NZ + z0
    rows, cols = rope_tables()
    kv, q, side = call(
        prepare_kernel,
        (
            jax.ShapeDtypeStruct((NS, 2, TK, W), BF),
            jax.ShapeDtypeStruct((NS, TQ, W), BF),
            jax.ShapeDtypeStruct((TQ + 8, W), BF),
        ),
        1,
        11,
        "prepare",
    )(
        jnp.stack([seq, 1 - guide]),
        img_query[0],
        img_key[0],
        img_value[0],
        txt_key[0],
        txt_value[0],
        query_gain[None],
        key_gain,
        jnp.asarray(rows),
        jnp.asarray(cols),
        img_hidden[0],
        gate[0],
    )
    side = lax.ppermute(side, "g", [(0, 1), (1, 0)])
    q = lax.all_to_all(q, ("xh", "z1"), 0, 0, tiled=True)
    kv = lax.all_to_all(kv, ("xh", "z0"), 0, 0, tiled=True)

    src = jnp.arange(NS)
    src_seq = ((src // NZ) * NZ + z1) * NZ + src % NZ
    within = jnp.arange(TK)
    pos = src_seq[:, None] * TT + within[None, :]
    live = (within >= TT)[None, :] | (pos < text_len[xh])
    bias = jnp.where(live, 0.0, -1e30).astype(F32).reshape(1, NS * TK)
    out = call(attend_kernel, jax.ShapeDtypeStruct((NS, TQ + STAT, W), BF), 0, 3, "attend")(q, kv, bias)
    out = lax.all_to_all(out, ("xh", "z1"), 0, 0, tiled=True)
    part = call(
        project_kernel,
        jax.ShapeDtypeStruct((16, TQ, W), BF),
        1,
        2,
        "project",
        [pltpu.VMEM((2 * TQ, W), BF)],
    )((z1 % 2)[None], out, proj_weight)
    part = lax.all_to_all(part, ("g", "y", "c"), 0, 0, tiled=True)
    index = step_index[0]
    u_now = 1.0 - index.astype(F32) / STEPS
    u_next = 1.0 - (index + 1).astype(F32) / STEPS
    step = 3.0 * u_next / (1.0 + 2.0 * u_next) - 3.0 * u_now / (1.0 + 2.0 * u_now)
    shape = jax.ShapeDtypeStruct((1, TQ, W), BF)
    return call(finish_kernel, (shape, shape), 2, 6, "finish")(
        guide[None],
        jnp.stack([guidance[guide], step]),
        part,
        img_hidden[0],
        gate[0],
        side,
        proj_bias[None],
        latent,
    )


def solution(mesh):
    fine = Mesh(mesh.devices.reshape(2, 2, NZ, NZ, 4, 2), ("g", "xh", "z1", "z0", "y", "c"))
    seq = ("xh", "z1", "z0")
    blk = ("y", "c")
    act = P("g", None, seq, blk)
    return jax.shard_map(
        shards,
        mesh=fine,
        in_specs=(
            act,
            act,
            act,
            act,
            act,
            act,
            P(),
            P(),
            P("g", None, blk),
            P(blk, None),
            P(blk),
            P(),
            P(),
            P(),
            P("g", seq, blk),
        ),
        out_specs=(P("g", seq, blk), P("g", seq, blk)),
        check_vma=False,
    )
```

time: 422 us -> 143 us (0.34)
  the two profiles are of different devices: /device:TPU:1 before, /device:TPU:64 now
where the time goes in v1:
time: 143 us; the launch traced here: 142 us
  waiting for transfers between devices  53.6 us (37%)
  blocking collectives  45.2 us (32%)
  starting transfers between devices  19.9 us (14%)
  local copies, waits for them, and re-layouts  12.7 us (9%)
  Pallas kernels  7.65 us (5%)
  other arithmetic  1.53 us (1%)
  between operations  1.5 us (1%)
    all_to_all x1, blocking collectives, shards(): q = lax.all_to_all(q, ('xh', 'z1'), 0, 0, tiled=True)  45.2 us
    all_to_all x1, waiting for transfers between devices, shards(): out = lax.all_to_all(out, ('xh', 'z1'), 0, 0, tiled=True)  27.1 us
    all_to_all x1, waiting for transfers between devices, shards(): kv = lax.all_to_all(kv, ('xh', 'z0'), 0, 0, tiled=True)  18.2 us
    unnamed x42, local copies, waits for them, and re-layouts  11.4 us
    all_to_all x1, starting transfers between devices, shards(): out = lax.all_to_all(out, ('xh', 'z1'), 0, 0, tiled=True)  7.17 us
    ppermute x1, waiting for transfers between devices, shards(): side = lax.ppermute(side, 'g', [(0, 1), (1, 0)])  6.87 us
    all_to_all x1, starting transfers between devices, shards(): part = lax.all_to_all(part, ('g', 'y', 'c'), 0, 0, tiled=True)  4.61 us
    all_to_all x1, starting transfers between devices, shards(): kv = lax.all_to_all(kv, ('xh', 'z0'), 0, 0, tiled=True)  4.33 us
  transfers between devices with their start and end apart: 4, of which 4 were waited for; matrix products, arithmetic and copies ran while one was open for 2% of the time, Pallas kernels for 0%

profile of v1, /device:TPU:64, one launch (start us, length us, event | category | flops | bytes accessed | tf_op | source)
XLA Modules:
  0.0 142.0 jit_solution(5434282957547105589)
XLA Ops:
  0.7 0.9 copy-done.4
  1.6 0.9 copy-done.6
  2.5 0.9 copy-done.7
  3.4 0.9 copy-done.8
  4.3 0.8 copy-done.9
  5.1 0.8 copy-done.11
  5.9 0.7 copy-done.12
  6.6 0.7 copy-done.13
  7.4 0.7 copy-done.14
  8.1 0.7 copy-done.16
  8.7 0.7 copy-done.17
  9.4 1.8 %prepare.1 = (bf16[8,2,80,384]{3,2,1,0:T(8,128)(2,1)S(1)}, bf16[8,64,384]{2,1,0:T(8,128)(2,1)S(1)}, bf16[72,384]{1,0:T(8,128)(2,1)S(1)}) custom-call(s32[2]{0:T(128)S(1)} %pad_add_fusion.ids, bf16[2,64,384]{2,1,0:T(8,128)(2,1)S(1)} %bitcast.15, bf16[2,64,384]{2,1,0:T(8,128)(2,1)S(1)} %bitcast.16, bf16[2,64,384]{2,1,0:T(8,128)(2,1)S(1)} %bitcast.17, ...), custom_call_target="tpu_custom_call" | custom-call | tf_op jit(solution)/shard_map/prepare/pallas_call | solution.py:204
  11.3 1.0 copy-done.3
  12.2 45.2 %all_to_all.20.q_ref = bf16[8,64,384]{2,1,0:T(8,128)(2,1)} all-to-all(bf16[8,64,384]{2,1,0:T(8,128)(2,1)S(1)} %get-tuple-element.5), channel_id=1, replica_groups=mesh['g'=2,'xh'=2,'z1'=4,'z0'=4,'y'=4,'c'=2] {'xh','z1'}, dimensions={0} | all-to-all | bytes 786432 | tf_op jit(solution)/shard_map/all_to_all | solution.py:229
  57.4 4.3 %all-to-all-start.1 = ((bf16[8,2,80,384]{3,2,1,0:T(8,128)(2,1)}), bf16[8,2,80,384]{3,2,1,0:T(8,128)(2,1)S(1)}, u32[]{:S(2)}, u32[]{:S(2)}) async-start(bf16[8,2,80,384]{3,2,1,0:T(8,128)(2,1)} %copy-done.3), calls=%async_computation.1 | async-start | bytes 1966080 | tf_op jit(solution)/shard_map/all_to_all | solution.py:230
  61.7 0.6 dynamic_slice.7
  62.3 0.7 fusion.1
  63.0 0.1 select_n.52.bias_ref
  63.1 18.2 %all-to-all-done.1.kv_ref = bf16[8,2,80,384]{3,2,1,0:T(8,128)(2,1)S(1)} async-done(((bf16[8,2,80,384]{3,2,1,0:T(8,128)(2,1)}), bf16[8,2,80,384]{3,2,1,0:T(8,128)(2,1)S(1)}, u32[]{:S(2)}, u32[]{:S(2)}) %all-to-all-start.1) | async-done | bytes 983072 | tf_op jit(solution)/shard_map/all_to_all | solution.py:230
  81.3 1.0 copy-done.2
  82.3 2.2 %attend.1 = bf16[8,72,384]{2,1,0:T(8,128)(2,1)S(1)} custom-call(bf16[8,64,384]{2,1,0:T(8,128)(2,1)S(1)} %copy-done.2, bf16[8,2,80,384]{3,2,1,0:T(8,128)(2,1)S(1)} %all-to-all-done.1.kv_ref, f32[1,640]{1,0:T(1,128)S(1)} %select_n.52.bias_ref), custom_call_target="tpu_custom_call" | custom-call | tf_op jit(solution)/shard_map/attend/pallas_call | solution.py:238
  84.5 0.8 copy-done.1
  85.3 7.2 %all-to-all-start.2 = ((bf16[8,72,384]{2,1,0:T(8,128)(2,1)}), bf16[8,72,384]{2,1,0:T(8,128)(2,1)S(1)}, u32[]{:S(2)}, u32[]{:S(2)}) async-start(bf16[8,72,384]{2,1,0:T(8,128)(2,1)} %copy-done.1), calls=%async_computation.2 | async-start | bytes 884736 | tf_op jit(solution)/shard_map/all_to_all | solution.py:239
  92.4 27.1 %all-to-all-done.2.o_ref = bf16[8,72,384]{2,1,0:T(8,128)(2,1)S(1)} async-done(((bf16[8,72,384]{2,1,0:T(8,128)(2,1)}), bf16[8,72,384]{2,1,0:T(8,128)(2,1)S(1)}, u32[]{:S(2)}, u32[]{:S(2)}) %all-to-all-start.2) | async-done | bytes 442400 | tf_op jit(solution)/shard_map/all_to_all | solution.py:239
  119.5 2.3 %project.1 = bf16[16,64,384]{2,1,0:T(8,128)(2,1)} custom-call(s32[1]{0:T(128)} %bitcast.1.ids, bf16[8,72,384]{2,1,0:T(8,128)(2,1)S(1)} %all-to-all-done.2.o_ref, bf16[384,3072]{1,0:T(8,128)(2,1)S(1)} %copy-done), custom_call_target="tpu_custom_call" | custom-call | tf_op jit(solution)/shard_map/project/pallas_call | solution.py:240
  121.8 4.6 %all-to-all-start.3 = ((bf16[16,64,384]{2,1,0:T(8,128)(2,1)}), bf16[16,64,384]{2,1,0:T(8,128)(2,1)S(1)}, u32[]{:S(2)}, u32[]{:S(2)}) async-start(bf16[16,64,384]{2,1,0:T(8,128)(2,1)} %project.1), calls=%async_computation.3 | async-start | bytes 1572864 | tf_op jit(solution)/shard_map/all_to_all | solution.py:248
  126.5 3.8 %collective-permute-start = (bf16[72,384]{1,0:T(8,128)(2,1)S(1)}, bf16[72,384]{1,0:T(8,128)(2,1)S(1)}, u32[]{:S(2)}, u32[]{:S(2)}) collective-permute-start(bf16[72,384]{1,0:T(8,128)(2,1)S(1)} %get-tuple-element.7), channel_id=1, source_target_pairs={{0,256},{256,0},{1,257},{257,1},{2,258},{258,2},{3,259},{259,3},{4... | collective-permute-start | bytes 165896 | tf_op jit(solution)/shard_map/ppermute | solution.py:228
  131.0 0.6 dynamic_slice.6
  131.6 0.7 pad_maximum_fusion.scal
  132.4 6.9 %collective-permute-done.side_ref = bf16[72,384]{1,0:T(8,128)(2,1)S(1)} collective-permute-done((bf16[72,384]{1,0:T(8,128)(2,1)S(1)}, bf16[72,384]{1,0:T(8,128)(2,1)S(1)}, u32[]{:S(2)}, u32[]{:S(2)}) %collective-permute-start) | collective-permute-done | bytes 55328 | tf_op jit(solution)/shard_map/ppermute | solution.py:228
  139.2 1.4 %all-to-all-done.3.part_ref = bf16[16,64,384]{2,1,0:T(8,128)(2,1)S(1)} async-done(((bf16[16,64,384]{2,1,0:T(8,128)(2,1)}), bf16[16,64,384]{2,1,0:T(8,128)(2,1)S(1)}, u32[]{:S(2)}, u32[]{:S(2)}) %all-to-all-start.3) | async-done | bytes 786464 | tf_op jit(solution)/shard_map/all_to_all | solution.py:248
  140.7 1.3 finish.1
  (32 shorter events, 0.1 us)
Async XLA Ops:
  0.6 61.1 %copy-start.19 = (s32[2]{0:T(128)S(1)}, s32[2]{0:T(128)}, u32[]{:S(2)}) copy-start(s32[2]{0:T(128)} %param.29) | copy-start | bytes 28
  0.7 0.9 copy-start.4
  1.6 0.9 copy-start.6
  2.5 0.9 copy-start.7
  3.4 0.9 copy-start.8
  4.3 0.8 copy-start.9
  5.1 0.8 copy-start.11
  5.9 0.7 copy-start.12
  6.6 0.7 copy-start.13
  7.4 0.7 copy-start.14
  8.1 0.7 copy-start.16
  8.7 0.7 copy-start.17
  11.2 1.0 copy-start.3
  57.4 62.1 %copy-start = (bf16[384,3072]{1,0:T(8,128)(2,1)S(1)}, bf16[384,3072]{1,0:T(8,128)(2,1)}, u32[]{:S(2)}) copy-start(bf16[384,3072]{1,0:T(8,128)(2,1)} %w_ref.1) | copy-start | bytes 7077892
  57.4 23.9 %all-to-all-start.1 = ((bf16[8,2,80,384]{3,2,1,0:T(8,128)(2,1)}), bf16[8,2,80,384]{3,2,1,0:T(8,128)(2,1)S(1)}, u32[]{:S(2)}, u32[]{:S(2)}) async-start(bf16[8,2,80,384]{3,2,1,0:T(8,128)(2,1)} %copy-done.3), calls=%async_computation.1 | async-start | bytes 1966080 | tf_op jit(solution)/shard_map/all_to_all | solution.py:230
  81.3 1.0 copy-start.2
  84.5 0.8 copy-start.1
  85.3 34.2 %all-to-all-start.2 = ((bf16[8,72,384]{2,1,0:T(8,128)(2,1)}), bf16[8,72,384]{2,1,0:T(8,128)(2,1)S(1)}, u32[]{:S(2)}, u32[]{:S(2)}) async-start(bf16[8,72,384]{2,1,0:T(8,128)(2,1)} %copy-done.1), calls=%async_computation.2 | async-start | bytes 884736 | tf_op jit(solution)/shard_map/all_to_all | solution.py:239
  119.5 11.5 %copy-start.20 = (f32[2]{0:T(128)S(1)}, f32[2]{0:T(128)}, u32[]{:S(2)}) copy-start(f32[2]{0:T(128)} %param.28) | copy-start | bytes 28
  119.5 12.9 %copy-start.18 = (f32[384]{0:T(512)S(1)}, f32[384]{0:T(512)}, u32[]{:S(2)}) copy-start(f32[384]{0:T(512)} %param.27) | copy-start | bytes 4612
  119.5 21.2 %copy-start.5 = (bf16[1,2,64,384]{3,2,1,0:T(8,128)(2,1)S(1)}, bf16[1,2,64,384]{3,2,1,0:T(8,128)(2,1)}, u32[]{:S(2)}) copy-start(bf16[1,2,64,384]{3,2,1,0:T(8,128)(2,1)} %param.17) | copy-start | bytes 294916
  119.5 21.2 %copy-start.10 = (bf16[1,64,384]{2,1,0:T(8,128)(2,1)S(1)}, bf16[1,64,384]{2,1,0:T(8,128)(2,1)}, u32[]{:S(2)}) copy-start(bf16[1,64,384]{2,1,0:T(8,128)(2,1)} %lat_ref.1) | copy-start | bytes 147460
  119.5 21.2 %copy-start.15 = (f32[1,2,384]{2,1,0:T(2,128)S(1)}, f32[1,2,384]{2,1,0:T(2,128)}, u32[]{:S(2)}) copy-start(f32[1,2,384]{2,1,0:T(2,128)} %param.25) | copy-start | bytes 9220
  121.8 18.8 %all-to-all-start.3 = ((bf16[16,64,384]{2,1,0:T(8,128)(2,1)}), bf16[16,64,384]{2,1,0:T(8,128)(2,1)S(1)}, u32[]{:S(2)}, u32[]{:S(2)}) async-start(bf16[16,64,384]{2,1,0:T(8,128)(2,1)} %project.1), calls=%async_computation.3 | async-start | bytes 1572864 | tf_op jit(solution)/shard_map/all_to_all | solution.py:248
  126.5 12.8 %collective-permute-start = (bf16[72,384]{1,0:T(8,128)(2,1)S(1)}, bf16[72,384]{1,0:T(8,128)(2,1)S(1)}, u32[]{:S(2)}, u32[]{:S(2)}) collective-permute-start(bf16[72,384]{1,0:T(8,128)(2,1)S(1)} %get-tuple-element.7), channel_id=1, source_target_pairs={{0,256},{256,0},{1,257},{257,1},{2,258},{258,2},{3,259},{259,3},{4... | collective-permute-start | bytes 165896 | tf_op jit(solution)/shard_map/ppermute | solution.py:228

commit v2 on v1

--- a/solution.py
+++ b/solution.py
@@ -51,15 +51,26 @@
 
 
 def prepare_kernel(
-    ids, q_ref, k_ref, v_ref, tk_ref, tv_ref, qg_ref, kg_ref, row_ref, col_ref, hid_ref, gate_ref, kv_out, q_out, side_out
+    ids, q_hbm, k_hbm, v_hbm, tk_hbm, tv_hbm, hid_hbm, gate_hbm, qg_hbm, kg_hbm, row_hbm, col_hbm,
+    kv_out, q_out, side_out,
+    q_ref, k_ref, v_ref, tk_ref, tv_ref, hid_ref, gate_ref, qg_ref, kg_ref, row_ref, col_ref, sems,
 ):
     seq = ids[0]
     other = ids[1]
+    pairs = (
+        (qg_hbm, qg_ref), (kg_hbm, kg_ref), (row_hbm.at[:, pl.ds(seq, 1)], row_ref), (col_hbm, col_ref), (q_hbm, q_ref),
+        (k_hbm, k_ref), (tk_hbm, tk_ref), (v_hbm, v_ref), (tv_hbm, tv_ref), (hid_hbm.at[other], hid_ref), (gate_hbm, gate_ref),
+    )
+    copies = [pltpu.make_async_copy(src, dst, sems.at[i]) for i, (src, dst) in enumerate(pairs)]
+    for copy in copies:
+        copy.start()
+    for copy in copies[:5]:
+        copy.wait()
     lane = lax.broadcasted_iota(jnp.int32, (TQ, HD), 1)
     even = lane % 2 == 0
     in_row = lane < 72
-    cos_t = jnp.where(in_row, row_ref[0, pl.ds(seq, 1), :], col_ref[0])
-    sin_t = jnp.where(in_row, row_ref[1, pl.ds(seq, 1), :], col_ref[1])
+    cos_t = jnp.where(in_row, row_ref[0], col_ref[0])
+    sin_t = jnp.where(in_row, row_ref[1], col_ref[1])
 
     def normed(x, gain):
         x = x.astype(F32)
@@ -72,17 +83,20 @@
     for p in range(2):
         for h in range(HPD):
             hs = slice(h * HD, (h + 1) * HD)
-            q = rotated(normed(q_ref[p, :, hs], qg_ref[...])).astype(BF)
-            k = rotated(normed(k_ref[p, :, hs], kg_ref[0:1])).astype(BF)
-            t = normed(tk_ref[p, :, hs], kg_ref[1:2]).astype(BF)
-            for z in range(NZ):
-                q_out[p * NZ + z, :, hs] = q
-                kv_out[p * NZ + z, 0, 0:TT, hs] = t
-                kv_out[p * NZ + z, 0, TT:TK, hs] = k
-        for z in range(NZ):
-            kv_out[p * NZ + z, 1, 0:TT, :] = tv_ref[p]
-            kv_out[p * NZ + z, 1, TT:TK, :] = v_ref[p]
-    side_out[0:TQ, :] = hid_ref[other]
+            q_out[p, :, hs] = rotated(normed(q_ref[p, :, hs], qg_ref[...])).astype(BF)
+    copies[5].wait()
+    copies[6].wait()
+    for p in range(2):
+        for h in range(HPD):
+            hs = slice(h * HD, (h + 1) * HD)
+            kv_out[p, 0, 0:TT, hs] = normed(tk_ref[p, :, hs], kg_ref[1:2]).astype(BF)
+            kv_out[p, 0, TT:TK, hs] = rotated(normed(k_ref[p, :, hs], kg_ref[0:1])).astype(BF)
+    for copy in copies[7:]:
+        copy.wait()
+    for p in range(2):
+        kv_out[p, 1, 0:TT, :] = tv_ref[p]
+        kv_out[p, 1, TT:TK, :] = v_ref[p]
+    side_out[0:TQ, :] = hid_ref[...]
     hi, mid, lo = split3(gate_ref[pl.ds(other, 1), :])
     rows = lax.broadcasted_iota(jnp.int32, (8, W), 0)
     packed = jnp.where(rows == 0, hi.astype(F32), jnp.where(rows == 1, mid.astype(F32), lo.astype(F32)))
@@ -104,13 +118,15 @@
         e = jnp.exp2(s - top)
         total = jnp.sum(e, -1, keepdims=True)
         o = jnp.dot(e.astype(BF), v, preferred_element_type=F32) / total
-        out_ref[:, 0:TQ, hs] = o.astype(BF).reshape(NS, TQ, HD)
+        o = o.astype(BF).reshape(NS, TQ, HD)
+        for d in range(NS):
+            out_ref[d, 0:TQ, hs] = o[(d % NZ) * 2 + d // NZ]
         lse = top + jnp.log2(total)
         hi = lse.astype(BF).astype(F32)
         stats = jnp.where(lane == h, hi, jnp.where(lane == HPD + h, lse - hi, stats))
     rows = jnp.transpose(stats)[0:STAT, :].astype(BF)
     for d in range(NS):
-        a = (d // 2) * HD
+        a = (d % NZ) * HD
         out_ref[d, TQ : TQ + STAT, 0:HD] = rows[:, a : a + HD]
         out_ref[d, TQ : TQ + STAT, HD:W] = jnp.zeros((STAT, W - HD), BF)
 
@@ -201,16 +217,31 @@
     z0 = lax.axis_index("z0")
     seq = (xh * NZ + z1) * NZ + z0
     rows, cols = rope_tables()
-    kv, q, side = call(
+    kv, q, side = pl.pallas_call(
         prepare_kernel,
-        (
-            jax.ShapeDtypeStruct((NS, 2, TK, W), BF),
-            jax.ShapeDtypeStruct((NS, TQ, W), BF),
+        out_shape=(
+            jax.ShapeDtypeStruct((2, 2, TK, W), BF),
+            jax.ShapeDtypeStruct((2, TQ, W), BF),
             jax.ShapeDtypeStruct((TQ + 8, W), BF),
         ),
-        1,
-        11,
-        "prepare",
+        in_specs=[SMEM()] + [pl.BlockSpec(memory_space=pltpu.HBM)] * 11,
+        out_specs=(VMEM(), VMEM(), VMEM()),
+        scratch_shapes=[
+            pltpu.VMEM((2, TQ, W), BF),
+            pltpu.VMEM((2, TQ, W), BF),
+            pltpu.VMEM((2, TQ, W), BF),
+            pltpu.VMEM((2, TT, W), BF),
+            pltpu.VMEM((2, TT, W), BF),
+            pltpu.VMEM((TQ, W), BF),
+            pltpu.VMEM((2, W), F32),
+            pltpu.VMEM((1, HD), F32),
+            pltpu.VMEM((2, HD), F32),
+            pltpu.VMEM((2, 1, HD), F32),
+            pltpu.VMEM((2, TQ, HD), F32),
+            pltpu.SemaphoreType.DMA((11,)),
+        ],
+        compiler_params=pltpu.CompilerParams(vmem_limit_bytes=63 * 1024 * 1024),
+        name="prepare",
     )(
         jnp.stack([seq, 1 - guide]),
         img_query[0],
@@ -218,19 +249,21 @@
         img_value[0],
         txt_key[0],
         txt_value[0],
+        img_hidden[0],
+        gate[0],
         query_gain[None],
         key_gain,
         jnp.asarray(rows),
         jnp.asarray(cols),
-        img_hidden[0],
-        gate[0],
     )
     side = lax.ppermute(side, "g", [(0, 1), (1, 0)])
-    q = lax.all_to_all(q, ("xh", "z1"), 0, 0, tiled=True)
-    kv = lax.all_to_all(kv, ("xh", "z0"), 0, 0, tiled=True)
+    q = lax.all_to_all(q, "xh", 0, 0, tiled=True)
+    kv = lax.all_to_all(kv, "xh", 0, 0, tiled=True)
+    q = lax.all_gather(q, "z1", axis=0, tiled=True)
+    kv = lax.all_gather(kv, "z0", axis=0, tiled=True)
 
     src = jnp.arange(NS)
-    src_seq = ((src // NZ) * NZ + z1) * NZ + src % NZ
+    src_seq = ((src % 2) * NZ + z1) * NZ + src // 2
     within = jnp.arange(TK)
     pos = src_seq[:, None] * TT + within[None, :]
     live = (within >= TT)[None, :] | (pos < text_len[xh])
@@ -244,7 +277,7 @@
         2,
         "project",
         [pltpu.VMEM((2 * TQ, W), BF)],
-    )((z1 % 2)[None], out, proj_weight)
+    )(xh[None], out, proj_weight)
     part = lax.all_to_all(part, ("g", "y", "c"), 0, 0, tiled=True)
     index = step_index[0]
     u_now = 1.0 - index.astype(F32) / STEPS

time: 143 us -> 124 us (0.87)
  the two profiles are of different devices: /device:TPU:64 before, /device:TPU:1 now
where the time goes in v2:
time: 124 us
  blocking collectives  78.5 us (63%)
  starting transfers between devices  20.4 us (16%)
  waiting for transfers between devices  10.2 us (8%)
  Pallas kernels  9.45 us (8%)
  other arithmetic  2.03 us (2%)
  local copies, waits for them, and re-layouts  1.95 us (2%)
  between operations  1.48 us (1%)
    all_to_all x1, blocking collectives, shards(): out = lax.all_to_all(out, ('xh', 'z1'), 0, 0, tiled=True)  34.9 us
    all_gather x1, blocking collectives, shards(): q = lax.all_gather(q, 'z1', axis=0, tiled=True)  26.6 us
    all_gather x1, blocking collectives, shards(): kv = lax.all_gather(kv, 'z0', axis=0, tiled=True)  17 us
    all_to_all x1, starting transfers between devices, shards(): part = lax.all_to_all(part, ('g', 'y', 'c'), 0, 0, tiled=True)  8.63 us
    ppermute x1, waiting for transfers between devices, shards(): side = lax.ppermute(side, 'g', [(0, 1), (1, 0)])  6.63 us
    all_to_all x1, starting transfers between devices, shards(): q = lax.all_to_all(q, 'xh', 0, 0, tiled=True)  4.85 us
    pallas_call x1, Pallas kernels, shards(): pl.pallas_call(prepare_kernel, out_shape=(jax.ShapeDtypeStruct((2, 2, TK,...  3.61 us
    all_to_all x1, starting transfers between devices, shards(): kv = lax.all_to_all(kv, 'xh', 0, 0, tiled=True)  3.57 us
  transfers between devices with their start and end apart: 4, of which 3 were waited for; matrix products, arithmetic and copies ran while one was open for 3% of the time, Pallas kernels for 0%

profile of v2, /device:TPU:1, one launch (start us, length us, event | category | flops | bytes accessed | tf_op | source)
XLA Modules:
  0.0 123.9 jit_solution(17402353839694473058)
XLA Ops:
  0.6 0.6 pad_add_fusion.ids
  1.2 3.6 %prepare.1 = (bf16[2,2,80,384]{3,2,1,0:T(8,128)(2,1)}, bf16[2,64,384]{2,1,0:T(8,128)(2,1)}, bf16[72,384]{1,0:T(8,128)(2,1)}) custom-call(s32[2]{0:T(128)} %pad_add_fusion.ids, bf16[2,64,384]{2,1,0:T(8,128)(2,1)} %bitcast.17, bf16[2,64,384]{2,1,0:T(8,128)(2,1)} %bitcast.18, bf16[2,64,384]{2,1,0:T(8,128)(2,1)} %bitcast.19, bf16[2,16,384]{2,1,0:T(8,128)(2,1)} %bitcast.20, ...), custom_call_target="tpu_custom_call" | custom-call | tf_op jit(solution)/shard_map/prepare/pallas_call | solution.py:220
  4.8 4.9 %all-to-all-start = ((bf16[2,64,384]{2,1,0:T(8,128)(2,1)}), bf16[2,64,384]{2,1,0:T(8,128)(2,1)S(1)}, u32[]{:S(2)}, u32[]{:S(2)}) async-start(bf16[2,64,384]{2,1,0:T(8,128)(2,1)} %get-tuple-element.5), calls=%async_computation | async-start | bytes 196608 | tf_op jit(solution)/shard_map/all_to_all | solution.py:260
  9.7 1.2 %dynamic_slice.7 = s32[1]{0:T(128)} dynamic-slice(s32[2]{0:T(128)} %param.29, s32[]{:T(128)S(6)} %select_n.43), dynamic_slice_sizes={1} | dynamic-slice | bytes 12 | tf_op jit(solution)/shard_map/dynamic_slice | solution.py:269
  10.9 0.7 fusion.1
  11.7 0.1 select_n.45.bias_ref
  11.7 2.6 %all-to-all-done = bf16[2,64,384]{2,1,0:T(8,128)(2,1)S(1)} async-done(((bf16[2,64,384]{2,1,0:T(8,128)(2,1)}), bf16[2,64,384]{2,1,0:T(8,128)(2,1)S(1)}, u32[]{:S(2)}, u32[]{:S(2)}) %all-to-all-start) | async-done | bytes 98336 | tf_op jit(solution)/shard_map/all_to_all | solution.py:260
  14.3 0.0 copy-start
  14.3 3.6 %all-to-all-start.1 = ((bf16[2,2,80,384]{3,2,1,0:T(8,128)(2,1)}), bf16[2,2,80,384]{3,2,1,0:T(8,128)(2,1)S(1)}, u32[]{:S(2)}, u32[]{:S(2)}) async-start(bf16[2,2,80,384]{3,2,1,0:T(8,128)(2,1)} %get-tuple-element.6), calls=%async_computation.1 | async-start | bytes 491520 | tf_op jit(solution)/shard_map/all_to_all | solution.py:261
  17.9 26.6 %all_gather.6.q_ref = bf16[8,64,384]{2,1,0:T(8,128)(2,1)S(1)} all-gather(bf16[2,64,384]{2,1,0:T(8,128)(2,1)S(1)} %all-to-all-done), channel_id=1, replica_groups=mesh['g'=2,'xh'=2,'z1'=4,'z0'=4,'y'=4,'c'=2] {'z1'}, dimensions={0}, use_global_device_ids=true | all-gather | bytes 491520 | tf_op jit(solution)/shard_map/all_gather | solution.py:262
  44.6 0.0 all-to-all-done.1
  44.6 17.0 %all_gather.7.kv_ref = bf16[8,2,80,384]{3,2,1,0:T(8,128)(2,1)S(1)} all-gather(bf16[2,2,80,384]{3,2,1,0:T(8,128)(2,1)S(1)} %all-to-all-done.1), channel_id=1, replica_groups=mesh['g'=2,'xh'=2,'z1'=4,'z0'=4,'y'=4,'c'=2] {'z0'}, dimensions={0}, use_global_device_ids=true | all-gather | bytes 1228800 | tf_op jit(solution)/shard_map/all_gather | solution.py:263
  61.5 2.2 %attend.1 = bf16[8,72,384]{2,1,0:T(8,128)(2,1)S(1)} custom-call(bf16[8,64,384]{2,1,0:T(8,128)(2,1)S(1)} %all_gather.6.q_ref, bf16[8,2,80,384]{3,2,1,0:T(8,128)(2,1)S(1)} %all_gather.7.kv_ref, f32[1,640]{1,0:T(1,128)S(1)} %select_n.45.bias_ref), custom_call_target="tpu_custom_call" | custom-call | tf_op jit(solution)/shard_map/attend/pallas_call | solution.py:271
  63.7 34.9 %all_to_all.20.o_ref = bf16[8,72,384]{2,1,0:T(8,128)(2,1)S(1)} all-to-all(bf16[8,72,384]{2,1,0:T(8,128)(2,1)S(1)} %attend.1), channel_id=1, replica_groups=mesh['g'=2,'xh'=2,'z1'=4,'z0'=4,'y'=4,'c'=2] {'xh','z1'}, dimensions={0} | all-to-all | bytes 884736 | tf_op jit(solution)/shard_map/all_to_all | solution.py:272
  98.6 0.0 copy-done
  98.6 0.0 copy-start.1
  98.6 0.0 copy-start.2
  98.6 0.0 copy-start.3
  98.6 2.3 %project.1 = bf16[16,64,384]{2,1,0:T(8,128)(2,1)} custom-call(s32[1]{0:T(128)} %bitcast.1.ids, bf16[8,72,384]{2,1,0:T(8,128)(2,1)S(1)} %all_to_all.20.o_ref, bf16[384,3072]{1,0:T(8,128)(2,1)S(1)} %copy-done), custom_call_target="tpu_custom_call" | custom-call | tf_op jit(solution)/shard_map/project/pallas_call | solution.py:273
  101.0 8.6 %all-to-all-start.3 = ((bf16[16,64,384]{2,1,0:T(8,128)(2,1)}), bf16[16,64,384]{2,1,0:T(8,128)(2,1)S(1)}, u32[]{:S(2)}, u32[]{:S(2)}) async-start(bf16[16,64,384]{2,1,0:T(8,128)(2,1)} %project.1), calls=%async_computation.3 | async-start | bytes 1572864 | tf_op jit(solution)/shard_map/all_to_all | solution.py:281
  109.6 0.0 copy-done.5
  109.6 3.3 %collective-permute-start = (bf16[72,384]{1,0:T(8,128)(2,1)S(1)}, bf16[72,384]{1,0:T(8,128)(2,1)S(1)}, u32[]{:S(2)}, u32[]{:S(2)}) collective-permute-start(bf16[72,384]{1,0:T(8,128)(2,1)S(1)} %copy-done.5), channel_id=1, source_target_pairs={{0,256},{256,0},{1,257},{257,1},{2,258},{258,2},{3,259},{259,3},{4... | collective-permute-start | bytes 165896 | tf_op jit(solution)/shard_map/ppermute | solution.py:259
  113.6 0.0 copy-done.6
  113.6 0.6 dynamic_slice.6
  114.3 0.7 pad_maximum_fusion.scal
  115.0 0.0 copy-done.4
  115.0 6.6 %collective-permute-done.side_ref = bf16[72,384]{1,0:T(8,128)(2,1)S(1)} collective-permute-done((bf16[72,384]{1,0:T(8,128)(2,1)S(1)}, bf16[72,384]{1,0:T(8,128)(2,1)S(1)}, u32[]{:S(2)}, u32[]{:S(2)}) %collective-permute-start) | collective-permute-done | bytes 55328 | tf_op jit(solution)/shard_map/ppermute | solution.py:259
  121.6 1.0 all-to-all-done.3.part_ref
  122.6 0.0 copy-done.1
  122.6 0.0 copy-done.2
  122.6 0.0 copy-done.3
  122.6 1.3 %finish.1 = (bf16[1,64,384]{2,1,0:T(8,128)(2,1)}, bf16[1,64,384]{2,1,0:T(8,128)(2,1)}) custom-call(s32[1]{0:T(128)} %bitcast.ids, f32[2]{0:T(128)S(1)} %pad_maximum_fusion.scal, bf16[16,64,384]{2,1,0:T(8,128)(2,1)S(1)} %all-to-all-done.3.part_ref, bf16[2,64,384]{2,1,0:T(8,128)(2,1)S(1)} %bitcast.14, f32[2,384]{1,0:T(2,128)S(1)} %bitcast.16, ...), custom_call_target="tpu_custom_call" | custom-call | tf_op jit(solution)/shard_map/finish/pallas_call | solution.py:287
  (6 shorter events, 0.0 us)
Async XLA Ops:
  4.8 9.5 %all-to-all-start = ((bf16[2,64,384]{2,1,0:T(8,128)(2,1)}), bf16[2,64,384]{2,1,0:T(8,128)(2,1)S(1)}, u32[]{:S(2)}, u32[]{:S(2)}) async-start(bf16[2,64,384]{2,1,0:T(8,128)(2,1)} %get-tuple-element.5), calls=%async_computation | async-start | bytes 196608 | tf_op jit(solution)/shard_map/all_to_all | solution.py:260
  14.3 84.2 %copy-start = (bf16[384,3072]{1,0:T(8,128)(2,1)S(1)}, bf16[384,3072]{1,0:T(8,128)(2,1)}, u32[]{:S(2)}) copy-start(bf16[384,3072]{1,0:T(8,128)(2,1)} %w_ref.1) | copy-start | bytes 7077892
  14.3 30.2 %all-to-all-start.1 = ((bf16[2,2,80,384]{3,2,1,0:T(8,128)(2,1)}), bf16[2,2,80,384]{3,2,1,0:T(8,128)(2,1)S(1)}, u32[]{:S(2)}, u32[]{:S(2)}) async-start(bf16[2,2,80,384]{3,2,1,0:T(8,128)(2,1)} %get-tuple-element.6), calls=%async_computation.1 | async-start | bytes 491520 | tf_op jit(solution)/shard_map/all_to_all | solution.py:261
  98.6 11.0 %copy-start.5 = (bf16[72,384]{1,0:T(8,128)(2,1)S(1)}, bf16[72,384]{1,0:T(8,128)(2,1)}, u32[]{:S(2)}) copy-start(bf16[72,384]{1,0:T(8,128)(2,1)} %get-tuple-element.7) | copy-start | bytes 165892
  98.6 15.0 %copy-start.6 = (f32[2]{0:T(128)S(1)}, f32[2]{0:T(128)}, u32[]{:S(2)}) copy-start(f32[2]{0:T(128)} %param.28) | copy-start | bytes 28
  98.6 16.4 %copy-start.4 = (f32[384]{0:T(512)S(1)}, f32[384]{0:T(512)}, u32[]{:S(2)}) copy-start(f32[384]{0:T(512)} %param.27) | copy-start | bytes 4612
  98.6 24.0 %copy-start.1 = (bf16[1,2,64,384]{3,2,1,0:T(8,128)(2,1)S(1)}, bf16[1,2,64,384]{3,2,1,0:T(8,128)(2,1)}, u32[]{:S(2)}) copy-start(bf16[1,2,64,384]{3,2,1,0:T(8,128)(2,1)} %param.17) | copy-start | bytes 294916
  98.6 24.0 %copy-start.2 = (bf16[1,64,384]{2,1,0:T(8,128)(2,1)S(1)}, bf16[1,64,384]{2,1,0:T(8,128)(2,1)}, u32[]{:S(2)}) copy-start(bf16[1,64,384]{2,1,0:T(8,128)(2,1)} %lat_ref.1) | copy-start | bytes 147460
  98.6 24.0 %copy-start.3 = (f32[1,2,384]{2,1,0:T(2,128)S(1)}, f32[1,2,384]{2,1,0:T(2,128)}, u32[]{:S(2)}) copy-start(f32[1,2,384]{2,1,0:T(2,128)} %param.25) | copy-start | bytes 9220
  101.0 21.6 %all-to-all-start.3 = ((bf16[16,64,384]{2,1,0:T(8,128)(2,1)}), bf16[16,64,384]{2,1,0:T(8,128)(2,1)S(1)}, u32[]{:S(2)}, u32[]{:S(2)}) async-start(bf16[16,64,384]{2,1,0:T(8,128)(2,1)} %project.1), calls=%async_computation.3 | async-start | bytes 1572864 | tf_op jit(solution)/shard_map/all_to_all | solution.py:281
  109.6 12.0 %collective-permute-start = (bf16[72,384]{1,0:T(8,128)(2,1)S(1)}, bf16[72,384]{1,0:T(8,128)(2,1)S(1)}, u32[]{:S(2)}, u32[]{:S(2)}) collective-permute-start(bf16[72,384]{1,0:T(8,128)(2,1)S(1)} %copy-done.5), channel_id=1, source_target_pairs={{0,256},{256,0},{1,257},{257,1},{2,258},{258,2},{3,259},{259,3},{4... | collective-permute-start | bytes 165896 | tf_op jit(solution)/shard_map/ppermute | solution.py:259

commit v3 on v1

--- a/solution.py
+++ b/solution.py
@@ -50,39 +50,75 @@
     return hi, mid, lo
 
 
-def prepare_kernel(
-    ids, q_ref, k_ref, v_ref, tk_ref, tv_ref, qg_ref, kg_ref, row_ref, col_ref, hid_ref, gate_ref, kv_out, q_out, side_out
+def rope_of(row_ref, col_ref):
+    in_row = lax.broadcasted_iota(jnp.int32, (TQ, HD), 1) < 72
+    return jnp.where(in_row, row_ref[0], col_ref[0]), jnp.where(in_row, row_ref[1], col_ref[1])
+
+
+def normed(x, gain):
+    x = x.astype(F32)
+    return x * lax.rsqrt(jnp.mean(x * x, -1, keepdims=True) + 1e-06) * gain
+
+
+def rotated(x, table):
+    even = lax.broadcasted_iota(jnp.int32, (TQ, HD), 1) % 2 == 0
+    swapped = jnp.where(even, pltpu.roll(x, HD - 1, 1), pltpu.roll(x, 1, 1))
+    return x * table[0] + swapped * table[1]
+
+
+def start_all(pairs, sems):
+    copies = [pltpu.make_async_copy(src, dst, sems.at[i]) for i, (src, dst) in enumerate(pairs)]
+    for copy in copies:
+        copy.start()
+    return copies
+
+
+def keys_kernel(
+    ids, k_hbm, v_hbm, tk_hbm, tv_hbm, kg_hbm, row_hbm, col_hbm,
+    kv_out,
+    k_ref, v_ref, tk_ref, tv_ref, kg_ref, row_ref, col_ref, sems,
 ):
-    seq = ids[0]
-    other = ids[1]
-    lane = lax.broadcasted_iota(jnp.int32, (TQ, HD), 1)
-    even = lane % 2 == 0
-    in_row = lane < 72
-    cos_t = jnp.where(in_row, row_ref[0, pl.ds(seq, 1), :], col_ref[0])
-    sin_t = jnp.where(in_row, row_ref[1, pl.ds(seq, 1), :], col_ref[1])
-
-    def normed(x, gain):
-        x = x.astype(F32)
-        return x * lax.rsqrt(jnp.mean(x * x, -1, keepdims=True) + 1e-06) * gain
-
-    def rotated(x):
-        swapped = jnp.where(even, pltpu.roll(x, HD - 1, 1), pltpu.roll(x, 1, 1))
-        return x * cos_t + swapped * sin_t
-
+    copies = start_all(
+        ((kg_hbm, kg_ref), (tk_hbm, tk_ref), (row_hbm.at[:, pl.ds(ids[0], 1)], row_ref), (col_hbm, col_ref), (k_hbm, k_ref), (v_hbm, v_ref), (tv_hbm, tv_ref)),
+        sems,
+    )
+    for copy in copies[:5]:
+        copy.wait()
+    table = rope_of(row_ref, col_ref)
     for p in range(2):
         for h in range(HPD):
             hs = slice(h * HD, (h + 1) * HD)
-            q = rotated(normed(q_ref[p, :, hs], qg_ref[...])).astype(BF)
-            k = rotated(normed(k_ref[p, :, hs], kg_ref[0:1])).astype(BF)
-            t = normed(tk_ref[p, :, hs], kg_ref[1:2]).astype(BF)
+            kv_out[p, 0, 0:TT, hs] = normed(tk_ref[p, :, hs], kg_ref[1:2]).astype(BF)
+            kv_out[p, 0, TT:TK, hs] = rotated(normed(k_ref[p, :, hs], kg_ref[0:1]), table).astype(BF)
+    for copy in copies[5:]:
+        copy.wait()
+    for p in range(2):
+        kv_out[p, 1, 0:TT, :] = tv_ref[p]
+        kv_out[p, 1, TT:TK, :] = v_ref[p]
+
+
+def queries_kernel(
+    ids, q_hbm, hid_hbm, gate_hbm, qg_hbm, row_hbm, col_hbm,
+    q_out, side_out,
+    q_ref, hid_ref, gate_ref, qg_ref, row_ref, col_ref, sems,
+):
+    other = ids[1]
+    copies = start_all(
+        ((qg_hbm, qg_ref), (row_hbm.at[:, pl.ds(ids[0], 1)], row_ref), (col_hbm, col_ref), (q_hbm, q_ref), (hid_hbm.at[other], hid_ref), (gate_hbm, gate_ref)),
+        sems,
+    )
+    for copy in copies[:4]:
+        copy.wait()
+    table = rope_of(row_ref, col_ref)
+    for p in range(2):
+        for h in range(HPD):
+            hs = slice(h * HD, (h + 1) * HD)
+            q = rotated(normed(q_ref[p, :, hs], qg_ref[...]), table).astype(BF)
             for z in range(NZ):
                 q_out[p * NZ + z, :, hs] = q
-                kv_out[p * NZ + z, 0, 0:TT, hs] = t
-                kv_out[p * NZ + z, 0, TT:TK, hs] = k
-        for z in range(NZ):
-            kv_out[p * NZ + z, 1, 0:TT, :] = tv_ref[p]
-            kv_out[p * NZ + z, 1, TT:TK, :] = v_ref[p]
-    side_out[0:TQ, :] = hid_ref[other]
+    for copy in copies[4:]:
+        copy.wait()
+    side_out[0:TQ, :] = hid_ref[...]
     hi, mid, lo = split3(gate_ref[pl.ds(other, 1), :])
     rows = lax.broadcasted_iota(jnp.int32, (8, W), 0)
     packed = jnp.where(rows == 0, hi.astype(F32), jnp.where(rows == 1, mid.astype(F32), lo.astype(F32)))
@@ -104,7 +140,9 @@
         e = jnp.exp2(s - top)
         total = jnp.sum(e, -1, keepdims=True)
         o = jnp.dot(e.astype(BF), v, preferred_element_type=F32) / total
-        out_ref[:, 0:TQ, hs] = o.astype(BF).reshape(NS, TQ, HD)
+        o = o.astype(BF).reshape(NS, TQ, HD)
+        for d in range(NS):
+            out_ref[d, 0:TQ, hs] = o[d]
         lse = top + jnp.log2(total)
         hi = lse.astype(BF).astype(F32)
         stats = jnp.where(lane == h, hi, jnp.where(lane == HPD + h, lse - hi, stats))
@@ -178,6 +216,18 @@
     )
 
 
+def from_hbm(kernel, outs, n_hbm, name, scratch):
+    return pl.pallas_call(
+        kernel,
+        out_shape=outs,
+        in_specs=[SMEM()] + [pl.BlockSpec(memory_space=pltpu.HBM)] * n_hbm,
+        out_specs=jax.tree.map(lambda _: VMEM(), outs),
+        scratch_shapes=scratch + [pltpu.SemaphoreType.DMA((n_hbm,))],
+        compiler_params=pltpu.CompilerParams(vmem_limit_bytes=63 * 1024 * 1024),
+        name=name,
+    )
+
+
 def shards(
     img_hidden,
     img_query,
@@ -201,42 +251,45 @@
     z0 = lax.axis_index("z0")
     seq = (xh * NZ + z1) * NZ + z0
     rows, cols = rope_tables()
-    kv, q, side = call(
-        prepare_kernel,
-        (
-            jax.ShapeDtypeStruct((NS, 2, TK, W), BF),
-            jax.ShapeDtypeStruct((NS, TQ, W), BF),
-            jax.ShapeDtypeStruct((TQ + 8, W), BF),
-        ),
-        1,
-        11,
-        "prepare",
-    )(
-        jnp.stack([seq, 1 - guide]),
-        img_query[0],
-        img_key[0],
-        img_value[0],
-        txt_key[0],
-        txt_value[0],
-        query_gain[None],
-        key_gain,
-        jnp.asarray(rows),
-        jnp.asarray(cols),
-        img_hidden[0],
-        gate[0],
-    )
+    ids = jnp.stack([seq, 1 - guide])
+    row_t = jnp.asarray(rows)
+    col_t = jnp.asarray(cols)
+    rope_scratch = [pltpu.VMEM((2, 1, HD), F32), pltpu.VMEM((2, TQ, HD), F32)]
+    kv = from_hbm(
+        keys_kernel,
+        jax.ShapeDtypeStruct((2, 2, TK, W), BF),
+        7,
+        "keys",
+        [
+            pltpu.VMEM((2, TQ, W), BF),
+            pltpu.VMEM((2, TQ, W), BF),
+            pltpu.VMEM((2, TT, W), BF),
+            pltpu.VMEM((2, TT, W), BF),
+            pltpu.VMEM((2, HD), F32),
+        ]
+        + rope_scratch,
+    )(ids, img_key[0], img_value[0], txt_key[0], txt_value[0], key_gain, row_t, col_t)
+    kv = lax.all_to_all(kv, "xh", 0, 0, tiled=True)
+    q, side = from_hbm(
+        queries_kernel,
+        (jax.ShapeDtypeStruct((NS, TQ, W), BF), jax.ShapeDtypeStruct((TQ + 8, W), BF)),
+        6,
+        "queries",
+        [pltpu.VMEM((2, TQ, W), BF), pltpu.VMEM((TQ, W), BF), pltpu.VMEM((2, W), F32), pltpu.VMEM((1, HD), F32)] + rope_scratch,
+    )(ids, img_query[0], img_hidden[0], gate[0], query_gain[None], row_t, col_t)
     side = lax.ppermute(side, "g", [(0, 1), (1, 0)])
-    q = lax.all_to_all(q, ("xh", "z1"), 0, 0, tiled=True)
-    kv = lax.all_to_all(kv, ("xh", "z0"), 0, 0, tiled=True)
+    q, kv = lax.optimization_barrier((q, kv))
+    q = lax.all_to_all(q, ("xh", "z0"), 0, 0, tiled=True)
+    kv = lax.all_gather(kv, "z1", axis=0, tiled=True)
 
     src = jnp.arange(NS)
-    src_seq = ((src // NZ) * NZ + z1) * NZ + src % NZ
+    src_seq = ((src % 2) * NZ + src // 2) * NZ + z0
     within = jnp.arange(TK)
     pos = src_seq[:, None] * TT + within[None, :]
     live = (within >= TT)[None, :] | (pos < text_len[xh])
     bias = jnp.where(live, 0.0, -1e30).astype(F32).reshape(1, NS * TK)
     out = call(attend_kernel, jax.ShapeDtypeStruct((NS, TQ + STAT, W), BF), 0, 3, "attend")(q, kv, bias)
-    out = lax.all_to_all(out, ("xh", "z1"), 0, 0, tiled=True)
+    out = lax.all_to_all(out, ("xh", "z0"), 0, 0, tiled=True)
     part = call(
         project_kernel,
         jax.ShapeDtypeStruct((16, TQ, W), BF),
@@ -244,7 +297,7 @@
         2,
         "project",
         [pltpu.VMEM((2 * TQ, W), BF)],
-    )((z1 % 2)[None], out, proj_weight)
+    )((z0 & 1)[None], out, proj_weight)
     part = lax.all_to_all(part, ("g", "y", "c"), 0, 0, tiled=True)
     index = step_index[0]
     u_now = 1.0 - index.astype(F32) / STEPS

time: 143 us -> 119 us (0.83)
  the two profiles are of different devices: /device:TPU:64 before, /device:TPU:1 now
where the time goes in v3:
time: 119 us
  starting transfers between devices  49.6 us (42%)
  blocking collectives  29 us (24%)
  waiting for transfers between devices  20.9 us (18%)
  Pallas kernels  12.8 us (11%)
  local copies, waits for them, and re-layouts  2.71 us (2%)
  other arithmetic  2.1 us (2%)
  between operations  1.49 us (1%)
    all_gather x1, blocking collectives, shards(): kv = lax.all_gather(kv, 'z1', axis=0, tiled=True)  29 us
    all_to_all x1, starting transfers between devices, shards(): out = lax.all_to_all(out, ('xh', 'z0'), 0, 0, tiled=True)  24.3 us
    all_to_all x1, starting transfers between devices, shards(): part = lax.all_to_all(part, ('g', 'y', 'c'), 0, 0, tiled=True)  11.1 us
    all_to_all x1, waiting for transfers between devices, shards(): out = lax.all_to_all(out, ('xh', 'z0'), 0, 0, tiled=True)  10.8 us
    ppermute x1, waiting for transfers between devices, shards(): side = lax.ppermute(side, 'g', [(0, 1), (1, 0)])  6.63 us
    all_to_all x1, starting transfers between devices, shards(): q = lax.all_to_all(q, ('xh', 'z0'), 0, 0, tiled=True)  6.18 us
    all_to_all x1, starting transfers between devices, shards(): kv = lax.all_to_all(kv, 'xh', 0, 0, tiled=True)  4.85 us
    ppermute x1, starting transfers between devices, shards(): side = lax.ppermute(side, 'g', [(0, 1), (1, 0)])  3.3 us
  transfers between devices with their start and end apart: 5, of which 4 were waited for; matrix products, arithmetic and copies ran while one was open for 3% of the time, Pallas kernels for 3%

profile of v3, /device:TPU:1, one launch (start us, length us, event | category | flops | bytes accessed | tf_op | source)
XLA Modules:
  0.0 118.6 jit_solution(8422805466677888663)
XLA Ops:
  0.6 0.6 pad_add_fusion.ids
  1.3 3.0 %keys.1 = bf16[2,2,80,384]{3,2,1,0:T(8,128)(2,1)} custom-call(s32[2]{0:T(128)} %pad_add_fusion.ids, bf16[2,64,384]{2,1,0:T(8,128)(2,1)} %bitcast.18, bf16[2,64,384]{2,1,0:T(8,128)(2,1)} %bitcast.19, bf16[2,16,384]{2,1,0:T(8,128)(2,1)} %bitcast.20, bf16[2,16,384]{2,1,0:T(8,128)(2,1)} %bitcast.21, f32[2,128]{1,0:T(2,128)} %kg_hbm.1, ...), custom_call_target="tpu_custom_call" | custom-call | tf_op jit(solution)/shard_map/keys/pallas_call | solution.py:258
  4.3 4.9 %all-to-all-start = ((bf16[2,2,80,384]{3,2,1,0:T(8,128)(2,1)}), bf16[2,2,80,384]{3,2,1,0:T(8,128)(2,1)S(1)}, u32[]{:S(2)}, u32[]{:S(2)}) async-start(bf16[2,2,80,384]{3,2,1,0:T(8,128)(2,1)} %keys.1), calls=%async_computation | async-start | bytes 491520 | tf_op jit(solution)/shard_map/all_to_all | solution.py:272
  9.1 3.0 %queries.1 = (bf16[8,64,384]{2,1,0:T(8,128)(2,1)}, bf16[72,384]{1,0:T(8,128)(2,1)}) custom-call(s32[2]{0:T(128)} %pad_add_fusion.ids, bf16[2,64,384]{2,1,0:T(8,128)(2,1)} %bitcast.17, bf16[2,64,384]{2,1,0:T(8,128)(2,1)} %bitcast.13, f32[2,384]{1,0:T(2,128)} %bitcast.15, f32[1,128]{1,0:T(1,128)} %bitcast.22, f32[2,32,128]{2,1,0:T(8,128)} %constant.85.clone.row_hbm, ...), custom_call_target="tpu_custom_call" | custom-call | tf_op jit(solution)/shard_map/queries/pallas_call | solution.py:273
  12.1 2.4 %all-to-all-done = bf16[2,2,80,384]{3,2,1,0:T(8,128)(2,1)S(1)} async-done(((bf16[2,2,80,384]{3,2,1,0:T(8,128)(2,1)}), bf16[2,2,80,384]{3,2,1,0:T(8,128)(2,1)S(1)}, u32[]{:S(2)}, u32[]{:S(2)}) %all-to-all-start) | async-done | bytes 245792 | tf_op jit(solution)/shard_map/all_to_all | solution.py:272
  14.6 6.2 %all-to-all-start.1 = ((bf16[8,64,384]{2,1,0:T(8,128)(2,1)}), bf16[8,64,384]{2,1,0:T(8,128)(2,1)}, u32[]{:S(2)}, u32[]{:S(2)}) async-start(bf16[8,64,384]{2,1,0:T(8,128)(2,1)} %get-tuple-element.7), calls=%async_computation.1 | async-start | bytes 786432 | tf_op jit(solution)/shard_map/all_to_all | solution.py:282
  20.8 1.2 %dynamic_slice.7 = s32[1]{0:T(128)} dynamic-slice(s32[2]{0:T(128)} %param.29, s32[]{:T(128)S(6)} %select_n.43), dynamic_slice_sizes={1} | dynamic-slice | bytes 12 | tf_op jit(solution)/shard_map/dynamic_slice | solution.py:289
  22.0 0.7 fusion.1
  22.7 0.0 copy-done.5
  22.7 0.1 select_n.45.bias_ref
  22.8 29.0 %all_gather.3.kv_ref = bf16[8,2,80,384]{3,2,1,0:T(8,128)(2,1)S(1)} all-gather(bf16[2,2,80,384]{3,2,1,0:T(8,128)(2,1)} %copy-done.5), channel_id=1, replica_groups=mesh['g'=2,'xh'=2,'z1'=4,'z0'=4,'y'=4,'c'=2] {'z1'}, dimensions={0}, use_global_device_ids=true | all-gather | bytes 1228800 | tf_op jit(solution)/shard_map/all_gather | solution.py:283
  51.8 0.0 all-to-all-done.1.q_ref
  51.8 3.2 %attend.1 = bf16[8,72,384]{2,1,0:T(8,128)(2,1)S(1)} custom-call(bf16[8,64,384]{2,1,0:T(8,128)(2,1)} %all-to-all-done.1.q_ref, bf16[8,2,80,384]{3,2,1,0:T(8,128)(2,1)S(1)} %all_gather.3.kv_ref, f32[1,640]{1,0:T(1,128)S(1)} %select_n.45.bias_ref), custom_call_target="tpu_custom_call" | custom-call | tf_op jit(solution)/shard_map/attend/pallas_call | solution.py:291
  55.0 0.0 copy-start.1
  55.0 0.8 copy-done.1
  55.8 24.3 %all-to-all-start.2 = ((bf16[8,72,384]{2,1,0:T(8,128)(2,1)}), bf16[8,72,384]{2,1,0:T(8,128)(2,1)S(1)}, u32[]{:S(2)}, u32[]{:S(2)}) async-start(bf16[8,72,384]{2,1,0:T(8,128)(2,1)} %copy-done.1), calls=%async_computation.2 | async-start | bytes 884736 | tf_op jit(solution)/shard_map/all_to_all | solution.py:292
  80.0 10.8 %all-to-all-done.2.o_ref = bf16[8,72,384]{2,1,0:T(8,128)(2,1)S(1)} async-done(((bf16[8,72,384]{2,1,0:T(8,128)(2,1)}), bf16[8,72,384]{2,1,0:T(8,128)(2,1)S(1)}, u32[]{:S(2)}, u32[]{:S(2)}) %all-to-all-start.2) | async-done | bytes 442400 | tf_op jit(solution)/shard_map/all_to_all | solution.py:292
  90.9 0.0 copy-done
  90.9 0.0 copy-start.2
  90.9 0.0 copy-start.3
  90.9 0.0 copy-start.4
  90.9 2.3 %project.1 = bf16[16,64,384]{2,1,0:T(8,128)(2,1)} custom-call(s32[1]{0:T(128)} %bitcast.1.ids, bf16[8,72,384]{2,1,0:T(8,128)(2,1)S(1)} %all-to-all-done.2.o_ref, bf16[384,3072]{1,0:T(8,128)(2,1)S(1)} %copy-done), custom_call_target="tpu_custom_call" | custom-call | tf_op jit(solution)/shard_map/project/pallas_call | solution.py:293
  93.2 11.1 %all-to-all-start.3 = ((bf16[16,64,384]{2,1,0:T(8,128)(2,1)}), bf16[16,64,384]{2,1,0:T(8,128)(2,1)S(1)}, u32[]{:S(2)}, u32[]{:S(2)}) async-start(bf16[16,64,384]{2,1,0:T(8,128)(2,1)} %project.1), calls=%async_computation.3 | async-start | bytes 1572864 | tf_op jit(solution)/shard_map/all_to_all | solution.py:301
  104.3 3.3 %collective-permute-start = (bf16[72,384]{1,0:T(8,128)(2,1)S(1)}, bf16[72,384]{1,0:T(8,128)(2,1)S(1)}, u32[]{:S(2)}, u32[]{:S(2)}) collective-permute-start(bf16[72,384]{1,0:T(8,128)(2,1)S(1)} %copy-done.7), channel_id=1, source_target_pairs={{0,256},{256,0},{1,257},{257,1},{2,258},{258,2},{3,259},{259,3},{4... | collective-permute-start | bytes 165896 | tf_op jit(solution)/shard_map/ppermute | solution.py:280
  108.3 0.6 dynamic_slice.6
  109.0 0.7 pad_maximum_fusion.scal
  109.7 0.0 copy-done.6
  109.7 6.6 %collective-permute-done.side_ref = bf16[72,384]{1,0:T(8,128)(2,1)S(1)} collective-permute-done((bf16[72,384]{1,0:T(8,128)(2,1)S(1)}, bf16[72,384]{1,0:T(8,128)(2,1)S(1)}, u32[]{:S(2)}, u32[]{:S(2)}) %collective-permute-start) | collective-permute-done | bytes 55328 | tf_op jit(solution)/shard_map/ppermute | solution.py:280
  116.3 1.0 all-to-all-done.3.part_ref
  117.3 0.0 copy-done.2
  117.3 0.0 copy-done.4
  117.3 1.3 %finish.1 = (bf16[1,64,384]{2,1,0:T(8,128)(2,1)}, bf16[1,64,384]{2,1,0:T(8,128)(2,1)}) custom-call(s32[1]{0:T(128)} %bitcast.ids, f32[2]{0:T(128)S(1)} %pad_maximum_fusion.scal, bf16[16,64,384]{2,1,0:T(8,128)(2,1)S(1)} %all-to-all-done.3.part_ref, bf16[2,64,384]{2,1,0:T(8,128)(2,1)S(1)} %bitcast.14, f32[2,384]{1,0:T(2,128)S(1)} %bitcast.16, ...), custom_call_target="tpu_custom_call" | custom-call | tf_op jit(solution)/shard_map/finish/pallas_call | solution.py:307
  (11 shorter events, 0.0 us)
Async XLA Ops:
  4.3 10.3 %all-to-all-start = ((bf16[2,2,80,384]{3,2,1,0:T(8,128)(2,1)}), bf16[2,2,80,384]{3,2,1,0:T(8,128)(2,1)S(1)}, u32[]{:S(2)}, u32[]{:S(2)}) async-start(bf16[2,2,80,384]{3,2,1,0:T(8,128)(2,1)} %keys.1), calls=%async_computation | async-start | bytes 491520 | tf_op jit(solution)/shard_map/all_to_all | solution.py:272
  14.6 8.2 %copy-start.5 = (bf16[2,2,80,384]{3,2,1,0:T(8,128)(2,1)}, bf16[2,2,80,384]{3,2,1,0:T(8,128)(2,1)S(1)}, u32[]{:S(2)}) copy-start(bf16[2,2,80,384]{3,2,1,0:T(8,128)(2,1)S(1)} %all-to-all-done) | copy-start | bytes 737284
  14.6 76.3 %copy-start = (bf16[384,3072]{1,0:T(8,128)(2,1)S(1)}, bf16[384,3072]{1,0:T(8,128)(2,1)}, u32[]{:S(2)}) copy-start(bf16[384,3072]{1,0:T(8,128)(2,1)} %w_ref.1) | copy-start | bytes 7077892
  14.6 37.3 %all-to-all-start.1 = ((bf16[8,64,384]{2,1,0:T(8,128)(2,1)}), bf16[8,64,384]{2,1,0:T(8,128)(2,1)}, u32[]{:S(2)}, u32[]{:S(2)}) async-start(bf16[8,64,384]{2,1,0:T(8,128)(2,1)} %get-tuple-element.7), calls=%async_computation.1 | async-start | bytes 786432 | tf_op jit(solution)/shard_map/all_to_all | solution.py:282
  55.0 0.8 copy-start.1
  55.8 35.1 %all-to-all-start.2 = ((bf16[8,72,384]{2,1,0:T(8,128)(2,1)}), bf16[8,72,384]{2,1,0:T(8,128)(2,1)S(1)}, u32[]{:S(2)}, u32[]{:S(2)}) async-start(bf16[8,72,384]{2,1,0:T(8,128)(2,1)} %copy-done.1), calls=%async_computation.2 | async-start | bytes 884736 | tf_op jit(solution)/shard_map/all_to_all | solution.py:292
  90.9 13.4 %copy-start.7 = (bf16[72,384]{1,0:T(8,128)(2,1)S(1)}, bf16[72,384]{1,0:T(8,128)(2,1)}, u32[]{:S(2)}) copy-start(bf16[72,384]{1,0:T(8,128)(2,1)} %get-tuple-element.9) | copy-start | bytes 165892
  90.9 17.4 %copy-start.8 = (f32[2]{0:T(128)S(1)}, f32[2]{0:T(128)}, u32[]{:S(2)}) copy-start(f32[2]{0:T(128)} %param.28) | copy-start | bytes 28
  90.9 18.8 %copy-start.6 = (f32[384]{0:T(512)S(1)}, f32[384]{0:T(512)}, u32[]{:S(2)}) copy-start(f32[384]{0:T(512)} %param.27) | copy-start | bytes 4612
  90.9 26.4 %copy-start.2 = (bf16[1,2,64,384]{3,2,1,0:T(8,128)(2,1)S(1)}, bf16[1,2,64,384]{3,2,1,0:T(8,128)(2,1)}, u32[]{:S(2)}) copy-start(bf16[1,2,64,384]{3,2,1,0:T(8,128)(2,1)} %param.17) | copy-start | bytes 294916
  90.9 26.4 %copy-start.3 = (bf16[1,64,384]{2,1,0:T(8,128)(2,1)S(1)}, bf16[1,64,384]{2,1,0:T(8,128)(2,1)}, u32[]{:S(2)}) copy-start(bf16[1,64,384]{2,1,0:T(8,128)(2,1)} %lat_ref.1) | copy-start | bytes 147460
  90.9 26.4 %copy-start.4 = (f32[1,2,384]{2,1,0:T(2,128)S(1)}, f32[1,2,384]{2,1,0:T(2,128)}, u32[]{:S(2)}) copy-start(f32[1,2,384]{2,1,0:T(2,128)} %param.25) | copy-start | bytes 9220
  93.2 24.0 %all-to-all-start.3 = ((bf16[16,64,384]{2,1,0:T(8,128)(2,1)}), bf16[16,64,384]{2,1,0:T(8,128)(2,1)S(1)}, u32[]{:S(2)}, u32[]{:S(2)}) async-start(bf16[16,64,384]{2,1,0:T(8,128)(2,1)} %project.1), calls=%async_computation.3 | async-start | bytes 1572864 | tf_op jit(solution)/shard_map/all_to_all | solution.py:301
  104.3 12.0 %collective-permute-start = (bf16[72,384]{1,0:T(8,128)(2,1)S(1)}, bf16[72,384]{1,0:T(8,128)(2,1)S(1)}, u32[]{:S(2)}, u32[]{:S(2)}) collective-permute-start(bf16[72,384]{1,0:T(8,128)(2,1)S(1)} %copy-done.7), channel_id=1, source_target_pairs={{0,256},{256,0},{1,257},{257,1},{2,258},{258,2},{3,259},{259,3},{4... | collective-permute-start | bytes 165896 | tf_op jit(solution)/shard_map/ppermute | solution.py:280

commit v4 on v3

--- a/solution.py
+++ b/solution.py
@@ -74,37 +74,40 @@
 
 
 def keys_kernel(
-    ids, k_hbm, v_hbm, tk_hbm, tv_hbm, kg_hbm, row_hbm, col_hbm,
-    kv_out,
+    seq_id, xh_id, k_hbm, v_hbm, tk_hbm, tv_hbm, kg_hbm, row_hbm, col_hbm,
+    keep_out, send_out,
     k_ref, v_ref, tk_ref, tv_ref, kg_ref, row_ref, col_ref, sems,
 ):
+    rows = row_hbm.at[:, pl.ds(seq_id[0], 1)]
     copies = start_all(
-        ((kg_hbm, kg_ref), (tk_hbm, tk_ref), (row_hbm.at[:, pl.ds(ids[0], 1)], row_ref), (col_hbm, col_ref), (k_hbm, k_ref), (v_hbm, v_ref), (tv_hbm, tv_ref)),
+        ((rows, row_ref), (col_hbm, col_ref), (kg_hbm, kg_ref), (tk_hbm, tk_ref), (k_hbm, k_ref), (v_hbm, v_ref), (tv_hbm, tv_ref)),
         sems,
     )
     for copy in copies[:5]:
         copy.wait()
     table = rope_of(row_ref, col_ref)
-    for p in range(2):
+    own = xh_id[0]
+    for out, p in ((send_out, 1 - own), (keep_out, own)):
         for h in range(HPD):
             hs = slice(h * HD, (h + 1) * HD)
-            kv_out[p, 0, 0:TT, hs] = normed(tk_ref[p, :, hs], kg_ref[1:2]).astype(BF)
-            kv_out[p, 0, TT:TK, hs] = rotated(normed(k_ref[p, :, hs], kg_ref[0:1]), table).astype(BF)
+            out[0, 0:TT, hs] = normed(tk_ref[p, :, hs], kg_ref[1:2]).astype(BF)
+            out[0, TT:TK, hs] = rotated(normed(k_ref[p, :, hs], kg_ref[0:1]), table).astype(BF)
     for copy in copies[5:]:
         copy.wait()
-    for p in range(2):
-        kv_out[p, 1, 0:TT, :] = tv_ref[p]
-        kv_out[p, 1, TT:TK, :] = v_ref[p]
+    for out, p in ((send_out, 1 - own), (keep_out, own)):
+        out[1, 0:TT, :] = tv_ref[p]
+        out[1, TT:TK, :] = v_ref[p]
 
 
 def queries_kernel(
-    ids, q_hbm, hid_hbm, gate_hbm, qg_hbm, row_hbm, col_hbm,
+    seq_id, guide_id, q_hbm, hid_hbm, gate_hbm, qg_hbm, row_hbm, col_hbm, after_hbm,
     q_out, side_out,
     q_ref, hid_ref, gate_ref, qg_ref, row_ref, col_ref, sems,
 ):
-    other = ids[1]
+    other = 1 - guide_id[0]
+    rows = row_hbm.at[:, pl.ds(seq_id[0], 1)]
     copies = start_all(
-        ((qg_hbm, qg_ref), (row_hbm.at[:, pl.ds(ids[0], 1)], row_ref), (col_hbm, col_ref), (q_hbm, q_ref), (hid_hbm.at[other], hid_ref), (gate_hbm, gate_ref)),
+        ((rows, row_ref), (col_hbm, col_ref), (qg_hbm, qg_ref), (q_hbm, q_ref), (hid_hbm.at[other], hid_ref), (gate_hbm, gate_ref)),
         sems,
     )
     for copy in copies[:4]:
@@ -125,24 +128,36 @@
     side_out[TQ : TQ + 8, :] = packed.astype(BF)
 
 
-def attend_kernel(q_ref, kv_ref, bias_ref, out_ref):
+def attend_kernel(xh_id, z0_id, len_ref, q_ref, kv_ref, out_hbm, out_ref, sems):
     scale = HD ** (-0.5) * 1.4426950408889634
+    own = xh_id[0]
+    at = lax.broadcasted_iota(jnp.int32, (1, NS * TK), 1)
+    block = jnp.zeros_like(at)
+    for i in range(1, NS):
+        block = block + (at >= i * TK).astype(jnp.int32)
+    within = at - block * TK
+    from_own = (block & 1) == 0
+    seq = (jnp.where(from_own, own, 1 - own) * NZ + (block >> 1)) * NZ + z0_id[0]
+    dead = (within < TT) & (seq * TT + within >= len_ref[own])
+    bias = jnp.where(dead, -1e30, 0.0)
     lane = lax.broadcasted_iota(jnp.int32, (NS * TQ, HD), 1)
     stats = jnp.zeros((NS * TQ, HD), F32)
+    copies = []
     for h in range(HPD):
         hs = slice(h * HD, (h + 1) * HD)
         q = q_ref[:, :, hs].reshape(NS * TQ, HD)
-        k = kv_ref[:, 0, :, hs].reshape(NS * TK, HD)
-        v = kv_ref[:, 1, :, hs].reshape(NS * TK, HD)
+        k = kv_ref[:, :, 0, :, hs].reshape(NS * TK, HD)
+        v = kv_ref[:, :, 1, :, hs].reshape(NS * TK, HD)
         s = lax.dot_general(q, k, (((1,), (1,)), ((), ())), preferred_element_type=F32)
-        s = s * scale + bias_ref[...]
+        s = s * scale + bias
         top = jnp.max(s, -1, keepdims=True)
         e = jnp.exp2(s - top)
         total = jnp.sum(e, -1, keepdims=True)
         o = jnp.dot(e.astype(BF), v, preferred_element_type=F32) / total
-        o = o.astype(BF).reshape(NS, TQ, HD)
-        for d in range(NS):
-            out_ref[d, 0:TQ, hs] = o[d]
+        out_ref[:, 0:TQ, hs] = o.astype(BF).reshape(NS, TQ, HD)
+        copy = pltpu.make_async_copy(out_ref.at[:, 0:TQ, hs], out_hbm.at[:, 0:TQ, hs], sems.at[h])
+        copy.start()
+        copies.append(copy)
         lse = top + jnp.log2(total)
         hi = lse.astype(BF).astype(F32)
         stats = jnp.where(lane == h, hi, jnp.where(lane == HPD + h, lse - hi, stats))
@@ -151,9 +166,14 @@
         a = (d // 2) * HD
         out_ref[d, TQ : TQ + STAT, 0:HD] = rows[:, a : a + HD]
         out_ref[d, TQ : TQ + STAT, HD:W] = jnp.zeros((STAT, W - HD), BF)
-
-
-def project_kernel(ids, o_ref, w_ref, out_ref, attn_ref):
+    copy = pltpu.make_async_copy(out_ref.at[:, TQ : TQ + STAT, :], out_hbm.at[:, TQ : TQ + STAT, :], sems.at[HPD])
+    copy.start()
+    copies.append(copy)
+    for copy in copies:
+        copy.wait()
+
+
+def project_kernel(ids, o_ref, w_ref, out_hbm, attn_ref, out_ref, sems):
     odd = ids[0]
     stats = o_ref[:, TQ : TQ + STAT, 0:HD].astype(F32).reshape(NS * STAT, HD)
     cols = jnp.transpose(jnp.concatenate([stats, stats], 0))
@@ -173,10 +193,16 @@
                 acc = acc + ws[z] * o_ref[p * NZ + z, 0:TQ, hs].astype(F32)
             attn_ref[p * TQ : (p + 1) * TQ, hs] = (acc / total).astype(BF)
     attn = attn_ref[...]
+    copies = []
     for b in range(8):
         part = jnp.dot(attn, w_ref[:, b * W : (b + 1) * W], preferred_element_type=F32).astype(BF)
-        out_ref[b] = part[0:TQ]
-        out_ref[8 + b] = part[TQ : 2 * TQ]
+        out_ref[0, b] = part[0:TQ]
+        out_ref[1, b] = part[TQ : 2 * TQ]
+        copy = pltpu.make_async_copy(out_ref.at[:, b], out_hbm.at[:, b], sems.at[b])
+        copy.start()
+        copies.append(copy)
+    for copy in copies:
+        copy.wait()
 
 
 def finish_kernel(ids, scal, part_ref, hid_ref, gate_ref, side_ref, bias_ref, lat_ref, guided_ref, next_ref):
@@ -202,28 +228,17 @@
 
 SMEM = functools.partial(pl.BlockSpec, memory_space=pltpu.SMEM)
 VMEM = functools.partial(pl.BlockSpec, memory_space=pltpu.VMEM)
-
-
-def call(kernel, outs, n_smem, n_vmem, name, scratch=()):
+HBM = functools.partial(pl.BlockSpec, memory_space=pltpu.HBM)
+
+
+def call(kernel, outs, ins, out_specs, name, scratch=(), limit=VMEM_LIMIT):
     return pl.pallas_call(
         kernel,
         out_shape=outs,
-        in_specs=[SMEM()] * n_smem + [VMEM()] * n_vmem,
-        out_specs=jax.tree.map(lambda _: VMEM(), outs),
+        in_specs=ins,
+        out_specs=out_specs,
         scratch_shapes=list(scratch),
-        compiler_params=pltpu.CompilerParams(vmem_limit_bytes=VMEM_LIMIT),
-        name=name,
-    )
-
-
-def from_hbm(kernel, outs, n_hbm, name, scratch):
-    return pl.pallas_call(
-        kernel,
-        out_shape=outs,
-        in_specs=[SMEM()] + [pl.BlockSpec(memory_space=pltpu.HBM)] * n_hbm,
-        out_specs=jax.tree.map(lambda _: VMEM(), outs),
-        scratch_shapes=scratch + [pltpu.SemaphoreType.DMA((n_hbm,))],
-        compiler_params=pltpu.CompilerParams(vmem_limit_bytes=63 * 1024 * 1024),
+        compiler_params=pltpu.CompilerParams(vmem_limit_bytes=limit),
         name=name,
     )
 
@@ -251,14 +266,15 @@
     z0 = lax.axis_index("z0")
     seq = (xh * NZ + z1) * NZ + z0
     rows, cols = rope_tables()
-    ids = jnp.stack([seq, 1 - guide])
+    kv_shape = jax.ShapeDtypeStruct((2, TK, W), BF)
     row_t = jnp.asarray(rows)
     col_t = jnp.asarray(cols)
     rope_scratch = [pltpu.VMEM((2, 1, HD), F32), pltpu.VMEM((2, TQ, HD), F32)]
-    kv = from_hbm(
+    keep, send = call(
         keys_kernel,
-        jax.ShapeDtypeStruct((2, 2, TK, W), BF),
-        7,
+        (kv_shape, kv_shape),
+        [SMEM()] * 2 + [HBM()] * 7,
+        (VMEM(),) * 2,
         "keys",
         [
             pltpu.VMEM((2, TQ, W), BF),
@@ -266,45 +282,58 @@
             pltpu.VMEM((2, TT, W), BF),
             pltpu.VMEM((2, TT, W), BF),
             pltpu.VMEM((2, HD), F32),
-        ]
-        + rope_scratch,
-    )(ids, img_key[0], img_value[0], txt_key[0], txt_value[0], key_gain, row_t, col_t)
-    kv = lax.all_to_all(kv, "xh", 0, 0, tiled=True)
-    q, side = from_hbm(
+            *rope_scratch,
+            pltpu.SemaphoreType.DMA((7,)),
+        ],
+        63 * 1024 * 1024,
+    )(seq[None], xh[None], img_key[0], img_value[0], txt_key[0], txt_value[0], key_gain, row_t, col_t)
+    swap = [(0, 1), (1, 0)]
+    got = lax.ppermute(send, "xh", swap)
+    q, side = call(
         queries_kernel,
         (jax.ShapeDtypeStruct((NS, TQ, W), BF), jax.ShapeDtypeStruct((TQ + 8, W), BF)),
-        6,
+        [SMEM()] * 2 + [HBM()] * 7,
+        (VMEM(),) * 2,
         "queries",
-        [pltpu.VMEM((2, TQ, W), BF), pltpu.VMEM((TQ, W), BF), pltpu.VMEM((2, W), F32), pltpu.VMEM((1, HD), F32)] + rope_scratch,
-    )(ids, img_query[0], img_hidden[0], gate[0], query_gain[None], row_t, col_t)
-    side = lax.ppermute(side, "g", [(0, 1), (1, 0)])
-    q, kv = lax.optimization_barrier((q, kv))
+        [
+            pltpu.VMEM((2, TQ, W), BF),
+            pltpu.VMEM((TQ, W), BF),
+            pltpu.VMEM((2, W), F32),
+            pltpu.VMEM((1, HD), F32),
+            *rope_scratch,
+            pltpu.SemaphoreType.DMA((6,)),
+        ],
+        63 * 1024 * 1024,
+    )(seq[None], guide[None], img_query[0], img_hidden[0], gate[0], query_gain[None], row_t, col_t, send)
+    side = lax.ppermute(side, "g", swap)
+    q, got = lax.optimization_barrier((q, got))
     q = lax.all_to_all(q, ("xh", "z0"), 0, 0, tiled=True)
-    kv = lax.all_gather(kv, "z1", axis=0, tiled=True)
-
-    src = jnp.arange(NS)
-    src_seq = ((src % 2) * NZ + src // 2) * NZ + z0
-    within = jnp.arange(TK)
-    pos = src_seq[:, None] * TT + within[None, :]
-    live = (within >= TT)[None, :] | (pos < text_len[xh])
-    bias = jnp.where(live, 0.0, -1e30).astype(F32).reshape(1, NS * TK)
-    out = call(attend_kernel, jax.ShapeDtypeStruct((NS, TQ + STAT, W), BF), 0, 3, "attend")(q, kv, bias)
+    kv = lax.all_gather(jnp.stack([keep, got]), "z1", axis=0)
+
+    out = call(
+        attend_kernel,
+        jax.ShapeDtypeStruct((NS, TQ + STAT, W), BF),
+        [SMEM()] * 3 + [VMEM()] * 2,
+        HBM(),
+        "attend",
+        [pltpu.VMEM((NS, TQ + STAT, W), BF), pltpu.SemaphoreType.DMA((HPD + 1,))],
+    )(xh[None], z0[None], text_len, q, kv)
     out = lax.all_to_all(out, ("xh", "z0"), 0, 0, tiled=True)
     part = call(
         project_kernel,
-        jax.ShapeDtypeStruct((16, TQ, W), BF),
-        1,
-        2,
+        jax.ShapeDtypeStruct((2, 8, TQ, W), BF),
+        [SMEM()] + [VMEM()] * 2,
+        HBM(),
         "project",
-        [pltpu.VMEM((2 * TQ, W), BF)],
+        [pltpu.VMEM((2 * TQ, W), BF), pltpu.VMEM((2, 8, TQ, W), BF), pltpu.SemaphoreType.DMA((8,))],
     )((z0 & 1)[None], out, proj_weight)
-    part = lax.all_to_all(part, ("g", "y", "c"), 0, 0, tiled=True)
+    part = lax.all_to_all(part.reshape(16, TQ, W), ("g", "y", "c"), 0, 0, tiled=True)
     index = step_index[0]
     u_now = 1.0 - index.astype(F32) / STEPS
     u_next = 1.0 - (index + 1).astype(F32) / STEPS
     step = 3.0 * u_next / (1.0 + 2.0 * u_next) - 3.0 * u_now / (1.0 + 2.0 * u_now)
     shape = jax.ShapeDtypeStruct((1, TQ, W), BF)
-    return call(finish_kernel, (shape, shape), 2, 6, "finish")(
+    return call(finish_kernel, (shape, shape), [SMEM()] * 2 + [VMEM()] * 6, (VMEM(),) * 2, "finish")(
         guide[None],
         jnp.stack([guidance[guide], step]),
         part,

time: 119 us -> 117 us (0.983)
  waiting for transfers between devices: 20.9 us -> 18.4 us
  starting transfers between devices: 49.6 us -> 51.2 us
  local copies, waits for them, and re-layouts: 2.71 us -> 1.39 us
    all_to_all x2 -> x1, starting transfers between devices: 15.9 us -> 9.95 us  [shards(): lax.all_to_all(part.reshape(16, TQ, W), ('g', 'y', 'c'), 0, 0, tiled=True)]
    ppermute x1 -> x2, starting transfers between devices: 3.3 us -> 8.78 us  [the longest x1 5.48 us: shards(): got = lax.ppermute(send, 'xh', swap)]
    all_to_all x1, starting transfers between devices: 6.18 us -> 8.76 us  [shards(): q = lax.all_to_all(q, ('xh', 'z0'), 0, 0, tiled=True)]
    all_to_all x2 -> x1, waiting for transfers between devices: 3.4 us -> 0.97 us  [shards(): lax.all_to_all(part.reshape(16, TQ, W), ('g', 'y', 'c'), 0, 0, tiled=True)]
    dynamic_slice x1 -> x0, local copies, waits for them, and re-layouts: 1.24 us -> none  [shards(): live = (within >= TT)[None, :] | (pos < text_len[xh])]
    ppermute x1 -> x2, waiting for transfers between devices: 6.63 us -> 6.72 us  [the longest x1 6.63 us: shards(): side = lax.ppermute(side, 'g', swap)]
  transfers between devices with their start and end apart: 5 -> 5, of which waited for: 4 -> 4; matrix products, arithmetic and copies ran while one was open for 3% -> 2% of each run, Pallas kernels for 3% -> 2%
where the time goes in v4:
time: 117 us; the launch traced here: 116 us
  starting transfers between devices  51.2 us (44%)
  blocking collectives  29.8 us (25%)
  waiting for transfers between devices  18.4 us (16%)
  Pallas kernels  12.1 us (10%)
  other arithmetic  1.8 us (2%)
  between operations  1.52 us (1%)
  local copies, waits for them, and re-layouts  1.39 us (1%)
    all_gather x1, blocking collectives, shards(): kv = lax.all_gather(jnp.stack([keep, got]), 'z1', axis=0)  29.8 us
    all_to_all x1, starting transfers between devices, shards(): out = lax.all_to_all(out, ('xh', 'z0'), 0, 0, tiled=True)  23.7 us
    all_to_all x1, waiting for transfers between devices, shards(): out = lax.all_to_all(out, ('xh', 'z0'), 0, 0, tiled=True)  10.7 us
    all_to_all x1, starting transfers between devices, shards(): lax.all_to_all(part.reshape(16, TQ, W), ('g', 'y', 'c'), 0, 0, tiled=True)  9.95 us
    all_to_all x1, starting transfers between devices, shards(): q = lax.all_to_all(q, ('xh', 'z0'), 0, 0, tiled=True)  8.76 us
    ppermute x1, waiting for transfers between devices, shards(): side = lax.ppermute(side, 'g', swap)  6.63 us
    ppermute x1, starting transfers between devices, shards(): got = lax.ppermute(send, 'xh', swap)  5.48 us
    pallas_call x1, Pallas kernels, shards(): call(attend_kernel, jax.ShapeDtypeStruct((NS, TQ + STAT, W), BF), [SMEM()...  3.96 us
  transfers between devices with their start and end apart: 5, of which 4 were waited for; matrix products, arithmetic and copies ran while one was open for 2% of the time, Pallas kernels for 2%

profile of v4, /device:TPU:1, one launch (start us, length us, event | category | flops | bytes accessed | tf_op | source)
XLA Modules:
  0.0 116.3 jit_solution(3558550939504577054)
XLA Ops:
  0.6 0.0 copy-start.5
  0.7 2.3 %keys.1 = (bf16[2,80,384]{2,1,0:T(8,128)(2,1)}, bf16[2,80,384]{2,1,0:T(8,128)(2,1)}) custom-call(s32[1]{0:T(128)} %bitcast.4.seq_id, s32[1]{0:T(128)} %bitcast.2.xh_id, bf16[2,64,384]{2,1,0:T(8,128)(2,1)} %bitcast.24, bf16[2,64,384]{2,1,0:T(8,128)(2,1)} %bitcast.25, bf16[2,16,384]{2,1,0:T(8,128)(2,1)} %bitcast.27, bf16[2,16,384]{2,1,0:T(8,128)(2,1)} %bitcast.28, ...), custom_call_target="tpu_custom_call" | custom-call | tf_op jit(solution)/shard_map/keys/pallas_call | solution.py:273
  3.0 5.5 %collective-permute-start = (bf16[2,80,384]{2,1,0:T(8,128)(2,1)}, bf16[2,80,384]{2,1,0:T(8,128)(2,1)S(1)}, u32[]{:S(2)}, u32[]{:S(2)}) collective-permute-start(bf16[2,80,384]{2,1,0:T(8,128)(2,1)} %get-tuple-element.8.after_hbm), channel_id=1, source_target_pairs={{0,128},{128,0},{1,129},{129,1},{2,130},{130,2},{3,131},{131,3},{4... | collective-permute-start | bytes 368648 | tf_op jit(solution)/shard_map/ppermute | solution.py:291
  8.5 2.4 %queries.1 = (bf16[8,64,384]{2,1,0:T(8,128)(2,1)}, bf16[72,384]{1,0:T(8,128)(2,1)}) custom-call(s32[1]{0:T(128)} %bitcast.4.seq_id, s32[1]{0:T(128)} %bitcast.guide_id.ids, bf16[2,64,384]{2,1,0:T(8,128)(2,1)} %bitcast.26, bf16[2,64,384]{2,1,0:T(8,128)(2,1)} %bitcast.18, f32[2,384]{1,0:T(2,128)} %bitcast.20, f32[1,128]{1,0:T(1,128)} %bitcast.29, ...), custom_call_target="tpu_custom_call" | custom-call | tf_op jit(solution)/shard_map/queries/pallas_call | solution.py:292
  10.8 0.1 collective-permute-done
  10.9 8.8 %all-to-all-start = ((bf16[8,64,384]{2,1,0:T(8,128)(2,1)}), bf16[8,64,384]{2,1,0:T(8,128)(2,1)}, u32[]{:S(2)}, u32[]{:S(2)}) async-start(bf16[8,64,384]{2,1,0:T(8,128)(2,1)} %get-tuple-element.10), calls=%async_computation | async-start | bytes 786432 | tf_op jit(solution)/shard_map/all_to_all | solution.py:310
  19.7 1.1 pad_maximum_fusion
  20.8 29.8 %all-gather = bf16[8,2,80,384]{3,2,1,0:T(8,128)(2,1)S(1)} all-gather(bf16[2,2,80,384]{3,2,1,0:T(8,128)(2,1)S(1)} %pad_maximum_fusion), channel_id=2, replica_groups=mesh['g'=2,'xh'=2,'z1'=4,'z0'=4,'y'=4,'c'=2] {'z1'}, dimensions={0}, use_global_device_ids=true | all-gather | bytes 1228800 | tf_op jit(solution)/shard_map/all_gather | solution.py:311
  50.6 0.0 all-to-all-done.q_ref
  50.6 0.0 copy-done.5
  50.6 4.0 %attend.1 = bf16[8,72,384]{2,1,0:T(8,128)(2,1)S(1)} custom-call(s32[1]{0:T(128)} %bitcast.2.xh_id, s32[1]{0:T(128)} %bitcast.3.z0_id, s32[2]{0:T(128)S(1)} %copy-done.5, bf16[8,64,384]{2,1,0:T(8,128)(2,1)} %all-to-all-done.q_ref, bf16[4,2,2,80,384]{4,3,2,1,0:T(8,128)(2,1)S(1)} %bitcast.17), custom_call_target="tpu_custom_call" | custom-call | tf_op jit(solution)/shard_map/attend/pallas_call | solution.py:313
  54.6 0.0 copy-start.1
  54.6 0.8 copy-done.1
  55.3 23.7 %all-to-all-start.1 = ((bf16[8,72,384]{2,1,0:T(8,128)(2,1)}), bf16[8,72,384]{2,1,0:T(8,128)(2,1)S(1)}, u32[]{:S(2)}, u32[]{:S(2)}) async-start(bf16[8,72,384]{2,1,0:T(8,128)(2,1)} %copy-done.1), calls=%async_computation.1 | async-start | bytes 884736 | tf_op jit(solution)/shard_map/all_to_all | solution.py:321
  79.1 10.7 %all-to-all-done.1.o_ref = bf16[8,72,384]{2,1,0:T(8,128)(2,1)S(1)} async-done(((bf16[8,72,384]{2,1,0:T(8,128)(2,1)}), bf16[8,72,384]{2,1,0:T(8,128)(2,1)S(1)}, u32[]{:S(2)}, u32[]{:S(2)}) %all-to-all-start.1) | async-done | bytes 442400 | tf_op jit(solution)/shard_map/all_to_all | solution.py:321
  89.8 0.0 copy-done
  89.8 0.0 copy-start.2
  89.8 0.0 copy-start.3
  89.8 0.0 copy-start.4
  89.9 2.1 %project.1 = bf16[2,8,64,384]{3,2,1,0:T(8,128)(2,1)} custom-call(s32[1]{0:T(128)} %bitcast.1.ids, bf16[8,72,384]{2,1,0:T(8,128)(2,1)S(1)} %all-to-all-done.1.o_ref, bf16[384,3072]{1,0:T(8,128)(2,1)S(1)} %copy-done), custom_call_target="tpu_custom_call" | custom-call | tf_op jit(solution)/shard_map/project/pallas_call | solution.py:322
  92.0 10.0 %all-to-all-start.2 = ((bf16[16,64,384]{2,1,0:T(8,128)(2,1)}), bf16[16,64,384]{2,1,0:T(8,128)(2,1)S(1)}, u32[]{:S(2)}, u32[]{:S(2)}) async-start(bf16[16,64,384]{2,1,0:T(8,128)(2,1)} %bitcast.16), calls=%async_computation.2 | async-start | bytes 1572864 | tf_op jit(solution)/shard_map/all_to_all | solution.py:330
  102.0 0.0 copy-done.7
  102.0 3.3 %collective-permute-start.1 = (bf16[72,384]{1,0:T(8,128)(2,1)S(1)}, bf16[72,384]{1,0:T(8,128)(2,1)S(1)}, u32[]{:S(2)}, u32[]{:S(2)}) collective-permute-start(bf16[72,384]{1,0:T(8,128)(2,1)S(1)} %copy-done.7), channel_id=1, source_target_pairs={{0,256},{256,0},{1,257},{257,1},{2,258},{258,2},{3,259},{259,3},{4... | collective-permute-start | bytes 165896 | tf_op jit(solution)/shard_map/ppermute | solution.py:308
  105.9 0.0 copy-done.8
  105.9 0.6 dynamic_slice.3
  106.6 0.7 pad_maximum_fusion.1.scal
  107.3 0.0 copy-done.6
  107.4 6.6 %collective-permute-done.1.side_ref = bf16[72,384]{1,0:T(8,128)(2,1)S(1)} collective-permute-done((bf16[72,384]{1,0:T(8,128)(2,1)S(1)}, bf16[72,384]{1,0:T(8,128)(2,1)S(1)}, u32[]{:S(2)}, u32[]{:S(2)}) %collective-permute-start.1) | collective-permute-done | bytes 55328 | tf_op jit(solution)/shard_map/ppermute | solution.py:308
  114.0 1.0 all-to-all-done.2.part_ref
  115.0 0.0 copy-done.2
  115.0 0.0 copy-done.4
  115.0 1.3 %finish.1 = (bf16[1,64,384]{2,1,0:T(8,128)(2,1)}, bf16[1,64,384]{2,1,0:T(8,128)(2,1)}) custom-call(s32[1]{0:T(128)} %bitcast.guide_id.ids, f32[2]{0:T(128)S(1)} %pad_maximum_fusion.1.scal, bf16[16,64,384]{2,1,0:T(8,128)(2,1)S(1)} %all-to-all-done.2.part_ref, bf16[2,64,384]{2,1,0:T(8,128)(2,1)S(1)} %bitcast.19, f32[2,384]{1,0:T(2,128)S(1)} %bitcast.21, ...), custom_call_target="tpu_custom_call" | custom-call | tf_op jit(solution)/shard_map/finish/pallas_call | solution.py:336
  (6 shorter events, 0.0 us)
Async XLA Ops:
  0.6 50.0 %copy-start.5 = (s32[2]{0:T(128)S(1)}, s32[2]{0:T(128)}, u32[]{:S(2)}) copy-start(s32[2]{0:T(128)} %len_ref.1) | copy-start | bytes 28
  3.0 8.0 %collective-permute-start = (bf16[2,80,384]{2,1,0:T(8,128)(2,1)}, bf16[2,80,384]{2,1,0:T(8,128)(2,1)S(1)}, u32[]{:S(2)}, u32[]{:S(2)}) collective-permute-start(bf16[2,80,384]{2,1,0:T(8,128)(2,1)} %get-tuple-element.8.after_hbm), channel_id=1, source_target_pairs={{0,128},{128,0},{1,129},{129,1},{2,130},{130,2},{3,131},{131,3},{4... | collective-permute-start | bytes 368648 | tf_op jit(solution)/shard_map/ppermute | solution.py:291
  10.9 39.7 %all-to-all-start = ((bf16[8,64,384]{2,1,0:T(8,128)(2,1)}), bf16[8,64,384]{2,1,0:T(8,128)(2,1)}, u32[]{:S(2)}, u32[]{:S(2)}) async-start(bf16[8,64,384]{2,1,0:T(8,128)(2,1)} %get-tuple-element.10), calls=%async_computation | async-start | bytes 786432 | tf_op jit(solution)/shard_map/all_to_all | solution.py:310
  19.7 70.1 %copy-start = (bf16[384,3072]{1,0:T(8,128)(2,1)S(1)}, bf16[384,3072]{1,0:T(8,128)(2,1)}, u32[]{:S(2)}) copy-start(bf16[384,3072]{1,0:T(8,128)(2,1)} %w_ref.1) | copy-start | bytes 7077892
  54.6 0.8 copy-start.1
  55.3 34.5 %all-to-all-start.1 = ((bf16[8,72,384]{2,1,0:T(8,128)(2,1)}), bf16[8,72,384]{2,1,0:T(8,128)(2,1)S(1)}, u32[]{:S(2)}, u32[]{:S(2)}) async-start(bf16[8,72,384]{2,1,0:T(8,128)(2,1)} %copy-done.1), calls=%async_computation.1 | async-start | bytes 884736 | tf_op jit(solution)/shard_map/all_to_all | solution.py:321
  89.8 12.2 %copy-start.7 = (bf16[72,384]{1,0:T(8,128)(2,1)S(1)}, bf16[72,384]{1,0:T(8,128)(2,1)}, u32[]{:S(2)}) copy-start(bf16[72,384]{1,0:T(8,128)(2,1)} %get-tuple-element.13) | copy-start | bytes 165892
  89.8 16.1 %copy-start.8 = (f32[2]{0:T(128)S(1)}, f32[2]{0:T(128)}, u32[]{:S(2)}) copy-start(f32[2]{0:T(128)} %param.28) | copy-start | bytes 28
  89.8 17.5 %copy-start.6 = (f32[384]{0:T(512)S(1)}, f32[384]{0:T(512)}, u32[]{:S(2)}) copy-start(f32[384]{0:T(512)} %param.27) | copy-start | bytes 4612
  89.8 25.1 %copy-start.2 = (bf16[1,2,64,384]{3,2,1,0:T(8,128)(2,1)S(1)}, bf16[1,2,64,384]{3,2,1,0:T(8,128)(2,1)}, u32[]{:S(2)}) copy-start(bf16[1,2,64,384]{3,2,1,0:T(8,128)(2,1)} %param.17) | copy-start | bytes 294916
  89.8 25.1 %copy-start.3 = (bf16[1,64,384]{2,1,0:T(8,128)(2,1)S(1)}, bf16[1,64,384]{2,1,0:T(8,128)(2,1)}, u32[]{:S(2)}) copy-start(bf16[1,64,384]{2,1,0:T(8,128)(2,1)} %lat_ref.1) | copy-start | bytes 147460
  89.8 25.1 %copy-start.4 = (f32[1,2,384]{2,1,0:T(2,128)S(1)}, f32[1,2,384]{2,1,0:T(2,128)}, u32[]{:S(2)}) copy-start(f32[1,2,384]{2,1,0:T(2,128)} %param.25) | copy-start | bytes 9220
  92.0 22.9 %all-to-all-start.2 = ((bf16[16,64,384]{2,1,0:T(8,128)(2,1)}), bf16[16,64,384]{2,1,0:T(8,128)(2,1)S(1)}, u32[]{:S(2)}, u32[]{:S(2)}) async-start(bf16[16,64,384]{2,1,0:T(8,128)(2,1)} %bitcast.16), calls=%async_computation.2 | async-start | bytes 1572864 | tf_op jit(solution)/shard_map/all_to_all | solution.py:330
  102.0 12.0 %collective-permute-start.1 = (bf16[72,384]{1,0:T(8,128)(2,1)S(1)}, bf16[72,384]{1,0:T(8,128)(2,1)S(1)}, u32[]{:S(2)}, u32[]{:S(2)}) collective-permute-start(bf16[72,384]{1,0:T(8,128)(2,1)S(1)} %copy-done.7), channel_id=1, source_target_pairs={{0,256},{256,0},{1,257},{257,1},{2,258},{258,2},{3,259},{259,3},{4... | collective-permute-start | bytes 165896 | tf_op jit(solution)/shard_map/ppermute | solution.py:308

commit v5 on v4

--- a/solution.py
+++ b/solution.py
@@ -74,7 +74,7 @@
 
 
 def keys_kernel(
-    seq_id, xh_id, k_hbm, v_hbm, tk_hbm, tv_hbm, kg_hbm, row_hbm, col_hbm,
+    seq_id, xh_id, k_hbm, v_hbm, tk_hbm, tv_hbm, kg_hbm, row_hbm, col_hbm, after_hbm,
     keep_out, send_out,
     k_ref, v_ref, tk_ref, tv_ref, kg_ref, row_ref, col_ref, sems,
 ):
@@ -100,7 +100,7 @@
 
 
 def queries_kernel(
-    seq_id, guide_id, q_hbm, hid_hbm, gate_hbm, qg_hbm, row_hbm, col_hbm, after_hbm,
+    seq_id, guide_id, q_hbm, hid_hbm, gate_hbm, qg_hbm, row_hbm, col_hbm,
     q_out, side_out,
     q_ref, hid_ref, gate_ref, qg_ref, row_ref, col_ref, sems,
 ):
@@ -128,7 +128,7 @@
     side_out[TQ : TQ + 8, :] = packed.astype(BF)
 
 
-def attend_kernel(xh_id, z0_id, len_ref, q_ref, kv_ref, out_hbm, out_ref, sems):
+def attend_kernel(xh_id, z0_id, len_ref, q_ref, kv_ref, out_ref):
     scale = HD ** (-0.5) * 1.4426950408889634
     own = xh_id[0]
     at = lax.broadcasted_iota(jnp.int32, (1, NS * TK), 1)
@@ -142,7 +142,6 @@
     bias = jnp.where(dead, -1e30, 0.0)
     lane = lax.broadcasted_iota(jnp.int32, (NS * TQ, HD), 1)
     stats = jnp.zeros((NS * TQ, HD), F32)
-    copies = []
     for h in range(HPD):
         hs = slice(h * HD, (h + 1) * HD)
         q = q_ref[:, :, hs].reshape(NS * TQ, HD)
@@ -155,9 +154,6 @@
         total = jnp.sum(e, -1, keepdims=True)
         o = jnp.dot(e.astype(BF), v, preferred_element_type=F32) / total
         out_ref[:, 0:TQ, hs] = o.astype(BF).reshape(NS, TQ, HD)
-        copy = pltpu.make_async_copy(out_ref.at[:, 0:TQ, hs], out_hbm.at[:, 0:TQ, hs], sems.at[h])
-        copy.start()
-        copies.append(copy)
         lse = top + jnp.log2(total)
         hi = lse.astype(BF).astype(F32)
         stats = jnp.where(lane == h, hi, jnp.where(lane == HPD + h, lse - hi, stats))
@@ -166,11 +162,6 @@
         a = (d // 2) * HD
         out_ref[d, TQ : TQ + STAT, 0:HD] = rows[:, a : a + HD]
         out_ref[d, TQ : TQ + STAT, HD:W] = jnp.zeros((STAT, W - HD), BF)
-    copy = pltpu.make_async_copy(out_ref.at[:, TQ : TQ + STAT, :], out_hbm.at[:, TQ : TQ + STAT, :], sems.at[HPD])
-    copy.start()
-    copies.append(copy)
-    for copy in copies:
-        copy.wait()
 
 
 def project_kernel(ids, o_ref, w_ref, out_hbm, attn_ref, out_ref, sems):
@@ -270,10 +261,26 @@
     row_t = jnp.asarray(rows)
     col_t = jnp.asarray(cols)
     rope_scratch = [pltpu.VMEM((2, 1, HD), F32), pltpu.VMEM((2, TQ, HD), F32)]
+    q, side = call(
+        queries_kernel,
+        (jax.ShapeDtypeStruct((NS, TQ, W), BF), jax.ShapeDtypeStruct((TQ + 8, W), BF)),
+        [SMEM()] * 2 + [HBM()] * 6,
+        (VMEM(),) * 2,
+        "queries",
+        [
+            pltpu.VMEM((2, TQ, W), BF),
+            pltpu.VMEM((TQ, W), BF),
+            pltpu.VMEM((2, W), F32),
+            pltpu.VMEM((1, HD), F32),
+            *rope_scratch,
+            pltpu.SemaphoreType.DMA((6,)),
+        ],
+        63 * 1024 * 1024,
+    )(seq[None], guide[None], img_query[0], img_hidden[0], gate[0], query_gain[None], row_t, col_t)
     keep, send = call(
         keys_kernel,
         (kv_shape, kv_shape),
-        [SMEM()] * 2 + [HBM()] * 7,
+        [SMEM()] * 2 + [HBM()] * 8,
         (VMEM(),) * 2,
         "keys",
         [
@@ -286,37 +293,20 @@
             pltpu.SemaphoreType.DMA((7,)),
         ],
         63 * 1024 * 1024,
-    )(seq[None], xh[None], img_key[0], img_value[0], txt_key[0], txt_value[0], key_gain, row_t, col_t)
+    )(seq[None], xh[None], img_key[0], img_value[0], txt_key[0], txt_value[0], key_gain, row_t, col_t, q)
+    q = lax.all_to_all(q, ("xh", "z0"), 0, 0, tiled=True)
     swap = [(0, 1), (1, 0)]
     got = lax.ppermute(send, "xh", swap)
-    q, side = call(
-        queries_kernel,
-        (jax.ShapeDtypeStruct((NS, TQ, W), BF), jax.ShapeDtypeStruct((TQ + 8, W), BF)),
-        [SMEM()] * 2 + [HBM()] * 7,
-        (VMEM(),) * 2,
-        "queries",
-        [
-            pltpu.VMEM((2, TQ, W), BF),
-            pltpu.VMEM((TQ, W), BF),
-            pltpu.VMEM((2, W), F32),
-            pltpu.VMEM((1, HD), F32),
-            *rope_scratch,
-            pltpu.SemaphoreType.DMA((6,)),
-        ],
-        63 * 1024 * 1024,
-    )(seq[None], guide[None], img_query[0], img_hidden[0], gate[0], query_gain[None], row_t, col_t, send)
     side = lax.ppermute(side, "g", swap)
-    q, got = lax.optimization_barrier((q, got))
-    q = lax.all_to_all(q, ("xh", "z0"), 0, 0, tiled=True)
+    got, side = lax.optimization_barrier((got, side))
     kv = lax.all_gather(jnp.stack([keep, got]), "z1", axis=0)
 
     out = call(
         attend_kernel,
         jax.ShapeDtypeStruct((NS, TQ + STAT, W), BF),
         [SMEM()] * 3 + [VMEM()] * 2,
-        HBM(),
+        VMEM(),
         "attend",
-        [pltpu.VMEM((NS, TQ + STAT, W), BF), pltpu.SemaphoreType.DMA((HPD + 1,))],
     )(xh[None], z0[None], text_len, q, kv)
     out = lax.all_to_all(out, ("xh", "z0"), 0, 0, tiled=True)
     part = call(

time: 117 us -> 118 us (level)
  starting transfers between devices: 51.2 us -> 28.5 us
  blocking collectives: 29.8 us -> 46.1 us
  waiting for transfers between devices: 18.4 us -> 26.6 us
    all_to_all x1, starting transfers between devices: 23.7 us -> 3.47 us  [shards(): out = lax.all_to_all(out, ('xh', 'z0'), 0, 0, tiled=True)]
    all_gather x1, blocking collectives: 29.8 us -> 46.1 us  [shards(): kv = lax.all_gather(jnp.stack([keep, got]), 'z1', axis=0)]
    all_to_all x1, waiting for transfers between devices: 0.97 us -> 10.9 us  [shards(): lax.all_to_all(part.reshape(16, TQ, W), ('g', 'y', 'c'), 0, 0, tiled=True)]
    ppermute x1, waiting for transfers between devices: 6.63 us -> 4.1 us  [shards(): side = lax.ppermute(side, 'g', swap)]
  transfers between devices with their start and end apart: 5 -> 5, of which waited for: 4 -> 3; matrix products, arithmetic and copies ran while one was open for 2% -> 2% of each run, Pallas kernels for 2% -> 2%
where the time goes in v5:
time: 118 us; the launch traced here: 117 us
  blocking collectives  46.1 us (39%)
  starting transfers between devices  28.5 us (24%)
  waiting for transfers between devices  26.6 us (23%)
  Pallas kernels  11.3 us (10%)
  other arithmetic  1.65 us (1%)
  between operations  1.54 us (1%)
  local copies, waits for them, and re-layouts  1.39 us (1%)
    all_gather x1, blocking collectives, shards(): kv = lax.all_gather(jnp.stack([keep, got]), 'z1', axis=0)  46.1 us
    all_to_all x1, waiting for transfers between devices, shards(): out = lax.all_to_all(out, ('xh', 'z0'), 0, 0, tiled=True)  11.6 us
    all_to_all x1, waiting for transfers between devices, shards(): lax.all_to_all(part.reshape(16, TQ, W), ('g', 'y', 'c'), 0, 0, tiled=True)  10.9 us
    all_to_all x1, starting transfers between devices, shards(): lax.all_to_all(part.reshape(16, TQ, W), ('g', 'y', 'c'), 0, 0, tiled=True)  8.92 us
    all_to_all x1, starting transfers between devices, shards(): q = lax.all_to_all(q, ('xh', 'z0'), 0, 0, tiled=True)  8.92 us
    ppermute x1, starting transfers between devices, shards(): got = lax.ppermute(send, 'xh', swap)  5.01 us
    ppermute x1, waiting for transfers between devices, shards(): side = lax.ppermute(side, 'g', swap)  4.1 us
    all_to_all x1, starting transfers between devices, shards(): out = lax.all_to_all(out, ('xh', 'z0'), 0, 0, tiled=True)  3.47 us
  transfers between devices with their start and end apart: 5, of which 3 were waited for; matrix products, arithmetic and copies ran while one was open for 2% of the time, Pallas kernels for 2%

profile of v5, /device:TPU:1, one launch (start us, length us, event | category | flops | bytes accessed | tf_op | source)
XLA Modules:
  0.0 117.1 jit_solution(14484296938231507871)
XLA Ops:
  0.6 0.0 copy-start.5
  0.7 2.4 %queries.1 = (bf16[8,64,384]{2,1,0:T(8,128)(2,1)}, bf16[72,384]{1,0:T(8,128)(2,1)}) custom-call(s32[1]{0:T(128)} %bitcast.4.seq_id, s32[1]{0:T(128)} %bitcast.guide_id.ids, bf16[2,64,384]{2,1,0:T(8,128)(2,1)} %bitcast.24, bf16[2,64,384]{2,1,0:T(8,128)(2,1)} %bitcast.18, f32[2,384]{1,0:T(2,128)} %bitcast.20, f32[1,128]{1,0:T(1,128)} %bitcast.29, ...), custom_call_target="tpu_custom_call" | custom-call | tf_op jit(solution)/shard_map/queries/pallas_call | solution.py:264
  3.0 8.9 %all-to-all-start = ((bf16[8,64,384]{2,1,0:T(8,128)(2,1)}), bf16[8,64,384]{2,1,0:T(8,128)(2,1)}, u32[]{:S(2)}, u32[]{:S(2)}) async-start(bf16[8,64,384]{2,1,0:T(8,128)(2,1)} %get-tuple-element.8.after_hbm), calls=%async_computation | async-start | bytes 786432 | tf_op jit(solution)/shard_map/all_to_all | solution.py:297
  12.0 2.3 %keys.1 = (bf16[2,80,384]{2,1,0:T(8,128)(2,1)}, bf16[2,80,384]{2,1,0:T(8,128)(2,1)}) custom-call(s32[1]{0:T(128)} %bitcast.4.seq_id, s32[1]{0:T(128)} %bitcast.2.xh_id, bf16[2,64,384]{2,1,0:T(8,128)(2,1)} %bitcast.25, bf16[2,64,384]{2,1,0:T(8,128)(2,1)} %bitcast.26, bf16[2,16,384]{2,1,0:T(8,128)(2,1)} %bitcast.27, bf16[2,16,384]{2,1,0:T(8,128)(2,1)} %bitcast.28, ...), custom_call_target="tpu_custom_call" | custom-call | tf_op jit(solution)/shard_map/keys/pallas_call | solution.py:280
  14.3 0.0 copy-start
  14.3 5.0 %collective-permute-start = (bf16[2,80,384]{2,1,0:T(8,128)(2,1)}, bf16[2,80,384]{2,1,0:T(8,128)(2,1)S(1)}, u32[]{:S(2)}, u32[]{:S(2)}) collective-permute-start(bf16[2,80,384]{2,1,0:T(8,128)(2,1)} %get-tuple-element.10), channel_id=1, source_target_pairs={{0,128},{128,0},{1,129},{129,1},{2,130},{130,2},{3,131},{131,3},{4... | collective-permute-start | bytes 368648 | tf_op jit(solution)/shard_map/ppermute | solution.py:299
  19.3 2.2 %collective-permute-start.1 = (bf16[72,384]{1,0:T(8,128)(2,1)}, bf16[72,384]{1,0:T(8,128)(2,1)S(1)}, u32[]{:S(2)}, u32[]{:S(2)}) collective-permute-start(bf16[72,384]{1,0:T(8,128)(2,1)} %get-tuple-element.11), channel_id=1, source_target_pairs={{0,256},{256,0},{1,257},{257,1},{2,258},{258,2},{3,259},{259,3},{4... | collective-permute-start | bytes 165896 | tf_op jit(solution)/shard_map/ppermute | solution.py:300
  21.6 4.1 %collective-permute-done.1.side_ref = bf16[72,384]{1,0:T(8,128)(2,1)S(1)} collective-permute-done((bf16[72,384]{1,0:T(8,128)(2,1)}, bf16[72,384]{1,0:T(8,128)(2,1)S(1)}, u32[]{:S(2)}, u32[]{:S(2)}) %collective-permute-start.1) | collective-permute-done | bytes 55328 | tf_op jit(solution)/shard_map/ppermute | solution.py:300
  25.7 0.0 collective-permute-done
  25.7 0.9 pad_maximum_fusion
  26.6 46.1 %all-gather = bf16[8,2,80,384]{3,2,1,0:T(8,128)(2,1)S(1)} all-gather(bf16[2,2,80,384]{3,2,1,0:T(8,128)(2,1)S(1)} %pad_maximum_fusion), channel_id=2, replica_groups=mesh['g'=2,'xh'=2,'z1'=4,'z0'=4,'y'=4,'c'=2] {'z1'}, dimensions={0}, use_global_device_ids=true | all-gather | bytes 1228800 | tf_op jit(solution)/shard_map/all_gather | solution.py:302
  72.7 0.0 all-to-all-done.q_ref
  72.7 0.0 copy-done.5
  72.7 3.1 %attend.1 = bf16[8,72,384]{2,1,0:T(8,128)(2,1)S(1)} custom-call(s32[1]{0:T(128)} %bitcast.2.xh_id, s32[1]{0:T(128)} %bitcast.3.z0_id, s32[2]{0:T(128)S(1)} %copy-done.5, bf16[8,64,384]{2,1,0:T(8,128)(2,1)} %all-to-all-done.q_ref, bf16[4,2,2,80,384]{4,3,2,1,0:T(8,128)(2,1)S(1)} %bitcast.17), custom_call_target="tpu_custom_call" | custom-call | tf_op jit(solution)/shard_map/attend/pallas_call | solution.py:304
  75.8 0.0 copy-start.1
  75.8 0.8 copy-done.1
  76.6 3.5 %all-to-all-start.1 = ((bf16[8,72,384]{2,1,0:T(8,128)(2,1)}), bf16[8,72,384]{2,1,0:T(8,128)(2,1)S(1)}, u32[]{:S(2)}, u32[]{:S(2)}) async-start(bf16[8,72,384]{2,1,0:T(8,128)(2,1)} %copy-done.1), calls=%async_computation.1 | async-start | bytes 884736 | tf_op jit(solution)/shard_map/all_to_all | solution.py:311
  80.1 11.6 %all-to-all-done.1.o_ref = bf16[8,72,384]{2,1,0:T(8,128)(2,1)S(1)} async-done(((bf16[8,72,384]{2,1,0:T(8,128)(2,1)}), bf16[8,72,384]{2,1,0:T(8,128)(2,1)S(1)}, u32[]{:S(2)}, u32[]{:S(2)}) %all-to-all-start.1) | async-done | bytes 442400 | tf_op jit(solution)/shard_map/all_to_all | solution.py:311
  91.7 0.0 copy-done
  91.7 0.0 copy-start.3
  91.7 0.0 copy-start.4
  91.7 2.1 %project.1 = bf16[2,8,64,384]{3,2,1,0:T(8,128)(2,1)} custom-call(s32[1]{0:T(128)} %bitcast.1.ids, bf16[8,72,384]{2,1,0:T(8,128)(2,1)S(1)} %all-to-all-done.1.o_ref, bf16[384,3072]{1,0:T(8,128)(2,1)S(1)} %copy-done), custom_call_target="tpu_custom_call" | custom-call | tf_op jit(solution)/shard_map/project/pallas_call | solution.py:312
  93.8 8.9 %all-to-all-start.2 = ((bf16[16,64,384]{2,1,0:T(8,128)(2,1)}), bf16[16,64,384]{2,1,0:T(8,128)(2,1)S(1)}, u32[]{:S(2)}, u32[]{:S(2)}) async-start(bf16[16,64,384]{2,1,0:T(8,128)(2,1)} %bitcast.16), calls=%async_computation.2 | async-start | bytes 1572864 | tf_op jit(solution)/shard_map/all_to_all | solution.py:320
  103.4 0.0 copy-done.6
  103.5 0.0 copy-done.7
  103.5 0.6 dynamic_slice.3
  104.1 0.7 pad_maximum_fusion.1.scal
  104.9 10.9 %all-to-all-done.2.part_ref = bf16[16,64,384]{2,1,0:T(8,128)(2,1)S(1)} async-done(((bf16[16,64,384]{2,1,0:T(8,128)(2,1)}), bf16[16,64,384]{2,1,0:T(8,128)(2,1)S(1)}, u32[]{:S(2)}, u32[]{:S(2)}) %all-to-all-start.2) | async-done | bytes 786464 | tf_op jit(solution)/shard_map/all_to_all | solution.py:320
  115.8 0.0 copy-done.2
  115.8 0.0 copy-done.3
  115.8 0.0 copy-done.4
  115.8 1.3 %finish.1 = (bf16[1,64,384]{2,1,0:T(8,128)(2,1)}, bf16[1,64,384]{2,1,0:T(8,128)(2,1)}) custom-call(s32[1]{0:T(128)} %bitcast.guide_id.ids, f32[2]{0:T(128)S(1)} %pad_maximum_fusion.1.scal, bf16[16,64,384]{2,1,0:T(8,128)(2,1)S(1)} %all-to-all-done.2.part_ref, bf16[2,64,384]{2,1,0:T(8,128)(2,1)S(1)} %bitcast.19, f32[2,384]{1,0:T(2,128)S(1)} %bitcast.21, ...), custom_call_target="tpu_custom_call" | custom-call | tf_op jit(solution)/shard_map/finish/pallas_call | solution.py:326
  (4 shorter events, 0.0 us)
Async XLA Ops:
  0.6 72.0 %copy-start.5 = (s32[2]{0:T(128)S(1)}, s32[2]{0:T(128)}, u32[]{:S(2)}) copy-start(s32[2]{0:T(128)} %len_ref.1) | copy-start | bytes 28
  3.0 69.6 %all-to-all-start = ((bf16[8,64,384]{2,1,0:T(8,128)(2,1)}), bf16[8,64,384]{2,1,0:T(8,128)(2,1)}, u32[]{:S(2)}, u32[]{:S(2)}) async-start(bf16[8,64,384]{2,1,0:T(8,128)(2,1)} %get-tuple-element.8.after_hbm), calls=%async_computation | async-start | bytes 786432 | tf_op jit(solution)/shard_map/all_to_all | solution.py:297
  14.3 77.4 %copy-start = (bf16[384,3072]{1,0:T(8,128)(2,1)S(1)}, bf16[384,3072]{1,0:T(8,128)(2,1)}, u32[]{:S(2)}) copy-start(bf16[384,3072]{1,0:T(8,128)(2,1)} %w_ref.1) | copy-start | bytes 7077892
  14.3 11.3 %collective-permute-start = (bf16[2,80,384]{2,1,0:T(8,128)(2,1)}, bf16[2,80,384]{2,1,0:T(8,128)(2,1)S(1)}, u32[]{:S(2)}, u32[]{:S(2)}) collective-permute-start(bf16[2,80,384]{2,1,0:T(8,128)(2,1)} %get-tuple-element.10), channel_id=1, source_target_pairs={{0,128},{128,0},{1,129},{129,1},{2,130},{130,2},{3,131},{131,3},{4... | collective-permute-start | bytes 368648 | tf_op jit(solution)/shard_map/ppermute | solution.py:299
  19.3 6.3 %collective-permute-start.1 = (bf16[72,384]{1,0:T(8,128)(2,1)}, bf16[72,384]{1,0:T(8,128)(2,1)S(1)}, u32[]{:S(2)}, u32[]{:S(2)}) collective-permute-start(bf16[72,384]{1,0:T(8,128)(2,1)} %get-tuple-element.11), channel_id=1, source_target_pairs={{0,256},{256,0},{1,257},{257,1},{2,258},{258,2},{3,259},{259,3},{4... | collective-permute-start | bytes 165896 | tf_op jit(solution)/shard_map/ppermute | solution.py:300
  75.8 0.8 copy-start.1
  76.6 15.1 %all-to-all-start.1 = ((bf16[8,72,384]{2,1,0:T(8,128)(2,1)}), bf16[8,72,384]{2,1,0:T(8,128)(2,1)S(1)}, u32[]{:S(2)}, u32[]{:S(2)}) async-start(bf16[8,72,384]{2,1,0:T(8,128)(2,1)} %copy-done.1), calls=%async_computation.1 | async-start | bytes 884736 | tf_op jit(solution)/shard_map/all_to_all | solution.py:311
  91.7 11.8 %copy-start.6 = (f32[384]{0:T(512)S(1)}, f32[384]{0:T(512)}, u32[]{:S(2)}) copy-start(f32[384]{0:T(512)} %param.27) | copy-start | bytes 4612
  91.7 11.8 %copy-start.7 = (f32[2]{0:T(128)S(1)}, f32[2]{0:T(128)}, u32[]{:S(2)}) copy-start(f32[2]{0:T(128)} %param.28) | copy-start | bytes 28
  91.7 24.1 %copy-start.2 = (bf16[1,2,64,384]{3,2,1,0:T(8,128)(2,1)S(1)}, bf16[1,2,64,384]{3,2,1,0:T(8,128)(2,1)}, u32[]{:S(2)}) copy-start(bf16[1,2,64,384]{3,2,1,0:T(8,128)(2,1)} %param.17) | copy-start | bytes 294916
  91.7 24.1 %copy-start.3 = (bf16[1,64,384]{2,1,0:T(8,128)(2,1)S(1)}, bf16[1,64,384]{2,1,0:T(8,128)(2,1)}, u32[]{:S(2)}) copy-start(bf16[1,64,384]{2,1,0:T(8,128)(2,1)} %lat_ref.1) | copy-start | bytes 147460
  91.7 24.1 %copy-start.4 = (f32[1,2,384]{2,1,0:T(2,128)S(1)}, f32[1,2,384]{2,1,0:T(2,128)}, u32[]{:S(2)}) copy-start(f32[1,2,384]{2,1,0:T(2,128)} %param.25) | copy-start | bytes 9220
  93.8 21.9 %all-to-all-start.2 = ((bf16[16,64,384]{2,1,0:T(8,128)(2,1)}), bf16[16,64,384]{2,1,0:T(8,128)(2,1)S(1)}, u32[]{:S(2)}, u32[]{:S(2)}) async-start(bf16[16,64,384]{2,1,0:T(8,128)(2,1)} %bitcast.16), calls=%async_computation.2 | async-start | bytes 1572864 | tf_op jit(solution)/shard_map/all_to_all | solution.py:320

commit v6 on v5

--- a/solution.py
+++ b/solution.py
@@ -73,41 +73,18 @@
     return copies
 
 
-def keys_kernel(
-    seq_id, xh_id, k_hbm, v_hbm, tk_hbm, tv_hbm, kg_hbm, row_hbm, col_hbm, after_hbm,
-    keep_out, send_out,
-    k_ref, v_ref, tk_ref, tv_ref, kg_ref, row_ref, col_ref, sems,
-):
-    rows = row_hbm.at[:, pl.ds(seq_id[0], 1)]
-    copies = start_all(
-        ((rows, row_ref), (col_hbm, col_ref), (kg_hbm, kg_ref), (tk_hbm, tk_ref), (k_hbm, k_ref), (v_hbm, v_ref), (tv_hbm, tv_ref)),
-        sems,
-    )
-    for copy in copies[:5]:
-        copy.wait()
-    table = rope_of(row_ref, col_ref)
-    own = xh_id[0]
-    for out, p in ((send_out, 1 - own), (keep_out, own)):
-        for h in range(HPD):
-            hs = slice(h * HD, (h + 1) * HD)
-            out[0, 0:TT, hs] = normed(tk_ref[p, :, hs], kg_ref[1:2]).astype(BF)
-            out[0, TT:TK, hs] = rotated(normed(k_ref[p, :, hs], kg_ref[0:1]), table).astype(BF)
-    for copy in copies[5:]:
-        copy.wait()
-    for out, p in ((send_out, 1 - own), (keep_out, own)):
-        out[1, 0:TT, :] = tv_ref[p]
-        out[1, TT:TK, :] = v_ref[p]
-
-
-def queries_kernel(
-    seq_id, guide_id, q_hbm, hid_hbm, gate_hbm, qg_hbm, row_hbm, col_hbm,
-    q_out, side_out,
-    q_ref, hid_ref, gate_ref, qg_ref, row_ref, col_ref, sems,
+def prepare_kernel(
+    seq_id, xh_id, guide_id, k_hbm, q_hbm, v_hbm, tk_hbm, tv_hbm, hid_hbm, gate_hbm, qg_hbm, kg_hbm, row_hbm, col_hbm,
+    keep_out, send_out, q_out, side_out,
+    k_ref, q_ref, v_ref, tk_ref, tv_ref, hid_ref, gate_ref, qg_ref, kg_ref, row_ref, col_ref, sems,
 ):
     other = 1 - guide_id[0]
     rows = row_hbm.at[:, pl.ds(seq_id[0], 1)]
     copies = start_all(
-        ((rows, row_ref), (col_hbm, col_ref), (qg_hbm, qg_ref), (q_hbm, q_ref), (hid_hbm.at[other], hid_ref), (gate_hbm, gate_ref)),
+        (
+            (rows, row_ref), (col_hbm, col_ref), (qg_hbm, qg_ref), (q_hbm, q_ref), (kg_hbm, kg_ref), (tk_hbm, tk_ref), (k_hbm, k_ref),
+            (v_hbm, v_ref), (tv_hbm, tv_ref), (hid_hbm.at[other], hid_ref), (gate_hbm, gate_ref),
+        ),
         sems,
     )
     for copy in copies[:4]:
@@ -119,8 +96,19 @@
             q = rotated(normed(q_ref[p, :, hs], qg_ref[...]), table).astype(BF)
             for z in range(NZ):
                 q_out[p * NZ + z, :, hs] = q
-    for copy in copies[4:]:
-        copy.wait()
+    for copy in copies[4:7]:
+        copy.wait()
+    own = xh_id[0]
+    for out, p in ((keep_out, own), (send_out, 1 - own)):
+        for h in range(HPD):
+            hs = slice(h * HD, (h + 1) * HD)
+            out[0, 0:TT, hs] = normed(tk_ref[p, :, hs], kg_ref[1:2]).astype(BF)
+            out[0, TT:TK, hs] = rotated(normed(k_ref[p, :, hs], kg_ref[0:1]), table).astype(BF)
+    for copy in copies[7:]:
+        copy.wait()
+    for out, p in ((keep_out, own), (send_out, 1 - own)):
+        out[1, 0:TT, :] = tv_ref[p]
+        out[1, TT:TK, :] = v_ref[p]
     side_out[0:TQ, :] = hid_ref[...]
     hi, mid, lo = split3(gate_ref[pl.ds(other, 1), :])
     rows = lax.broadcasted_iota(jnp.int32, (8, W), 0)
@@ -128,7 +116,21 @@
     side_out[TQ : TQ + 8, :] = packed.astype(BF)
 
 
-def attend_kernel(xh_id, z0_id, len_ref, q_ref, kv_ref, out_ref):
+def attend_kernel(xh_id, z0_id, len_ref, q_hbm, kv_hbm, out_hbm, q_ref, kv_ref, out_ref, in_sems, out_sems):
+    loads = []
+    for h in range(HPD):
+        hs = slice(h * HD, (h + 1) * HD)
+        loads.append(
+            start_all(
+                (
+                    (q_hbm.at[:, :, hs], q_ref.at[:, :, hs]),
+                    (kv_hbm.at[:, :, 0, :, hs], kv_ref.at[:, :, 0, :, hs]),
+                    (kv_hbm.at[:, :, 1, :, hs], kv_ref.at[:, :, 1, :, hs]),
+                ),
+                in_sems.at[h],
+            )
+        )
+    stores = []
     scale = HD ** (-0.5) * 1.4426950408889634
     own = xh_id[0]
     at = lax.broadcasted_iota(jnp.int32, (1, NS * TK), 1)
@@ -144,16 +146,20 @@
     stats = jnp.zeros((NS * TQ, HD), F32)
     for h in range(HPD):
         hs = slice(h * HD, (h + 1) * HD)
+        loads[h][0].wait()
+        loads[h][1].wait()
         q = q_ref[:, :, hs].reshape(NS * TQ, HD)
         k = kv_ref[:, :, 0, :, hs].reshape(NS * TK, HD)
-        v = kv_ref[:, :, 1, :, hs].reshape(NS * TK, HD)
         s = lax.dot_general(q, k, (((1,), (1,)), ((), ())), preferred_element_type=F32)
         s = s * scale + bias
         top = jnp.max(s, -1, keepdims=True)
         e = jnp.exp2(s - top)
         total = jnp.sum(e, -1, keepdims=True)
+        loads[h][2].wait()
+        v = kv_ref[:, :, 1, :, hs].reshape(NS * TK, HD)
         o = jnp.dot(e.astype(BF), v, preferred_element_type=F32) / total
         out_ref[:, 0:TQ, hs] = o.astype(BF).reshape(NS, TQ, HD)
+        stores += start_all(((out_ref.at[:, 0:TQ, hs], out_hbm.at[:, 0:TQ, hs]),), out_sems.at[pl.ds(h, 1)])
         lse = top + jnp.log2(total)
         hi = lse.astype(BF).astype(F32)
         stats = jnp.where(lane == h, hi, jnp.where(lane == HPD + h, lse - hi, stats))
@@ -162,6 +168,10 @@
         a = (d // 2) * HD
         out_ref[d, TQ : TQ + STAT, 0:HD] = rows[:, a : a + HD]
         out_ref[d, TQ : TQ + STAT, HD:W] = jnp.zeros((STAT, W - HD), BF)
+    tail = slice(TQ, TQ + STAT)
+    stores += start_all(((out_ref.at[:, tail], out_hbm.at[:, tail]),), out_sems.at[pl.ds(HPD, 1)])
+    for copy in stores:
+        copy.wait()
 
 
 def project_kernel(ids, o_ref, w_ref, out_hbm, attn_ref, out_ref, sems):
@@ -258,57 +268,67 @@
     seq = (xh * NZ + z1) * NZ + z0
     rows, cols = rope_tables()
     kv_shape = jax.ShapeDtypeStruct((2, TK, W), BF)
-    row_t = jnp.asarray(rows)
-    col_t = jnp.asarray(cols)
-    rope_scratch = [pltpu.VMEM((2, 1, HD), F32), pltpu.VMEM((2, TQ, HD), F32)]
-    q, side = call(
-        queries_kernel,
-        (jax.ShapeDtypeStruct((NS, TQ, W), BF), jax.ShapeDtypeStruct((TQ + 8, W), BF)),
-        [SMEM()] * 2 + [HBM()] * 6,
-        (VMEM(),) * 2,
-        "queries",
+    keep, send, q, side = call(
+        prepare_kernel,
+        (kv_shape, kv_shape, jax.ShapeDtypeStruct((NS, TQ, W), BF), jax.ShapeDtypeStruct((TQ + 8, W), BF)),
+        [SMEM()] * 3 + [HBM()] * 11,
+        (VMEM(),) * 4,
+        "prepare",
         [
             pltpu.VMEM((2, TQ, W), BF),
-            pltpu.VMEM((TQ, W), BF),
-            pltpu.VMEM((2, W), F32),
-            pltpu.VMEM((1, HD), F32),
-            *rope_scratch,
-            pltpu.SemaphoreType.DMA((6,)),
-        ],
-        63 * 1024 * 1024,
-    )(seq[None], guide[None], img_query[0], img_hidden[0], gate[0], query_gain[None], row_t, col_t)
-    keep, send = call(
-        keys_kernel,
-        (kv_shape, kv_shape),
-        [SMEM()] * 2 + [HBM()] * 8,
-        (VMEM(),) * 2,
-        "keys",
-        [
             pltpu.VMEM((2, TQ, W), BF),
             pltpu.VMEM((2, TQ, W), BF),
             pltpu.VMEM((2, TT, W), BF),
             pltpu.VMEM((2, TT, W), BF),
+            pltpu.VMEM((TQ, W), BF),
+            pltpu.VMEM((2, W), F32),
+            pltpu.VMEM((1, HD), F32),
             pltpu.VMEM((2, HD), F32),
-            *rope_scratch,
-            pltpu.SemaphoreType.DMA((7,)),
+            pltpu.VMEM((2, 1, HD), F32),
+            pltpu.VMEM((2, TQ, HD), F32),
+            pltpu.SemaphoreType.DMA((11,)),
         ],
         63 * 1024 * 1024,
-    )(seq[None], xh[None], img_key[0], img_value[0], txt_key[0], txt_value[0], key_gain, row_t, col_t, q)
+    )(
+        seq[None],
+        xh[None],
+        guide[None],
+        img_key[0],
+        img_query[0],
+        img_value[0],
+        txt_key[0],
+        txt_value[0],
+        img_hidden[0],
+        gate[0],
+        query_gain[None],
+        key_gain,
+        jnp.asarray(rows),
+        jnp.asarray(cols),
+    )
     q = lax.all_to_all(q, ("xh", "z0"), 0, 0, tiled=True)
     swap = [(0, 1), (1, 0)]
     got = lax.ppermute(send, "xh", swap)
-    side = lax.ppermute(side, "g", swap)
-    got, side = lax.optimization_barrier((got, side))
     kv = lax.all_gather(jnp.stack([keep, got]), "z1", axis=0)
 
     out = call(
         attend_kernel,
         jax.ShapeDtypeStruct((NS, TQ + STAT, W), BF),
-        [SMEM()] * 3 + [VMEM()] * 2,
-        VMEM(),
+        [SMEM()] * 3 + [HBM()] * 2,
+        HBM(),
         "attend",
+        [
+            pltpu.VMEM((NS, TQ, W), BF),
+            pltpu.VMEM((NZ, 2, 2, TK, W), BF),
+            pltpu.VMEM((NS, TQ + STAT, W), BF),
+            pltpu.SemaphoreType.DMA((HPD, 3)),
+            pltpu.SemaphoreType.DMA((HPD + 1,)),
+        ],
+        63 * 1024 * 1024,
     )(xh[None], z0[None], text_len, q, kv)
+    out, side = lax.optimization_barrier((out, side))
+    side = lax.ppermute(side, "g", swap)
     out = lax.all_to_all(out, ("xh", "z0"), 0, 0, tiled=True)
+    out, side = lax.optimization_barrier((out, side))
     part = call(
         project_kernel,
         jax.ShapeDtypeStruct((2, 8, TQ, W), BF),

time: 118 us -> 119 us (level)
  starting transfers between devices: 28.5 us -> 44.8 us
  blocking collectives: 46.1 us -> 30.9 us
  waiting for transfers between devices: 26.6 us -> 24.3 us
  local copies, waits for them, and re-layouts: 1.39 us -> 3.04 us
    all_to_all x1, starting transfers between devices: 3.47 us -> 19.1 us  [shards(): out = lax.all_to_all(out, ('xh', 'z0'), 0, 0, tiled=True)]
    all_gather x1, blocking collectives: 46.1 us -> 30.9 us  [shards(): kv = lax.all_gather(jnp.stack([keep, got]), 'z1', axis=0)]
    all_to_all x1, waiting for transfers between devices: 11.6 us -> 6.05 us  [shards(): out = lax.all_to_all(out, ('xh', 'z0'), 0, 0, tiled=True)]
    ppermute x1, waiting for transfers between devices: 0.01 us -> 4.29 us  [shards(): got = lax.ppermute(send, 'xh', swap)]
    pallas_call x1, Pallas kernels: 3.15 us -> 5.79 us  [shards(): call(attend_kernel, jax.ShapeDtypeStruct((NS, TQ + STAT, W), BF), [SMEM()...]
    unnamed x16, local copies, waits for them, and re-layouts: 0.8 us -> 2.45 us
    pallas_call x2 -> x1, Pallas kernels: 4.71 us -> 3.07 us  [shards(): call(prepare_kernel, (kv_shape, kv_shape, jax.ShapeDtypeStruct((NS, TQ, W...]
  transfers between devices with their start and end apart: 5 -> 5, of which waited for: 3 -> 4; matrix products, arithmetic and copies ran while one was open for 2% -> 2% of each run, Pallas kernels for 2% -> 0%
where the time goes in v6:
time: 119 us
  starting transfers between devices  44.8 us (38%)
  blocking collectives  30.9 us (26%)
  waiting for transfers between devices  24.3 us (20%)
  Pallas kernels  12.3 us (10%)
  local copies, waits for them, and re-layouts  3.04 us (3%)
  other arithmetic  1.65 us (1%)
  between operations  1.5 us (1%)
    all_gather x1, blocking collectives, shards(): kv = lax.all_gather(jnp.stack([keep, got]), 'z1', axis=0)  30.9 us
    all_to_all x1, starting transfers between devices, shards(): out = lax.all_to_all(out, ('xh', 'z0'), 0, 0, tiled=True)  19.1 us
    all_to_all x1, waiting for transfers between devices, shards(): lax.all_to_all(part.reshape(16, TQ, W), ('g', 'y', 'c'), 0, 0, tiled=True)  10.9 us
    all_to_all x1, starting transfers between devices, shards(): lax.all_to_all(part.reshape(16, TQ, W), ('g', 'y', 'c'), 0, 0, tiled=True)  9.26 us
    all_to_all x1, starting transfers between devices, shards(): q = lax.all_to_all(q, ('xh', 'z0'), 0, 0, tiled=True)  8.92 us
    all_to_all x1, waiting for transfers between devices, shards(): out = lax.all_to_all(out, ('xh', 'z0'), 0, 0, tiled=True)  6.05 us
    pallas_call x1, Pallas kernels, shards(): call(attend_kernel, jax.ShapeDtypeStruct((NS, TQ + STAT, W), BF), [SMEM()...  5.79 us
    ppermute x1, starting transfers between devices, shards(): got = lax.ppermute(send, 'xh', swap)  4.99 us
  transfers between devices with their start and end apart: 5, of which 4 were waited for; matrix products, arithmetic and copies ran while one was open for 2% of the time, Pallas kernels for 0%

profile of v6, /device:TPU:1, one launch (start us, length us, event | category | flops | bytes accessed | tf_op | source)
XLA Modules:
  0.0 118.5 jit_solution(3024507328555638623)
XLA Ops:
  0.6 3.1 %prepare.1 = (bf16[2,80,384]{2,1,0:T(8,128)(2,1)}, bf16[2,80,384]{2,1,0:T(8,128)(2,1)}, bf16[8,64,384]{2,1,0:T(8,128)(2,1)}, bf16[72,384]{1,0:T(8,128)(2,1)}) custom-call(s32[1]{0:T(128)} %bitcast.4.seq_id, s32[1]{0:T(128)} %bitcast.2.xh_id, s32[1]{0:T(128)} %bitcast.guide_id.ids, bf16[2,64,384]{2,1,0:T(8,128)(2,1)} %bitcast.24, ...), custom_call_target="tpu_custom_call" | custom-call | tf_op jit(solution)/shard_map/prepare/pallas_call | solution.py:271
  3.7 8.9 %all-to-all-start = ((bf16[8,64,384]{2,1,0:T(8,128)(2,1)}), bf16[8,64,384]{2,1,0:T(8,128)(2,1)S(1)}, u32[]{:S(2)}, u32[]{:S(2)}) async-start(bf16[8,64,384]{2,1,0:T(8,128)(2,1)} %get-tuple-element.10), calls=%async_computation | async-start | bytes 786432 | tf_op jit(solution)/shard_map/all_to_all | solution.py:308
  12.6 0.0 copy-start.6
  12.7 5.0 %collective-permute-start = (bf16[2,80,384]{2,1,0:T(8,128)(2,1)}, bf16[2,80,384]{2,1,0:T(8,128)(2,1)S(1)}, u32[]{:S(2)}, u32[]{:S(2)}) collective-permute-start(bf16[2,80,384]{2,1,0:T(8,128)(2,1)} %get-tuple-element.12), channel_id=1, source_target_pairs={{0,128},{128,0},{1,129},{129,1},{2,130},{130,2},{3,131},{131,3},{4... | collective-permute-start | bytes 368648 | tf_op jit(solution)/shard_map/ppermute | solution.py:310
  17.7 4.3 %collective-permute-done = bf16[2,80,384]{2,1,0:T(8,128)(2,1)S(1)} collective-permute-done((bf16[2,80,384]{2,1,0:T(8,128)(2,1)}, bf16[2,80,384]{2,1,0:T(8,128)(2,1)S(1)}, u32[]{:S(2)}, u32[]{:S(2)}) %collective-permute-start) | collective-permute-done | bytes 122912 | tf_op jit(solution)/shard_map/ppermute | solution.py:310
  21.9 0.9 pad_maximum_fusion
  22.9 30.9 %all-gather = bf16[8,2,80,384]{3,2,1,0:T(8,128)(2,1)} all-gather(bf16[2,2,80,384]{3,2,1,0:T(8,128)(2,1)S(1)} %pad_maximum_fusion), channel_id=2, replica_groups=mesh['g'=2,'xh'=2,'z1'=4,'z0'=4,'y'=4,'c'=2] {'z1'}, dimensions={0}, use_global_device_ids=true | all-gather | bytes 1228800 | tf_op jit(solution)/shard_map/all_gather | solution.py:311
  53.8 0.0 all-to-all-done.q_hbm
  53.8 0.8 copy-done.4
  54.5 5.8 %attend.1 = bf16[8,72,384]{2,1,0:T(8,128)(2,1)} custom-call(s32[1]{0:T(128)} %bitcast.2.xh_id, s32[1]{0:T(128)} %bitcast.3.z0_id, s32[2]{0:T(128)} %len_ref.1, bf16[8,64,384]{2,1,0:T(8,128)(2,1)} %copy-done.4, bf16[4,2,2,80,384]{4,3,2,1,0:T(8,128)(2,1)} %bitcast.21), custom_call_target="tpu_custom_call" | custom-call | tf_op jit(solution)/shard_map/attend/pallas_call | solution.py:313
  60.3 19.1 %all-to-all-start.1 = ((bf16[8,72,384]{2,1,0:T(8,128)(2,1)}), bf16[8,72,384]{2,1,0:T(8,128)(2,1)S(1)}, u32[]{:S(2)}, u32[]{:S(2)}) async-start(bf16[8,72,384]{2,1,0:T(8,128)(2,1)} %attend.1), calls=%async_computation.1 | async-start | bytes 884736 | tf_op jit(solution)/shard_map/all_to_all | solution.py:330
  79.4 0.0 copy-done.6
  79.4 2.6 %collective-permute-start.1 = (bf16[72,384]{1,0:T(8,128)(2,1)S(1)}, bf16[72,384]{1,0:T(8,128)(2,1)S(1)}, u32[]{:S(2)}, u32[]{:S(2)}) collective-permute-start(bf16[72,384]{1,0:T(8,128)(2,1)S(1)} %copy-done.6), channel_id=1, source_target_pairs={{0,256},{256,0},{1,257},{257,1},{2,258},{258,2},{3,259},{259,3},{4... | collective-permute-start | bytes 165896 | tf_op jit(solution)/shard_map/ppermute | solution.py:329
  82.0 3.1 %collective-permute-done.1.side_ref = bf16[72,384]{1,0:T(8,128)(2,1)S(1)} collective-permute-done((bf16[72,384]{1,0:T(8,128)(2,1)S(1)}, bf16[72,384]{1,0:T(8,128)(2,1)S(1)}, u32[]{:S(2)}, u32[]{:S(2)}) %collective-permute-start.1) | collective-permute-done | bytes 55328 | tf_op jit(solution)/shard_map/ppermute | solution.py:329
  85.1 6.0 %all-to-all-done.1.o_ref = bf16[8,72,384]{2,1,0:T(8,128)(2,1)S(1)} async-done(((bf16[8,72,384]{2,1,0:T(8,128)(2,1)}), bf16[8,72,384]{2,1,0:T(8,128)(2,1)S(1)}, u32[]{:S(2)}, u32[]{:S(2)}) %all-to-all-start.1) | async-done | bytes 442400 | tf_op jit(solution)/shard_map/all_to_all | solution.py:330
  91.1 0.0 copy-start
  91.1 1.7 %copy-done = bf16[384,3072]{1,0:T(8,128)(2,1)S(1)} copy-done((bf16[384,3072]{1,0:T(8,128)(2,1)S(1)}, bf16[384,3072]{1,0:T(8,128)(2,1)}, u32[]{:S(2)}) %copy-start) | copy-done | bytes 2359320
  92.8 0.0 copy-start.5
  92.8 0.0 copy-start.7
  92.8 0.0 copy-start.1
  92.8 0.0 copy-start.3
  92.8 2.1 %project.1 = bf16[2,8,64,384]{3,2,1,0:T(8,128)(2,1)} custom-call(s32[1]{0:T(128)} %bitcast.1.ids, bf16[8,72,384]{2,1,0:T(8,128)(2,1)S(1)} %all-to-all-done.1.o_ref, bf16[384,3072]{1,0:T(8,128)(2,1)S(1)} %copy-done), custom_call_target="tpu_custom_call" | custom-call | tf_op jit(solution)/shard_map/project/pallas_call | solution.py:332
  94.9 9.3 %all-to-all-start.2 = ((bf16[16,64,384]{2,1,0:T(8,128)(2,1)}), bf16[16,64,384]{2,1,0:T(8,128)(2,1)S(1)}, u32[]{:S(2)}, u32[]{:S(2)}) async-start(bf16[16,64,384]{2,1,0:T(8,128)(2,1)} %bitcast.16), calls=%async_computation.2 | async-start | bytes 1572864 | tf_op jit(solution)/shard_map/all_to_all | solution.py:340
  104.9 0.0 copy-done.5
  104.9 0.0 copy-done.7
  104.9 0.6 dynamic_slice.3
  105.6 0.7 pad_maximum_fusion.1.scal
  106.3 10.9 %all-to-all-done.2.part_ref = bf16[16,64,384]{2,1,0:T(8,128)(2,1)S(1)} async-done(((bf16[16,64,384]{2,1,0:T(8,128)(2,1)}), bf16[16,64,384]{2,1,0:T(8,128)(2,1)S(1)}, u32[]{:S(2)}, u32[]{:S(2)}) %all-to-all-start.2) | async-done | bytes 786464 | tf_op jit(solution)/shard_map/all_to_all | solution.py:340
  117.2 0.0 copy-done.1
  117.2 0.0 copy-done.2
  117.2 0.0 copy-done.3
  117.2 1.3 %finish.1 = (bf16[1,64,384]{2,1,0:T(8,128)(2,1)}, bf16[1,64,384]{2,1,0:T(8,128)(2,1)}) custom-call(s32[1]{0:T(128)} %bitcast.guide_id.ids, f32[2]{0:T(128)S(1)} %pad_maximum_fusion.1.scal, bf16[16,64,384]{2,1,0:T(8,128)(2,1)S(1)} %all-to-all-done.2.part_ref, bf16[2,64,384]{2,1,0:T(8,128)(2,1)S(1)} %bitcast.18, f32[2,384]{1,0:T(2,128)S(1)} %bitcast.20, ...), custom_call_target="tpu_custom_call" | custom-call | tf_op jit(solution)/shard_map/finish/pallas_call | solution.py:346
  (3 shorter events, 0.0 us)
Async XLA Ops:
  3.7 50.0 %all-to-all-start = ((bf16[8,64,384]{2,1,0:T(8,128)(2,1)}), bf16[8,64,384]{2,1,0:T(8,128)(2,1)S(1)}, u32[]{:S(2)}, u32[]{:S(2)}) async-start(bf16[8,64,384]{2,1,0:T(8,128)(2,1)} %get-tuple-element.10), calls=%async_computation | async-start | bytes 786432 | tf_op jit(solution)/shard_map/all_to_all | solution.py:308
  12.6 66.7 %copy-start.6 = (bf16[72,384]{1,0:T(8,128)(2,1)S(1)}, bf16[72,384]{1,0:T(8,128)(2,1)}, u32[]{:S(2)}) copy-start(bf16[72,384]{1,0:T(8,128)(2,1)} %get-tuple-element.15) | copy-start | bytes 165892
  12.7 9.3 %collective-permute-start = (bf16[2,80,384]{2,1,0:T(8,128)(2,1)}, bf16[2,80,384]{2,1,0:T(8,128)(2,1)S(1)}, u32[]{:S(2)}, u32[]{:S(2)}) collective-permute-start(bf16[2,80,384]{2,1,0:T(8,128)(2,1)} %get-tuple-element.12), channel_id=1, source_target_pairs={{0,128},{128,0},{1,129},{129,1},{2,130},{130,2},{3,131},{131,3},{4... | collective-permute-start | bytes 368648 | tf_op jit(solution)/shard_map/ppermute | solution.py:310
  53.8 0.8 copy-start.4
  60.3 30.8 %all-to-all-start.1 = ((bf16[8,72,384]{2,1,0:T(8,128)(2,1)}), bf16[8,72,384]{2,1,0:T(8,128)(2,1)S(1)}, u32[]{:S(2)}, u32[]{:S(2)}) async-start(bf16[8,72,384]{2,1,0:T(8,128)(2,1)} %attend.1), calls=%async_computation.1 | async-start | bytes 884736 | tf_op jit(solution)/shard_map/all_to_all | solution.py:330
  79.4 5.7 %collective-permute-start.1 = (bf16[72,384]{1,0:T(8,128)(2,1)S(1)}, bf16[72,384]{1,0:T(8,128)(2,1)S(1)}, u32[]{:S(2)}, u32[]{:S(2)}) collective-permute-start(bf16[72,384]{1,0:T(8,128)(2,1)S(1)} %copy-done.6), channel_id=1, source_target_pairs={{0,256},{256,0},{1,257},{257,1},{2,258},{258,2},{3,259},{259,3},{4... | collective-permute-start | bytes 165896 | tf_op jit(solution)/shard_map/ppermute | solution.py:329
  91.1 1.7 %copy-start = (bf16[384,3072]{1,0:T(8,128)(2,1)S(1)}, bf16[384,3072]{1,0:T(8,128)(2,1)}, u32[]{:S(2)}) copy-start(bf16[384,3072]{1,0:T(8,128)(2,1)} %w_ref.1) | copy-start | bytes 7077892
  92.8 12.1 %copy-start.5 = (f32[384]{0:T(512)S(1)}, f32[384]{0:T(512)}, u32[]{:S(2)}) copy-start(f32[384]{0:T(512)} %param.27) | copy-start | bytes 4612
  92.8 12.1 %copy-start.7 = (f32[2]{0:T(128)S(1)}, f32[2]{0:T(128)}, u32[]{:S(2)}) copy-start(f32[2]{0:T(128)} %param.28) | copy-start | bytes 28
  92.8 24.4 %copy-start.1 = (bf16[1,2,64,384]{3,2,1,0:T(8,128)(2,1)S(1)}, bf16[1,2,64,384]{3,2,1,0:T(8,128)(2,1)}, u32[]{:S(2)}) copy-start(bf16[1,2,64,384]{3,2,1,0:T(8,128)(2,1)} %param.17) | copy-start | bytes 294916
  92.8 24.4 %copy-start.2 = (bf16[1,64,384]{2,1,0:T(8,128)(2,1)S(1)}, bf16[1,64,384]{2,1,0:T(8,128)(2,1)}, u32[]{:S(2)}) copy-start(bf16[1,64,384]{2,1,0:T(8,128)(2,1)} %lat_ref.1) | copy-start | bytes 147460
  92.8 24.4 %copy-start.3 = (f32[1,2,384]{2,1,0:T(2,128)S(1)}, f32[1,2,384]{2,1,0:T(2,128)}, u32[]{:S(2)}) copy-start(f32[1,2,384]{2,1,0:T(2,128)} %param.25) | copy-start | bytes 9220
  94.9 22.2 %all-to-all-start.2 = ((bf16[16,64,384]{2,1,0:T(8,128)(2,1)}), bf16[16,64,384]{2,1,0:T(8,128)(2,1)S(1)}, u32[]{:S(2)}, u32[]{:S(2)}) async-start(bf16[16,64,384]{2,1,0:T(8,128)(2,1)} %bitcast.16), calls=%async_computation.2 | async-start | bytes 1572864 | tf_op jit(solution)/shard_map/all_to_all | solution.py:340

commit v7 on v6

--- a/solution.py
+++ b/solution.py
@@ -116,21 +116,12 @@
     side_out[TQ : TQ + 8, :] = packed.astype(BF)
 
 
-def attend_kernel(xh_id, z0_id, len_ref, q_hbm, kv_hbm, out_hbm, q_ref, kv_ref, out_ref, in_sems, out_sems):
-    loads = []
-    for h in range(HPD):
-        hs = slice(h * HD, (h + 1) * HD)
-        loads.append(
-            start_all(
-                (
-                    (q_hbm.at[:, :, hs], q_ref.at[:, :, hs]),
-                    (kv_hbm.at[:, :, 0, :, hs], kv_ref.at[:, :, 0, :, hs]),
-                    (kv_hbm.at[:, :, 1, :, hs], kv_ref.at[:, :, 1, :, hs]),
-                ),
-                in_sems.at[h],
-            )
-        )
-    stores = []
+def join_kernel(keep_ref, got_ref, out_ref):
+    out_ref[0] = keep_ref[...]
+    out_ref[1] = got_ref[...]
+
+
+def attend_kernel(xh_id, z0_id, len_ref, q_ref, kv_ref, out_ref):
     scale = HD ** (-0.5) * 1.4426950408889634
     own = xh_id[0]
     at = lax.broadcasted_iota(jnp.int32, (1, NS * TK), 1)
@@ -146,20 +137,16 @@
     stats = jnp.zeros((NS * TQ, HD), F32)
     for h in range(HPD):
         hs = slice(h * HD, (h + 1) * HD)
-        loads[h][0].wait()
-        loads[h][1].wait()
         q = q_ref[:, :, hs].reshape(NS * TQ, HD)
         k = kv_ref[:, :, 0, :, hs].reshape(NS * TK, HD)
+        v = kv_ref[:, :, 1, :, hs].reshape(NS * TK, HD)
         s = lax.dot_general(q, k, (((1,), (1,)), ((), ())), preferred_element_type=F32)
         s = s * scale + bias
         top = jnp.max(s, -1, keepdims=True)
         e = jnp.exp2(s - top)
         total = jnp.sum(e, -1, keepdims=True)
-        loads[h][2].wait()
-        v = kv_ref[:, :, 1, :, hs].reshape(NS * TK, HD)
         o = jnp.dot(e.astype(BF), v, preferred_element_type=F32) / total
         out_ref[:, 0:TQ, hs] = o.astype(BF).reshape(NS, TQ, HD)
-        stores += start_all(((out_ref.at[:, 0:TQ, hs], out_hbm.at[:, 0:TQ, hs]),), out_sems.at[pl.ds(h, 1)])
         lse = top + jnp.log2(total)
         hi = lse.astype(BF).astype(F32)
         stats = jnp.where(lane == h, hi, jnp.where(lane == HPD + h, lse - hi, stats))
@@ -168,10 +155,6 @@
         a = (d // 2) * HD
         out_ref[d, TQ : TQ + STAT, 0:HD] = rows[:, a : a + HD]
         out_ref[d, TQ : TQ + STAT, HD:W] = jnp.zeros((STAT, W - HD), BF)
-    tail = slice(TQ, TQ + STAT)
-    stores += start_all(((out_ref.at[:, tail], out_hbm.at[:, tail]),), out_sems.at[pl.ds(HPD, 1)])
-    for copy in stores:
-        copy.wait()
 
 
 def project_kernel(ids, o_ref, w_ref, out_hbm, attn_ref, out_ref, sems):
@@ -232,7 +215,7 @@
 HBM = functools.partial(pl.BlockSpec, memory_space=pltpu.HBM)
 
 
-def call(kernel, outs, ins, out_specs, name, scratch=(), limit=VMEM_LIMIT):
+def call(kernel, outs, ins, out_specs, name, scratch=(), limit=VMEM_LIMIT, cost=None):
     return pl.pallas_call(
         kernel,
         out_shape=outs,
@@ -240,6 +223,7 @@
         out_specs=out_specs,
         scratch_shapes=list(scratch),
         compiler_params=pltpu.CompilerParams(vmem_limit_bytes=limit),
+        cost_estimate=cost,
         name=name,
     )
 
@@ -308,22 +292,22 @@
     q = lax.all_to_all(q, ("xh", "z0"), 0, 0, tiled=True)
     swap = [(0, 1), (1, 0)]
     got = lax.ppermute(send, "xh", swap)
-    kv = lax.all_gather(jnp.stack([keep, got]), "z1", axis=0)
+    kv = call(
+        join_kernel,
+        jax.ShapeDtypeStruct((2, 2, TK, W), BF),
+        [VMEM()] * 2,
+        VMEM(),
+        "join",
+        cost=pl.CostEstimate(flops=10**11, bytes_accessed=10**6, transcendentals=0),
+    )(keep, got)
+    kv = lax.all_gather(kv, "z1", axis=0)
 
     out = call(
         attend_kernel,
         jax.ShapeDtypeStruct((NS, TQ + STAT, W), BF),
-        [SMEM()] * 3 + [HBM()] * 2,
-        HBM(),
+        [SMEM()] * 3 + [VMEM()] * 2,
+        VMEM(),
         "attend",
-        [
-            pltpu.VMEM((NS, TQ, W), BF),
-            pltpu.VMEM((NZ, 2, 2, TK, W), BF),
-            pltpu.VMEM((NS, TQ + STAT, W), BF),
-            pltpu.SemaphoreType.DMA((HPD, 3)),
-            pltpu.SemaphoreType.DMA((HPD + 1,)),
-        ],
-        63 * 1024 * 1024,
     )(xh[None], z0[None], text_len, q, kv)
     out, side = lax.optimization_barrier((out, side))
     side = lax.ppermute(side, "g", swap)

time: 119 us -> 114 us (0.958)
  waiting for transfers between devices: 24.3 us -> 19.9 us
  starting transfers between devices: 44.8 us -> 48.1 us
  Pallas kernels: 12.3 us -> 9.78 us
    all_to_all x1, starting transfers between devices: 19.1 us -> 25.4 us  [shards(): out = lax.all_to_all(out, ('xh', 'z0'), 0, 0, tiled=True)]
    ppermute x1, waiting for transfers between devices: 4.29 us -> 0.01 us  [shards(): got = lax.ppermute(send, 'xh', swap)]
    all_to_all x1, starting transfers between devices: 8.92 us -> 5.63 us  [shards(): q = lax.all_to_all(q, ('xh', 'z0'), 0, 0, tiled=True)]
    pallas_call x1, Pallas kernels: 5.79 us -> 3.18 us  [shards(): call(attend_kernel, jax.ShapeDtypeStruct((NS, TQ + STAT, W), BF), [SMEM()...]
    unnamed x16 -> x20, local copies, waits for them, and re-layouts: 2.45 us -> 1.7 us
  transfers between devices with their start and end apart: 5 -> 5, of which waited for: 4 -> 3; matrix products, arithmetic and copies ran while one was open for 2% -> 1% of each run, Pallas kernels for 0% -> 0%
where the time goes in v7:
time: 114 us; the launch traced here: 113 us
  starting transfers between devices  48.1 us (42%)
  blocking collectives  30.6 us (27%)
  waiting for transfers between devices  19.9 us (17%)
  Pallas kernels  9.78 us (9%)
  local copies, waits for them, and re-layouts  2.29 us (2%)
  between operations  1.54 us (1%)
    all_gather x1, blocking collectives, shards(): kv = lax.all_gather(kv, 'z1', axis=0)  30.6 us
    all_to_all x1, starting transfers between devices, shards(): out = lax.all_to_all(out, ('xh', 'z0'), 0, 0, tiled=True)  25.4 us
    all_to_all x1, waiting for transfers between devices, shards(): lax.all_to_all(part.reshape(16, TQ, W), ('g', 'y', 'c'), 0, 0, tiled=True)  10.9 us
    all_to_all x1, starting transfers between devices, shards(): lax.all_to_all(part.reshape(16, TQ, W), ('g', 'y', 'c'), 0, 0, tiled=True)  9.74 us
    all_to_all x1, starting transfers between devices, shards(): q = lax.all_to_all(q, ('xh', 'z0'), 0, 0, tiled=True)  5.63 us
    ppermute x1, starting transfers between devices, shards(): got = lax.ppermute(send, 'xh', swap)  5.48 us
    all_to_all x1, waiting for transfers between devices, shards(): out = lax.all_to_all(out, ('xh', 'z0'), 0, 0, tiled=True)  5.04 us
    ppermute x1, waiting for transfers between devices, shards(): side = lax.ppermute(side, 'g', swap)  3.92 us
  transfers between devices with their start and end apart: 5, of which 3 were waited for; matrix products, arithmetic and copies ran while one was open for 1% of the time, Pallas kernels for 0%

profile of v7, /device:TPU:1, one launch (start us, length us, event | category | flops | bytes accessed | tf_op | source)
XLA Modules:
  0.0 113.0 jit_solution(2363282436375598660)
XLA Ops:
  0.6 3.1 %prepare.1 = (bf16[2,80,384]{2,1,0:T(8,128)(2,1)}, bf16[2,80,384]{2,1,0:T(8,128)(2,1)}, bf16[8,64,384]{2,1,0:T(8,128)(2,1)}, bf16[72,384]{1,0:T(8,128)(2,1)}) custom-call(s32[1]{0:T(128)} %bitcast.4.seq_id, s32[1]{0:T(128)} %bitcast.2.xh_id, s32[1]{0:T(128)} %bitcast.guide_id.ids, bf16[2,64,384]{2,1,0:T(8,128)(2,1)} %bitcast.20, ...), custom_call_target="tpu_custom_call" | custom-call | tf_op jit(solution)/shard_map/prepare/pallas_call | solution.py:255
  3.8 5.5 %collective-permute-start = (bf16[2,80,384]{2,1,0:T(8,128)(2,1)}, bf16[2,80,384]{2,1,0:T(8,128)(2,1)S(1)}, u32[]{:S(2)}, u32[]{:S(2)}) collective-permute-start(bf16[2,80,384]{2,1,0:T(8,128)(2,1)} %get-tuple-element.12), channel_id=1, source_target_pairs={{0,128},{128,0},{1,129},{129,1},{2,130},{130,2},{3,131},{131,3},{4... | collective-permute-start | bytes 368648 | tf_op jit(solution)/shard_map/ppermute | solution.py:294
  9.2 5.6 %all-to-all-start = ((bf16[8,64,384]{2,1,0:T(8,128)(2,1)}), bf16[8,64,384]{2,1,0:T(8,128)(2,1)}, u32[]{:S(2)}, u32[]{:S(2)}) async-start(bf16[8,64,384]{2,1,0:T(8,128)(2,1)} %get-tuple-element.10), calls=%async_computation | async-start | bytes 786432 | tf_op jit(solution)/shard_map/all_to_all | solution.py:292
  14.9 0.0 collective-permute-done.got_ref
  14.9 0.0 copy-start.6
  14.9 0.9 copy-done.6
  15.8 0.0 copy-start.8
  15.8 0.0 copy-start
  15.8 30.6 %all-gather = bf16[8,2,80,384]{3,2,1,0:T(8,128)(2,1)S(1)} all-gather(bf16[2,2,80,384]{3,2,1,0:T(8,128)(2,1)S(1)} %join.1), channel_id=2, replica_groups=mesh['g'=2,'xh'=2,'z1'=4,'z0'=4,'y'=4,'c'=2] {'z1'}, dimensions={0}, use_global_device_ids=true | all-gather | bytes 1228800 | tf_op jit(solution)/shard_map/all_gather | solution.py:303
  46.5 0.0 all-to-all-done.q_ref
  46.5 0.0 copy-done.5
  46.5 3.2 %attend.1 = bf16[8,72,384]{2,1,0:T(8,128)(2,1)S(1)} custom-call(s32[1]{0:T(128)} %bitcast.2.xh_id, s32[1]{0:T(128)} %bitcast.3.z0_id, s32[2]{0:T(128)S(1)} %copy-done.5, bf16[8,64,384]{2,1,0:T(8,128)(2,1)} %all-to-all-done.q_ref, bf16[4,2,2,80,384]{4,3,2,1,0:T(8,128)(2,1)S(1)} %bitcast.15), custom_call_target="tpu_custom_call" | custom-call | tf_op jit(solution)/shard_map/attend/pallas_call | solution.py:305
  49.7 0.0 copy-start.1
  49.7 0.8 copy-done.1
  50.4 25.4 %all-to-all-start.1 = ((bf16[8,72,384]{2,1,0:T(8,128)(2,1)}), bf16[8,72,384]{2,1,0:T(8,128)(2,1)S(1)}, u32[]{:S(2)}, u32[]{:S(2)}) async-start(bf16[8,72,384]{2,1,0:T(8,128)(2,1)} %copy-done.1), calls=%async_computation.1 | async-start | bytes 884736 | tf_op jit(solution)/shard_map/all_to_all | solution.py:314
  75.8 0.0 copy-done.8
  75.8 1.9 %collective-permute-start.1 = (bf16[72,384]{1,0:T(8,128)(2,1)S(1)}, bf16[72,384]{1,0:T(8,128)(2,1)S(1)}, u32[]{:S(2)}, u32[]{:S(2)}) collective-permute-start(bf16[72,384]{1,0:T(8,128)(2,1)S(1)} %copy-done.8), channel_id=1, source_target_pairs={{0,256},{256,0},{1,257},{257,1},{2,258},{258,2},{3,259},{259,3},{4... | collective-permute-start | bytes 165896 | tf_op jit(solution)/shard_map/ppermute | solution.py:313
  77.7 3.9 %collective-permute-done.1.side_ref = bf16[72,384]{1,0:T(8,128)(2,1)S(1)} collective-permute-done((bf16[72,384]{1,0:T(8,128)(2,1)S(1)}, bf16[72,384]{1,0:T(8,128)(2,1)S(1)}, u32[]{:S(2)}, u32[]{:S(2)}) %collective-permute-start.1) | collective-permute-done | bytes 55328 | tf_op jit(solution)/shard_map/ppermute | solution.py:313
  81.7 5.0 %all-to-all-done.1.o_ref = bf16[8,72,384]{2,1,0:T(8,128)(2,1)S(1)} async-done(((bf16[8,72,384]{2,1,0:T(8,128)(2,1)}), bf16[8,72,384]{2,1,0:T(8,128)(2,1)S(1)}, u32[]{:S(2)}, u32[]{:S(2)}) %all-to-all-start.1) | async-done | bytes 442400 | tf_op jit(solution)/shard_map/all_to_all | solution.py:314
  86.7 0.0 copy-done
  86.7 0.0 copy-start.3
  86.7 0.0 copy-start.4
  86.7 2.1 %project.1 = bf16[2,8,64,384]{3,2,1,0:T(8,128)(2,1)} custom-call(s32[1]{0:T(128)} %bitcast.1.ids, bf16[8,72,384]{2,1,0:T(8,128)(2,1)S(1)} %all-to-all-done.1.o_ref, bf16[384,3072]{1,0:T(8,128)(2,1)S(1)} %copy-done), custom_call_target="tpu_custom_call" | custom-call | tf_op jit(solution)/shard_map/project/pallas_call | solution.py:316
  88.9 9.7 %all-to-all-start.2 = ((bf16[16,64,384]{2,1,0:T(8,128)(2,1)}), bf16[16,64,384]{2,1,0:T(8,128)(2,1)S(1)}, u32[]{:S(2)}, u32[]{:S(2)}) async-start(bf16[16,64,384]{2,1,0:T(8,128)(2,1)} %bitcast.14), calls=%async_computation.2 | async-start | bytes 1572864 | tf_op jit(solution)/shard_map/all_to_all | solution.py:324
  99.3 0.0 copy-done.7
  99.3 0.0 copy-done.9
  99.3 0.6 dynamic_slice.3
  100.0 0.7 pad_maximum_fusion.scal
  100.7 10.9 %all-to-all-done.2.part_ref = bf16[16,64,384]{2,1,0:T(8,128)(2,1)S(1)} async-done(((bf16[16,64,384]{2,1,0:T(8,128)(2,1)}), bf16[16,64,384]{2,1,0:T(8,128)(2,1)S(1)}, u32[]{:S(2)}, u32[]{:S(2)}) %all-to-all-start.2) | async-done | bytes 786464 | tf_op jit(solution)/shard_map/all_to_all | solution.py:324
  111.6 0.0 copy-done.2
  111.6 0.0 copy-done.4
  111.6 1.3 %finish.1 = (bf16[1,64,384]{2,1,0:T(8,128)(2,1)}, bf16[1,64,384]{2,1,0:T(8,128)(2,1)}) custom-call(s32[1]{0:T(128)} %bitcast.guide_id.ids, f32[2]{0:T(128)S(1)} %pad_maximum_fusion.scal, bf16[16,64,384]{2,1,0:T(8,128)(2,1)S(1)} %all-to-all-done.2.part_ref, bf16[2,64,384]{2,1,0:T(8,128)(2,1)S(1)} %bitcast.17, f32[2,384]{1,0:T(2,128)S(1)} %bitcast.19, ...), custom_call_target="tpu_custom_call" | custom-call | tf_op jit(solution)/shard_map/finish/pallas_call | solution.py:330
  (7 shorter events, 0.0 us)
Async XLA Ops:
  3.8 11.1 %collective-permute-start = (bf16[2,80,384]{2,1,0:T(8,128)(2,1)}, bf16[2,80,384]{2,1,0:T(8,128)(2,1)S(1)}, u32[]{:S(2)}, u32[]{:S(2)}) collective-permute-start(bf16[2,80,384]{2,1,0:T(8,128)(2,1)} %get-tuple-element.12), channel_id=1, source_target_pairs={{0,128},{128,0},{1,129},{129,1},{2,130},{130,2},{3,131},{131,3},{4... | collective-permute-start | bytes 368648 | tf_op jit(solution)/shard_map/ppermute | solution.py:294
  9.2 37.2 %all-to-all-start = ((bf16[8,64,384]{2,1,0:T(8,128)(2,1)}), bf16[8,64,384]{2,1,0:T(8,128)(2,1)}, u32[]{:S(2)}, u32[]{:S(2)}) async-start(bf16[8,64,384]{2,1,0:T(8,128)(2,1)} %get-tuple-element.10), calls=%async_computation | async-start | bytes 786432 | tf_op jit(solution)/shard_map/all_to_all | solution.py:292
  14.9 0.9 copy-start.6
  15.8 30.7 %copy-start.5 = (s32[2]{0:T(128)S(1)}, s32[2]{0:T(128)}, u32[]{:S(2)}) copy-start(s32[2]{0:T(128)} %len_ref.1) | copy-start | bytes 28
  15.8 60.0 %copy-start.8 = (bf16[72,384]{1,0:T(8,128)(2,1)S(1)}, bf16[72,384]{1,0:T(8,128)(2,1)}, u32[]{:S(2)}) copy-start(bf16[72,384]{1,0:T(8,128)(2,1)} %get-tuple-element.15) | copy-start | bytes 165892
  15.8 70.9 %copy-start = (bf16[384,3072]{1,0:T(8,128)(2,1)S(1)}, bf16[384,3072]{1,0:T(8,128)(2,1)}, u32[]{:S(2)}) copy-start(bf16[384,3072]{1,0:T(8,128)(2,1)} %w_ref.1) | copy-start | bytes 7077892
  49.7 0.8 copy-start.1
  50.4 36.3 %all-to-all-start.1 = ((bf16[8,72,384]{2,1,0:T(8,128)(2,1)}), bf16[8,72,384]{2,1,0:T(8,128)(2,1)S(1)}, u32[]{:S(2)}, u32[]{:S(2)}) async-start(bf16[8,72,384]{2,1,0:T(8,128)(2,1)} %copy-done.1), calls=%async_computation.1 | async-start | bytes 884736 | tf_op jit(solution)/shard_map/all_to_all | solution.py:314
  75.8 5.9 %collective-permute-start.1 = (bf16[72,384]{1,0:T(8,128)(2,1)S(1)}, bf16[72,384]{1,0:T(8,128)(2,1)S(1)}, u32[]{:S(2)}, u32[]{:S(2)}) collective-permute-start(bf16[72,384]{1,0:T(8,128)(2,1)S(1)} %copy-done.8), channel_id=1, source_target_pairs={{0,256},{256,0},{1,257},{257,1},{2,258},{258,2},{3,259},{259,3},{4... | collective-permute-start | bytes 165896 | tf_op jit(solution)/shard_map/ppermute | solution.py:313
  86.7 12.6 %copy-start.7 = (f32[384]{0:T(512)S(1)}, f32[384]{0:T(512)}, u32[]{:S(2)}) copy-start(f32[384]{0:T(512)} %param.27) | copy-start | bytes 4612
  86.7 12.6 %copy-start.9 = (f32[2]{0:T(128)S(1)}, f32[2]{0:T(128)}, u32[]{:S(2)}) copy-start(f32[2]{0:T(128)} %param.28) | copy-start | bytes 28
  86.7 24.9 %copy-start.2 = (bf16[1,2,64,384]{3,2,1,0:T(8,128)(2,1)S(1)}, bf16[1,2,64,384]{3,2,1,0:T(8,128)(2,1)}, u32[]{:S(2)}) copy-start(bf16[1,2,64,384]{3,2,1,0:T(8,128)(2,1)} %param.17) | copy-start | bytes 294916
  86.7 24.9 %copy-start.3 = (bf16[1,64,384]{2,1,0:T(8,128)(2,1)S(1)}, bf16[1,64,384]{2,1,0:T(8,128)(2,1)}, u32[]{:S(2)}) copy-start(bf16[1,64,384]{2,1,0:T(8,128)(2,1)} %lat_ref.1) | copy-start | bytes 147460
  86.7 24.9 %copy-start.4 = (f32[1,2,384]{2,1,0:T(2,128)S(1)}, f32[1,2,384]{2,1,0:T(2,128)}, u32[]{:S(2)}) copy-start(f32[1,2,384]{2,1,0:T(2,128)} %param.25) | copy-start | bytes 9220
  88.9 22.7 %all-to-all-start.2 = ((bf16[16,64,384]{2,1,0:T(8,128)(2,1)}), bf16[16,64,384]{2,1,0:T(8,128)(2,1)S(1)}, u32[]{:S(2)}, u32[]{:S(2)}) async-start(bf16[16,64,384]{2,1,0:T(8,128)(2,1)} %bitcast.14), calls=%async_computation.2 | async-start | bytes 1572864 | tf_op jit(solution)/shard_map/all_to_all | solution.py:324

commit v8 on v7

--- a/solution.py
+++ b/solution.py
@@ -99,14 +99,14 @@
     for copy in copies[4:7]:
         copy.wait()
     own = xh_id[0]
-    for out, p in ((keep_out, own), (send_out, 1 - own)):
+    for out, p in ((keep_out.at[0], own), (send_out, 1 - own)):
         for h in range(HPD):
             hs = slice(h * HD, (h + 1) * HD)
             out[0, 0:TT, hs] = normed(tk_ref[p, :, hs], kg_ref[1:2]).astype(BF)
             out[0, TT:TK, hs] = rotated(normed(k_ref[p, :, hs], kg_ref[0:1]), table).astype(BF)
     for copy in copies[7:]:
         copy.wait()
-    for out, p in ((keep_out, own), (send_out, 1 - own)):
+    for out, p in ((keep_out.at[0], own), (send_out, 1 - own)):
         out[1, 0:TT, :] = tv_ref[p]
         out[1, TT:TK, :] = v_ref[p]
     side_out[0:TQ, :] = hid_ref[...]
@@ -116,9 +116,11 @@
     side_out[TQ : TQ + 8, :] = packed.astype(BF)
 
 
-def join_kernel(keep_ref, got_ref, out_ref):
-    out_ref[0] = keep_ref[...]
-    out_ref[1] = got_ref[...]
+def join_kernel(kv_hbm, got_hbm, out_hbm, sem):
+    del kv_hbm
+    copy = pltpu.make_async_copy(got_hbm, out_hbm.at[1], sem)
+    copy.start()
+    copy.wait()
 
 
 def attend_kernel(xh_id, z0_id, len_ref, q_ref, kv_ref, out_ref):
@@ -215,7 +217,7 @@
 HBM = functools.partial(pl.BlockSpec, memory_space=pltpu.HBM)
 
 
-def call(kernel, outs, ins, out_specs, name, scratch=(), limit=VMEM_LIMIT, cost=None):
+def call(kernel, outs, ins, out_specs, name, scratch=(), limit=VMEM_LIMIT, cost=None, aliases={}):
     return pl.pallas_call(
         kernel,
         out_shape=outs,
@@ -224,6 +226,7 @@
         scratch_shapes=list(scratch),
         compiler_params=pltpu.CompilerParams(vmem_limit_bytes=limit),
         cost_estimate=cost,
+        input_output_aliases=aliases,
         name=name,
     )
 
@@ -251,10 +254,14 @@
     z0 = lax.axis_index("z0")
     seq = (xh * NZ + z1) * NZ + z0
     rows, cols = rope_tables()
-    kv_shape = jax.ShapeDtypeStruct((2, TK, W), BF)
     keep, send, q, side = call(
         prepare_kernel,
-        (kv_shape, kv_shape, jax.ShapeDtypeStruct((NS, TQ, W), BF), jax.ShapeDtypeStruct((TQ + 8, W), BF)),
+        (
+            jax.ShapeDtypeStruct((2, 2, TK, W), BF),
+            jax.ShapeDtypeStruct((2, TK, W), BF),
+            jax.ShapeDtypeStruct((NS, TQ, W), BF),
+            jax.ShapeDtypeStruct((TQ + 8, W), BF),
+        ),
         [SMEM()] * 3 + [HBM()] * 11,
         (VMEM(),) * 4,
         "prepare",
@@ -294,17 +301,19 @@
     got = lax.ppermute(send, "xh", swap)
     kv = call(
         join_kernel,
-        jax.ShapeDtypeStruct((2, 2, TK, W), BF),
-        [VMEM()] * 2,
-        VMEM(),
+        pltpu.HBM((2, 2, TK, W), BF),
+        [HBM()] * 2,
+        HBM(),
         "join",
+        [pltpu.SemaphoreType.DMA],
         cost=pl.CostEstimate(flops=10**11, bytes_accessed=10**6, transcendentals=0),
+        aliases={0: 0},
     )(keep, got)
     kv = lax.all_gather(kv, "z1", axis=0)
 
     out = call(
         attend_kernel,
-        jax.ShapeDtypeStruct((NS, TQ + STAT, W), BF),
+        pltpu.HBM((NS, TQ + STAT, W), BF),
         [SMEM()] * 3 + [VMEM()] * 2,
         VMEM(),
         "attend",

time: 114 us -> 114 us (level)
  local copies, waits for them, and re-layouts: 2.29 us -> 0.63 us
  Pallas kernels: 9.78 us -> 11.2 us
    unnamed x20 -> x16, local copies, waits for them, and re-layouts: 1.7 us -> 0.04 us
    pallas_call x3, Pallas kernels: 6.3 us -> 7.72 us  [the longest x1 3.95 us: shards(): call(attend_kernel, pltpu.HBM((NS, TQ + STAT, W), BF), [SMEM()] * 3 + [VM...]
  transfers between devices with their start and end apart: 5 -> 5, of which waited for: 3 -> 3; matrix products, arithmetic and copies ran while one was open for 1% -> 1% of each run, Pallas kernels for 0% -> 1%
where the time goes in v8:
time: 114 us; the launch traced here: 113 us
  starting transfers between devices  47.9 us (42%)
  blocking collectives  30.5 us (27%)
  waiting for transfers between devices  20.6 us (18%)
  Pallas kernels  11.2 us (10%)
  between operations  1.53 us (1%)
    all_gather x1, blocking collectives, shards(): kv = lax.all_gather(kv, 'z1', axis=0)  30.5 us
    all_to_all x1, starting transfers between devices, shards(): out = lax.all_to_all(out, ('xh', 'z0'), 0, 0, tiled=True)  25.9 us
    all_to_all x1, waiting for transfers between devices, shards(): lax.all_to_all(part.reshape(16, TQ, W), ('g', 'y', 'c'), 0, 0, tiled=True)  10.9 us
    all_to_all x1, starting transfers between devices, shards(): lax.all_to_all(part.reshape(16, TQ, W), ('g', 'y', 'c'), 0, 0, tiled=True)  8.91 us
    all_to_all x1, waiting for transfers between devices, shards(): out = lax.all_to_all(out, ('xh', 'z0'), 0, 0, tiled=True)  5.76 us
    all_to_all x1, starting transfers between devices, shards(): q = lax.all_to_all(q, ('xh', 'z0'), 0, 0, tiled=True)  5.63 us
    ppermute x1, starting transfers between devices, shards(): got = lax.ppermute(send, 'xh', swap)  5.48 us
    ppermute x1, waiting for transfers between devices, shards(): side = lax.ppermute(side, 'g', swap)  3.97 us
  transfers between devices with their start and end apart: 5, of which 3 were waited for; matrix products, arithmetic and copies ran while one was open for 1% of the time, Pallas kernels for 1%

profile of v8, /device:TPU:1, one launch (start us, length us, event | category | flops | bytes accessed | tf_op | source)
XLA Modules:
  0.0 113.1 jit_solution(2714075902259364935)
XLA Ops:
  0.6 3.1 %prepare.1 = (bf16[2,2,80,384]{3,2,1,0:T(8,128)(2,1)}, bf16[2,80,384]{2,1,0:T(8,128)(2,1)}, bf16[8,64,384]{2,1,0:T(8,128)(2,1)}, bf16[72,384]{1,0:T(8,128)(2,1)}) custom-call(s32[1]{0:T(128)} %bitcast.4.seq_id, s32[1]{0:T(128)} %bitcast.2.xh_id, s32[1]{0:T(128)} %bitcast.guide_id.ids, bf16[2,64,384]{2,1,0:T(8,128)(2,1)} %bitcast.20, ...), custom_call_target="tpu_custom_call" | custom-call | tf_op jit(solution)/shard_map/prepare/pallas_call | solution.py:257
  3.8 5.5 %collective-permute-start = (bf16[2,80,384]{2,1,0:T(8,128)(2,1)}, bf16[2,80,384]{2,1,0:T(8,128)(2,1)S(1)}, u32[]{:S(2)}, u32[]{:S(2)}) collective-permute-start(bf16[2,80,384]{2,1,0:T(8,128)(2,1)} %get-tuple-element.12), channel_id=1, source_target_pairs={{0,128},{128,0},{1,129},{129,1},{2,130},{130,2},{3,131},{131,3},{4... | collective-permute-start | bytes 368648 | tf_op jit(solution)/shard_map/ppermute | solution.py:301
  9.3 5.6 %all-to-all-start = ((bf16[8,64,384]{2,1,0:T(8,128)(2,1)}), bf16[8,64,384]{2,1,0:T(8,128)(2,1)}, u32[]{:S(2)}, u32[]{:S(2)}) async-start(bf16[8,64,384]{2,1,0:T(8,128)(2,1)} %get-tuple-element.10), calls=%async_computation | async-start | bytes 786432 | tf_op jit(solution)/shard_map/all_to_all | solution.py:299
  14.9 0.0 collective-permute-done.got_hbm
  14.9 0.0 copy-start.4
  14.9 0.7 join.1
  15.6 0.0 copy-start.6
  15.6 0.0 copy-start
  15.6 30.5 %all-gather = bf16[8,2,80,384]{3,2,1,0:T(8,128)(2,1)S(1)} all-gather(bf16[2,2,80,384]{3,2,1,0:T(8,128)(2,1)} %join.1), channel_id=2, replica_groups=mesh['g'=2,'xh'=2,'z1'=4,'z0'=4,'y'=4,'c'=2] {'z1'}, dimensions={0}, use_global_device_ids=true | all-gather | bytes 1228800 | tf_op jit(solution)/shard_map/all_gather | solution.py:312
  46.1 0.0 all-to-all-done.q_ref
  46.1 0.0 copy-done.4
  46.1 3.9 %attend.1 = bf16[8,72,384]{2,1,0:T(8,128)(2,1)} custom-call(s32[1]{0:T(128)} %bitcast.2.xh_id, s32[1]{0:T(128)} %bitcast.3.z0_id, s32[2]{0:T(128)S(1)} %copy-done.4, bf16[8,64,384]{2,1,0:T(8,128)(2,1)} %all-to-all-done.q_ref, bf16[4,2,2,80,384]{4,3,2,1,0:T(8,128)(2,1)S(1)} %bitcast.15), custom_call_target="tpu_custom_call" | custom-call | tf_op jit(solution)/shard_map/attend/pallas_call | solution.py:314
  50.0 25.9 %all-to-all-start.1 = ((bf16[8,72,384]{2,1,0:T(8,128)(2,1)}), bf16[8,72,384]{2,1,0:T(8,128)(2,1)S(1)}, u32[]{:S(2)}, u32[]{:S(2)}) async-start(bf16[8,72,384]{2,1,0:T(8,128)(2,1)} %attend.1), calls=%async_computation.1 | async-start | bytes 884736 | tf_op jit(solution)/shard_map/all_to_all | solution.py:323
  76.0 0.0 copy-done.6
  76.0 1.9 %collective-permute-start.1 = (bf16[72,384]{1,0:T(8,128)(2,1)S(1)}, bf16[72,384]{1,0:T(8,128)(2,1)S(1)}, u32[]{:S(2)}, u32[]{:S(2)}) collective-permute-start(bf16[72,384]{1,0:T(8,128)(2,1)S(1)} %copy-done.6), channel_id=1, source_target_pairs={{0,256},{256,0},{1,257},{257,1},{2,258},{258,2},{3,259},{259,3},{4... | collective-permute-start | bytes 165896 | tf_op jit(solution)/shard_map/ppermute | solution.py:322
  77.9 4.0 %collective-permute-done.1.side_ref = bf16[72,384]{1,0:T(8,128)(2,1)S(1)} collective-permute-done((bf16[72,384]{1,0:T(8,128)(2,1)S(1)}, bf16[72,384]{1,0:T(8,128)(2,1)S(1)}, u32[]{:S(2)}, u32[]{:S(2)}) %collective-permute-start.1) | collective-permute-done | bytes 55328 | tf_op jit(solution)/shard_map/ppermute | solution.py:322
  81.9 5.8 %all-to-all-done.1.o_ref = bf16[8,72,384]{2,1,0:T(8,128)(2,1)S(1)} async-done(((bf16[8,72,384]{2,1,0:T(8,128)(2,1)}), bf16[8,72,384]{2,1,0:T(8,128)(2,1)S(1)}, u32[]{:S(2)}, u32[]{:S(2)}) %all-to-all-start.1) | async-done | bytes 442400 | tf_op jit(solution)/shard_map/all_to_all | solution.py:323
  87.6 0.0 copy-done
  87.6 0.0 copy-start.5
  87.7 0.0 copy-start.2
  87.7 0.0 copy-start.3
  87.7 2.1 %project.1 = bf16[2,8,64,384]{3,2,1,0:T(8,128)(2,1)} custom-call(s32[1]{0:T(128)} %bitcast.1.ids, bf16[8,72,384]{2,1,0:T(8,128)(2,1)S(1)} %all-to-all-done.1.o_ref, bf16[384,3072]{1,0:T(8,128)(2,1)S(1)} %copy-done), custom_call_target="tpu_custom_call" | custom-call | tf_op jit(solution)/shard_map/project/pallas_call | solution.py:325
  89.8 8.9 %all-to-all-start.2 = ((bf16[16,64,384]{2,1,0:T(8,128)(2,1)}), bf16[16,64,384]{2,1,0:T(8,128)(2,1)S(1)}, u32[]{:S(2)}, u32[]{:S(2)}) async-start(bf16[16,64,384]{2,1,0:T(8,128)(2,1)} %bitcast.14), calls=%async_computation.2 | async-start | bytes 1572864 | tf_op jit(solution)/shard_map/all_to_all | solution.py:333
  99.4 0.0 copy-done.5
  99.4 0.0 copy-done.7
  99.4 0.6 dynamic_slice.3
  100.1 0.7 pad_maximum_fusion.scal
  100.8 10.9 %all-to-all-done.2.part_ref = bf16[16,64,384]{2,1,0:T(8,128)(2,1)S(1)} async-done(((bf16[16,64,384]{2,1,0:T(8,128)(2,1)}), bf16[16,64,384]{2,1,0:T(8,128)(2,1)S(1)}, u32[]{:S(2)}, u32[]{:S(2)}) %all-to-all-start.2) | async-done | bytes 786464 | tf_op jit(solution)/shard_map/all_to_all | solution.py:333
  111.7 0.0 copy-done.1
  111.7 0.0 copy-done.2
  111.7 0.0 copy-done.3
  111.7 1.3 %finish.1 = (bf16[1,64,384]{2,1,0:T(8,128)(2,1)}, bf16[1,64,384]{2,1,0:T(8,128)(2,1)}) custom-call(s32[1]{0:T(128)} %bitcast.guide_id.ids, f32[2]{0:T(128)S(1)} %pad_maximum_fusion.scal, bf16[16,64,384]{2,1,0:T(8,128)(2,1)S(1)} %all-to-all-done.2.part_ref, bf16[2,64,384]{2,1,0:T(8,128)(2,1)S(1)} %bitcast.17, f32[2,384]{1,0:T(2,128)S(1)} %bitcast.19, ...), custom_call_target="tpu_custom_call" | custom-call | tf_op jit(solution)/shard_map/finish/pallas_call | solution.py:339
  (3 shorter events, 0.0 us)
Async XLA Ops:
  3.8 11.1 %collective-permute-start = (bf16[2,80,384]{2,1,0:T(8,128)(2,1)}, bf16[2,80,384]{2,1,0:T(8,128)(2,1)S(1)}, u32[]{:S(2)}, u32[]{:S(2)}) collective-permute-start(bf16[2,80,384]{2,1,0:T(8,128)(2,1)} %get-tuple-element.12), channel_id=1, source_target_pairs={{0,128},{128,0},{1,129},{129,1},{2,130},{130,2},{3,131},{131,3},{4... | collective-permute-start | bytes 368648 | tf_op jit(solution)/shard_map/ppermute | solution.py:301
  9.3 36.8 %all-to-all-start = ((bf16[8,64,384]{2,1,0:T(8,128)(2,1)}), bf16[8,64,384]{2,1,0:T(8,128)(2,1)}, u32[]{:S(2)}, u32[]{:S(2)}) async-start(bf16[8,64,384]{2,1,0:T(8,128)(2,1)} %get-tuple-element.10), calls=%async_computation | async-start | bytes 786432 | tf_op jit(solution)/shard_map/all_to_all | solution.py:299
  14.9 31.2 %copy-start.4 = (s32[2]{0:T(128)S(1)}, s32[2]{0:T(128)}, u32[]{:S(2)}) copy-start(s32[2]{0:T(128)} %len_ref.1) | copy-start | bytes 28
  15.6 60.4 %copy-start.6 = (bf16[72,384]{1,0:T(8,128)(2,1)S(1)}, bf16[72,384]{1,0:T(8,128)(2,1)}, u32[]{:S(2)}) copy-start(bf16[72,384]{1,0:T(8,128)(2,1)} %get-tuple-element.15) | copy-start | bytes 165892
  15.6 72.1 %copy-start = (bf16[384,3072]{1,0:T(8,128)(2,1)S(1)}, bf16[384,3072]{1,0:T(8,128)(2,1)}, u32[]{:S(2)}) copy-start(bf16[384,3072]{1,0:T(8,128)(2,1)} %w_ref.1) | copy-start | bytes 7077892
  50.0 37.6 %all-to-all-start.1 = ((bf16[8,72,384]{2,1,0:T(8,128)(2,1)}), bf16[8,72,384]{2,1,0:T(8,128)(2,1)S(1)}, u32[]{:S(2)}, u32[]{:S(2)}) async-start(bf16[8,72,384]{2,1,0:T(8,128)(2,1)} %attend.1), calls=%async_computation.1 | async-start | bytes 884736 | tf_op jit(solution)/shard_map/all_to_all | solution.py:323
  76.0 5.9 %collective-permute-start.1 = (bf16[72,384]{1,0:T(8,128)(2,1)S(1)}, bf16[72,384]{1,0:T(8,128)(2,1)S(1)}, u32[]{:S(2)}, u32[]{:S(2)}) collective-permute-start(bf16[72,384]{1,0:T(8,128)(2,1)S(1)} %copy-done.6), channel_id=1, source_target_pairs={{0,256},{256,0},{1,257},{257,1},{2,258},{258,2},{3,259},{259,3},{4... | collective-permute-start | bytes 165896 | tf_op jit(solution)/shard_map/ppermute | solution.py:322
  87.6 11.8 %copy-start.5 = (f32[384]{0:T(512)S(1)}, f32[384]{0:T(512)}, u32[]{:S(2)}) copy-start(f32[384]{0:T(512)} %param.27) | copy-start | bytes 4612
  87.6 11.8 %copy-start.7 = (f32[2]{0:T(128)S(1)}, f32[2]{0:T(128)}, u32[]{:S(2)}) copy-start(f32[2]{0:T(128)} %param.28) | copy-start | bytes 28
  87.7 24.1 %copy-start.1 = (bf16[1,2,64,384]{3,2,1,0:T(8,128)(2,1)S(1)}, bf16[1,2,64,384]{3,2,1,0:T(8,128)(2,1)}, u32[]{:S(2)}) copy-start(bf16[1,2,64,384]{3,2,1,0:T(8,128)(2,1)} %param.17) | copy-start | bytes 294916
  87.7 24.1 %copy-start.2 = (bf16[1,64,384]{2,1,0:T(8,128)(2,1)S(1)}, bf16[1,64,384]{2,1,0:T(8,128)(2,1)}, u32[]{:S(2)}) copy-start(bf16[1,64,384]{2,1,0:T(8,128)(2,1)} %lat_ref.1) | copy-start | bytes 147460
  87.7 24.1 %copy-start.3 = (f32[1,2,384]{2,1,0:T(2,128)S(1)}, f32[1,2,384]{2,1,0:T(2,128)}, u32[]{:S(2)}) copy-start(f32[1,2,384]{2,1,0:T(2,128)} %param.25) | copy-start | bytes 9220
  89.8 21.9 %all-to-all-start.2 = ((bf16[16,64,384]{2,1,0:T(8,128)(2,1)}), bf16[16,64,384]{2,1,0:T(8,128)(2,1)S(1)}, u32[]{:S(2)}, u32[]{:S(2)}) async-start(bf16[16,64,384]{2,1,0:T(8,128)(2,1)} %bitcast.14), calls=%async_computation.2 | async-start | bytes 1572864 | tf_op jit(solution)/shard_map/all_to_all | solution.py:333

commit v9 on v8

--- a/solution.py
+++ b/solution.py
@@ -16,9 +16,12 @@
 TQ = 64
 TT = 16
 TK = TQ + TT
-NZ = 4
-NS = 8
+NK = 8
+NQ = 2
+NS = 2 * NQ
+NB = 2 * NK
 STAT = 8
+VR = 2 * TT + TQ
 BF = jnp.bfloat16
 F32 = jnp.float32
 VMEM_LIMIT = 48 * 1024 * 1024
@@ -75,7 +78,7 @@
 
 def prepare_kernel(
     seq_id, xh_id, guide_id, k_hbm, q_hbm, v_hbm, tk_hbm, tv_hbm, hid_hbm, gate_hbm, qg_hbm, kg_hbm, row_hbm, col_hbm,
-    keep_out, send_out, q_out, side_out,
+    keep_v, keep_k, send_out, q_out, side_out,
     k_ref, q_ref, v_ref, tk_ref, tv_ref, hid_ref, gate_ref, qg_ref, kg_ref, row_ref, col_ref, sems,
 ):
     other = 1 - guide_id[0]
@@ -94,21 +97,24 @@
         for h in range(HPD):
             hs = slice(h * HD, (h + 1) * HD)
             q = rotated(normed(q_ref[p, :, hs], qg_ref[...]), table).astype(BF)
-            for z in range(NZ):
-                q_out[p * NZ + z, :, hs] = q
+            for z in range(NQ):
+                q_out[p * NQ + z, :, hs] = q
     for copy in copies[4:7]:
         copy.wait()
     own = xh_id[0]
-    for out, p in ((keep_out.at[0], own), (send_out, 1 - own)):
-        for h in range(HPD):
-            hs = slice(h * HD, (h + 1) * HD)
-            out[0, 0:TT, hs] = normed(tk_ref[p, :, hs], kg_ref[1:2]).astype(BF)
-            out[0, TT:TK, hs] = rotated(normed(k_ref[p, :, hs], kg_ref[0:1]), table).astype(BF)
+    vals = ((keep_v.at[0], own), (send_out.at[0:VR], 1 - own))
+    imgs = ((keep_k.at[0], own), (send_out.at[VR:], 1 - own))
+    for h in range(HPD):
+        hs = slice(h * HD, (h + 1) * HD)
+        for out, p in vals:
+            out[0:TT, hs] = normed(tk_ref[p, :, hs], kg_ref[1:2]).astype(BF)
+        for out, p in imgs:
+            out[:, hs] = rotated(normed(k_ref[p, :, hs], kg_ref[0:1]), table).astype(BF)
     for copy in copies[7:]:
         copy.wait()
-    for out, p in ((keep_out.at[0], own), (send_out, 1 - own)):
-        out[1, 0:TT, :] = tv_ref[p]
-        out[1, TT:TK, :] = v_ref[p]
+    for out, p in vals:
+        out[TT : 2 * TT, :] = tv_ref[p]
+        out[2 * TT :, :] = v_ref[p]
     side_out[0:TQ, :] = hid_ref[...]
     hi, mid, lo = split3(gate_ref[pl.ds(other, 1), :])
     rows = lax.broadcasted_iota(jnp.int32, (8, W), 0)
@@ -116,38 +122,37 @@
     side_out[TQ : TQ + 8, :] = packed.astype(BF)
 
 
-def join_kernel(kv_hbm, got_hbm, out_hbm, sem):
-    del kv_hbm
-    copy = pltpu.make_async_copy(got_hbm, out_hbm.at[1], sem)
-    copy.start()
-    copy.wait()
-
-
-def attend_kernel(xh_id, z0_id, len_ref, q_ref, kv_ref, out_ref):
+def join_kernel(v_in, k_in, got_hbm, v_out, k_out, sems):
+    del v_in, k_in
+    for copy in start_all(((got_hbm.at[0:VR], v_out.at[1]), (got_hbm.at[VR:], k_out.at[1])), sems):
+        copy.wait()
+
+
+def attend_kernel(xh_id, z0_id, len_ref, q_ref, v_ref, k_ref, out_ref):
     scale = HD ** (-0.5) * 1.4426950408889634
     own = xh_id[0]
-    at = lax.broadcasted_iota(jnp.int32, (1, NS * TK), 1)
-    block = jnp.zeros_like(at)
-    for i in range(1, NS):
-        block = block + (at >= i * TK).astype(jnp.int32)
-    within = at - block * TK
-    from_own = (block & 1) == 0
-    seq = (jnp.where(from_own, own, 1 - own) * NZ + (block >> 1)) * NZ + z0_id[0]
-    dead = (within < TT) & (seq * TT + within >= len_ref[own])
-    bias = jnp.where(dead, -1e30, 0.0)
+    at = lax.broadcasted_iota(jnp.int32, (1, NB * TT), 1)
+    block = at >> 4
+    seq = (jnp.where((block & 1) == 0, own, 1 - own) * NK + (block >> 1)) * NQ + z0_id[0]
+    bias = jnp.where(seq * TT + (at & 15) >= len_ref[own], -1e30, 0.0)
     lane = lax.broadcasted_iota(jnp.int32, (NS * TQ, HD), 1)
     stats = jnp.zeros((NS * TQ, HD), F32)
     for h in range(HPD):
         hs = slice(h * HD, (h + 1) * HD)
         q = q_ref[:, :, hs].reshape(NS * TQ, HD)
-        k = kv_ref[:, :, 0, :, hs].reshape(NS * TK, HD)
-        v = kv_ref[:, :, 1, :, hs].reshape(NS * TK, HD)
-        s = lax.dot_general(q, k, (((1,), (1,)), ((), ())), preferred_element_type=F32)
-        s = s * scale + bias
-        top = jnp.max(s, -1, keepdims=True)
-        e = jnp.exp2(s - top)
-        total = jnp.sum(e, -1, keepdims=True)
-        o = jnp.dot(e.astype(BF), v, preferred_element_type=F32) / total
+        kt = v_ref[:, 0:TT, hs].reshape(NB * TT, HD)
+        vt = v_ref[:, TT : 2 * TT, hs].reshape(NB * TT, HD)
+        ki = k_ref[:, :, hs].reshape(NB * TQ, HD)
+        vi = v_ref[:, 2 * TT :, hs].reshape(NB * TQ, HD)
+        dims = (((1,), (1,)), ((), ()))
+        st = lax.dot_general(q, kt, dims, preferred_element_type=F32) * scale + bias
+        si = lax.dot_general(q, ki, dims, preferred_element_type=F32) * scale
+        top = jnp.maximum(jnp.max(st, -1, keepdims=True), jnp.max(si, -1, keepdims=True))
+        et = jnp.exp2(st - top)
+        ei = jnp.exp2(si - top)
+        total = jnp.sum(et, -1, keepdims=True) + jnp.sum(ei, -1, keepdims=True)
+        o = jnp.dot(ei.astype(BF), vi, preferred_element_type=F32)
+        o = (o + jnp.dot(et.astype(BF), vt, preferred_element_type=F32)) / total
         out_ref[:, 0:TQ, hs] = o.astype(BF).reshape(NS, TQ, HD)
         lse = top + jnp.log2(total)
         hi = lse.astype(BF).astype(F32)
@@ -162,21 +167,21 @@
 def project_kernel(ids, o_ref, w_ref, out_hbm, attn_ref, out_ref, sems):
     odd = ids[0]
     stats = o_ref[:, TQ : TQ + STAT, 0:HD].astype(F32).reshape(NS * STAT, HD)
-    cols = jnp.transpose(jnp.concatenate([stats, stats], 0))
+    cols = jnp.transpose(jnp.concatenate([stats] * (HD // (NS * STAT)), 0))
     cols = jnp.where(odd == 0, cols[0:TQ], cols[TQ : 2 * TQ])
     for p in range(2):
         for h in range(HPD):
             hs = slice(h * HD, (h + 1) * HD)
             lses = []
-            for z in range(NZ):
-                at = (p * NZ + z) * STAT + h
+            for z in range(NQ):
+                at = (p * NQ + z) * STAT + h
                 lses.append(cols[:, at : at + 1] + cols[:, at + HPD : at + HPD + 1])
             top = functools.reduce(jnp.maximum, lses)
             ws = [jnp.exp2(x - top) for x in lses]
             total = functools.reduce(jnp.add, ws)
             acc = jnp.zeros((TQ, HD), F32)
-            for z in range(NZ):
-                acc = acc + ws[z] * o_ref[p * NZ + z, 0:TQ, hs].astype(F32)
+            for z in range(NQ):
+                acc = acc + ws[z] * o_ref[p * NQ + z, 0:TQ, hs].astype(F32)
             attn_ref[p * TQ : (p + 1) * TQ, hs] = (acc / total).astype(BF)
     attn = attn_ref[...]
     copies = []
@@ -252,18 +257,19 @@
     xh = lax.axis_index("xh")
     z1 = lax.axis_index("z1")
     z0 = lax.axis_index("z0")
-    seq = (xh * NZ + z1) * NZ + z0
+    seq = (xh * NK + z1) * NQ + z0
     rows, cols = rope_tables()
-    keep, send, q, side = call(
+    keep_v, keep_k, send, q, side = call(
         prepare_kernel,
         (
-            jax.ShapeDtypeStruct((2, 2, TK, W), BF),
-            jax.ShapeDtypeStruct((2, TK, W), BF),
+            jax.ShapeDtypeStruct((2, VR, W), BF),
+            jax.ShapeDtypeStruct((2, TQ, W), BF),
+            jax.ShapeDtypeStruct((VR + TQ, W), BF),
             jax.ShapeDtypeStruct((NS, TQ, W), BF),
             jax.ShapeDtypeStruct((TQ + 8, W), BF),
         ),
         [SMEM()] * 3 + [HBM()] * 11,
-        (VMEM(),) * 4,
+        (VMEM(),) * 5,
         "prepare",
         [
             pltpu.VMEM((2, TQ, W), BF),
@@ -299,25 +305,26 @@
     q = lax.all_to_all(q, ("xh", "z0"), 0, 0, tiled=True)
     swap = [(0, 1), (1, 0)]
     got = lax.ppermute(send, "xh", swap)
-    kv = call(
+    v, k = call(
         join_kernel,
-        pltpu.HBM((2, 2, TK, W), BF),
-        [HBM()] * 2,
-        HBM(),
+        (pltpu.HBM((2, VR, W), BF), pltpu.HBM((2, TQ, W), BF)),
+        [HBM()] * 3,
+        (HBM(),) * 2,
         "join",
-        [pltpu.SemaphoreType.DMA],
+        [pltpu.SemaphoreType.DMA((2,))],
         cost=pl.CostEstimate(flops=10**11, bytes_accessed=10**6, transcendentals=0),
-        aliases={0: 0},
-    )(keep, got)
-    kv = lax.all_gather(kv, "z1", axis=0)
+        aliases={0: 0, 1: 1},
+    )(keep_v, keep_k, got)
+    v = lax.all_gather(v, "z1", axis=0, tiled=True)
+    k = lax.all_gather(k, "z1", axis=0, tiled=True)
 
     out = call(
         attend_kernel,
         pltpu.HBM((NS, TQ + STAT, W), BF),
-        [SMEM()] * 3 + [VMEM()] * 2,
+        [SMEM()] * 3 + [VMEM()] * 3,
         VMEM(),
         "attend",
-    )(xh[None], z0[None], text_len, q, kv)
+    )(xh[None], z0[None], text_len, q, v, k)
     out, side = lax.optimization_barrier((out, side))
     side = lax.ppermute(side, "g", swap)
     out = lax.all_to_all(out, ("xh", "z0"), 0, 0, tiled=True)
@@ -349,7 +356,7 @@
 
 
 def solution(mesh):
-    fine = Mesh(mesh.devices.reshape(2, 2, NZ, NZ, 4, 2), ("g", "xh", "z1", "z0", "y", "c"))
+    fine = Mesh(mesh.devices.reshape(2, 2, NK, NQ, 4, 2), ("g", "xh", "z1", "z0", "y", "c"))
     seq = ("xh", "z1", "z0")
     blk = ("y", "c")
     act = P("g", None, seq, blk)

time: 114 us -> 131 us (1.15)
  starting transfers between devices: 47.9 us -> 29.3 us
  waiting for transfers between devices: 20.6 us -> 35 us
  between operations: 1.53 us -> 14.9 us
  blocking collectives: 30.5 us -> 38.2 us
    all_to_all x1, starting transfers between devices: 25.9 us -> 7.07 us  [shards(): out = lax.all_to_all(out, ('xh', 'z0'), 0, 0, tiled=True)]
    all_gather x0 -> x1, waiting for transfers between devices: none -> 18.4 us  [shards(): v = lax.all_gather(v, 'z1', axis=0, tiled=True)]
    all_gather x1, blocking collectives: 30.5 us -> 38.2 us  [shards(): k = lax.all_gather(k, 'z1', axis=0, tiled=True)]
    all_to_all x1, waiting for transfers between devices: 5.76 us -> 0.73 us  [shards(): out = lax.all_to_all(out, ('xh', 'z0'), 0, 0, tiled=True)]
    ppermute x1, waiting for transfers between devices: 0.01 us -> 2.46 us  [shards(): got = lax.ppermute(send, 'xh', swap)]
    ppermute x1, waiting for transfers between devices: 3.97 us -> 2.52 us  [shards(): side = lax.ppermute(side, 'g', swap)]
  transfers between devices with their start and end apart: 5 -> 6, of which waited for: 3 -> 5; matrix products, arithmetic and copies ran while one was open for 1% -> 1% of each run, Pallas kernels for 1% -> 0%
where the time goes in v9:
time: 131 us; the launch traced here: 130 us
  blocking collectives  38.2 us (29%)
  waiting for transfers between devices  35 us (27%)
  starting transfers between devices  29.3 us (22%)
  between operations  14.9 us (11%)
  Pallas kernels  10.2 us (8%)
  local copies, waits for them, and re-layouts  1.9 us (1%)
    all_gather x1, blocking collectives, shards(): k = lax.all_gather(k, 'z1', axis=0, tiled=True)  38.2 us
    all_gather x1, waiting for transfers between devices, shards(): v = lax.all_gather(v, 'z1', axis=0, tiled=True)  18.4 us
    all_to_all x1, waiting for transfers between devices, shards(): lax.all_to_all(part.reshape(16, TQ, W), ('g', 'y', 'c'), 0, 0, tiled=True)  10.9 us
    all_to_all x1, starting transfers between devices, shards(): lax.all_to_all(part.reshape(16, TQ, W), ('g', 'y', 'c'), 0, 0, tiled=True)  8.2 us
    all_to_all x1, starting transfers between devices, shards(): out = lax.all_to_all(out, ('xh', 'z0'), 0, 0, tiled=True)  7.07 us
    all_to_all x1, starting transfers between devices, shards(): q = lax.all_to_all(q, ('xh', 'z0'), 0, 0, tiled=True)  6.18 us
    ppermute x1, starting transfers between devices, shards(): got = lax.ppermute(send, 'xh', swap)  5.48 us
    pallas_call x1, Pallas kernels, shards(): call(attend_kernel, pltpu.HBM((NS, TQ + STAT, W), BF), [SMEM()] * 3 + [VM...  3.21 us
  transfers between devices with their start and end apart: 6, of which 5 were waited for; matrix products, arithmetic and copies ran while one was open for 1% of the time, Pallas kernels for 0%

profile of v9, /device:TPU:1, one launch (start us, length us, event | category | flops | bytes accessed | tf_op | source)
XLA Modules:
  0.0 130.3 jit_solution(15234247017056813651)
XLA Ops:
  7.2 0.0 all-gather.2.cloned.1.call-start
  7.2 3.1 %prepare.1 = (bf16[2,96,384]{2,1,0:T(8,128)(2,1)}, bf16[2,64,384]{2,1,0:T(8,128)(2,1)}, bf16[160,384]{1,0:T(8,128)(2,1)}, bf16[4,64,384]{2,1,0:T(8,128)(2,1)}, bf16[72,384]{1,0:T(8,128)(2,1)}) custom-call(s32[1]{0:T(128)} %bitcast.4.seq_id, s32[1]{0:T(128)} %bitcast.2.xh_id, s32[1]{0:T(128)} %bitcast.guide_id.ids, bf16[2,64,384]{2,1,0:T(8,128)(2,1)} %bitcast.18, ...), custom_call_target="tpu_custom_call" | custom-call | tf_op jit(solution)/shard_map/prepare/pallas_call | solution.py:262
  10.3 5.5 %collective-permute-start = (bf16[160,384]{1,0:T(8,128)(2,1)}, bf16[160,384]{1,0:T(8,128)(2,1)S(1)}, u32[]{:S(2)}, u32[]{:S(2)}) collective-permute-start(bf16[160,384]{1,0:T(8,128)(2,1)} %get-tuple-element.16), channel_id=1, source_target_pairs={{0,128},{128,0},{1,129},{129,1},{2,130},{130,2},{3,131},{131,3},{4... | collective-permute-start | bytes 368648 | tf_op jit(solution)/shard_map/ppermute | solution.py:307
  15.8 2.5 %collective-permute-done.got_hbm = bf16[160,384]{1,0:T(8,128)(2,1)S(1)} collective-permute-done((bf16[160,384]{1,0:T(8,128)(2,1)}, bf16[160,384]{1,0:T(8,128)(2,1)S(1)}, u32[]{:S(2)}, u32[]{:S(2)}) %collective-permute-start) | collective-permute-done | bytes 122912 | tf_op jit(solution)/shard_map/ppermute | solution.py:307
  18.3 0.7 join.1
  18.9 0.0 copy-start
  18.9 0.0 all-gather.2.cloned.1.call-update
  19.0 6.2 %all-to-all-start = ((bf16[4,64,384]{2,1,0:T(8,128)(2,1)}), bf16[4,64,384]{2,1,0:T(8,128)(2,1)S(1)}, u32[]{:S(2)}, u32[]{:S(2)}) async-start(bf16[4,64,384]{2,1,0:T(8,128)(2,1)} %get-tuple-element.13), calls=%async_computation | async-start | bytes 393216 | tf_op jit(solution)/shard_map/all_to_all | solution.py:305
  25.1 38.2 %all_gather.7.k_ref = bf16[16,64,384]{2,1,0:T(8,128)(2,1)S(1)} all-gather(bf16[2,64,384]{2,1,0:T(8,128)(2,1)} %get-tuple-element.18), channel_id=1, replica_groups=mesh['g'=2,'xh'=2,'z1'=8,'z0'=2,'y'=4,'c'=2] {'z1'}, dimensions={0}, use_global_device_ids=true | all-gather | bytes 884736 | tf_op jit(solution)/shard_map/all_gather | solution.py:319
  63.4 0.0 all-to-all-done.q_ref
  63.4 18.4 %all-gather.2.cloned.1.call-done.v_ref = bf16[16,96,384]{2,1,0:T(8,128)(2,1)} async-done(((bf16[2,96,384]{2,1,0:T(8,128)(2,1)}), bf16[16,96,384]{2,1,0:T(8,128)(2,1)}) %all-gather.2.cloned.1.call-update) | async-done | bytes 1179664 | tf_op jit(solution)/shard_map/all_gather | solution.py:318
  81.7 0.0 copy-done.5
  81.7 1.3 copy-done.1
  83.0 3.2 %attend.1 = bf16[4,72,384]{2,1,0:T(8,128)(2,1)} custom-call(s32[1]{0:T(128)} %bitcast.2.xh_id, s32[1]{0:T(128)} %bitcast.3.z0_id, s32[2]{0:T(128)S(1)} %copy-done.5, bf16[4,64,384]{2,1,0:T(8,128)(2,1)S(1)} %all-to-all-done.q_ref, bf16[16,96,384]{2,1,0:T(8,128)(2,1)S(1)} %copy-done.1, bf16[16,64,384]{2,1,0:T(8,128)(2,1)S(1)} %all_gather.7.k_ref), custom_call_target="tpu_custom_call" | custom-call | tf_op jit(solution)/shard_map/attend/pallas_call | solution.py:321
  86.2 7.1 %all-to-all-start.1 = ((bf16[4,72,384]{2,1,0:T(8,128)(2,1)}), bf16[4,72,384]{2,1,0:T(8,128)(2,1)S(1)}, u32[]{:S(2)}, u32[]{:S(2)}) async-start(bf16[4,72,384]{2,1,0:T(8,128)(2,1)} %attend.1), calls=%async_computation.1 | async-start | bytes 442368 | tf_op jit(solution)/shard_map/all_to_all | solution.py:330
  93.3 0.0 copy-done.7
  93.3 2.4 %collective-permute-start.1 = (bf16[72,384]{1,0:T(8,128)(2,1)S(1)}, bf16[72,384]{1,0:T(8,128)(2,1)S(1)}, u32[]{:S(2)}, u32[]{:S(2)}) collective-permute-start(bf16[72,384]{1,0:T(8,128)(2,1)S(1)} %copy-done.7), channel_id=1, source_target_pairs={{0,256},{256,0},{1,257},{257,1},{2,258},{258,2},{3,259},{259,3},{4... | collective-permute-start | bytes 165896 | tf_op jit(solution)/shard_map/ppermute | solution.py:329
  95.6 2.5 %collective-permute-done.1.side_ref = bf16[72,384]{1,0:T(8,128)(2,1)S(1)} collective-permute-done((bf16[72,384]{1,0:T(8,128)(2,1)S(1)}, bf16[72,384]{1,0:T(8,128)(2,1)S(1)}, u32[]{:S(2)}, u32[]{:S(2)}) %collective-permute-start.1) | collective-permute-done | bytes 55328 | tf_op jit(solution)/shard_map/ppermute | solution.py:329
  98.2 0.7 all-to-all-done.1.o_ref
  98.9 0.0 copy-done
  98.9 0.0 copy-start.3
  98.9 0.0 copy-start.4
  98.9 1.9 %project.1 = bf16[2,8,64,384]{3,2,1,0:T(8,128)(2,1)} custom-call(s32[1]{0:T(128)} %bitcast.1.ids, bf16[4,72,384]{2,1,0:T(8,128)(2,1)S(1)} %all-to-all-done.1.o_ref, bf16[384,3072]{1,0:T(8,128)(2,1)S(1)} %copy-done), custom_call_target="tpu_custom_call" | custom-call | tf_op jit(solution)/shard_map/project/pallas_call | solution.py:332
  100.9 8.2 %all-to-all-start.2 = ((bf16[16,64,384]{2,1,0:T(8,128)(2,1)}), bf16[16,64,384]{2,1,0:T(8,128)(2,1)S(1)}, u32[]{:S(2)}, u32[]{:S(2)}) async-start(bf16[16,64,384]{2,1,0:T(8,128)(2,1)} %bitcast.13), calls=%async_computation.2 | async-start | bytes 1572864 | tf_op jit(solution)/shard_map/all_to_all | solution.py:340
  109.8 0.0 copy-done.6
  109.8 0.0 copy-done.8
  109.8 0.6 dynamic_slice.3
  110.5 0.7 pad_maximum_fusion.scal
  111.2 10.9 %all-to-all-done.2.part_ref = bf16[16,64,384]{2,1,0:T(8,128)(2,1)S(1)} async-done(((bf16[16,64,384]{2,1,0:T(8,128)(2,1)}), bf16[16,64,384]{2,1,0:T(8,128)(2,1)S(1)}, u32[]{:S(2)}, u32[]{:S(2)}) %all-to-all-start.2) | async-done | bytes 786464 | tf_op jit(solution)/shard_map/all_to_all | solution.py:340
  122.1 0.0 copy-done.2
  122.1 0.0 copy-done.3
  122.1 1.3 %finish.1 = (bf16[1,64,384]{2,1,0:T(8,128)(2,1)}, bf16[1,64,384]{2,1,0:T(8,128)(2,1)}) custom-call(s32[1]{0:T(128)} %bitcast.guide_id.ids, f32[2]{0:T(128)S(1)} %pad_maximum_fusion.scal, bf16[16,64,384]{2,1,0:T(8,128)(2,1)S(1)} %all-to-all-done.2.part_ref, bf16[2,64,384]{2,1,0:T(8,128)(2,1)S(1)} %bitcast.15, f32[2,384]{1,0:T(2,128)S(1)} %bitcast.17, ...), custom_call_target="tpu_custom_call" | custom-call | tf_op jit(solution)/shard_map/finish/pallas_call | solution.py:346
  (8 shorter events, 0.0 us)
Async XLA Ops:
  7.2 74.6 %all-gather.2.cloned.1.call-start = ((), (), s32[]{:S(2)}) async-start(), calls=%async_computation.3 | async-start | bytes 1327104 | tf_op jit(solution)/shard_map/all_gather | solution.py:318
  10.3 8.0 %collective-permute-start = (bf16[160,384]{1,0:T(8,128)(2,1)}, bf16[160,384]{1,0:T(8,128)(2,1)S(1)}, u32[]{:S(2)}, u32[]{:S(2)}) collective-permute-start(bf16[160,384]{1,0:T(8,128)(2,1)} %get-tuple-element.16), channel_id=1, source_target_pairs={{0,128},{128,0},{1,129},{129,1},{2,130},{130,2},{3,131},{131,3},{4... | collective-permute-start | bytes 368648 | tf_op jit(solution)/shard_map/ppermute | solution.py:307
  18.2 63.5 %copy-start.5 = (s32[2]{0:T(128)S(1)}, s32[2]{0:T(128)}, u32[]{:S(2)}) copy-start(s32[2]{0:T(128)} %len_ref.1) | copy-start | bytes 28
  18.2 75.0 %copy-start.7 = (bf16[72,384]{1,0:T(8,128)(2,1)S(1)}, bf16[72,384]{1,0:T(8,128)(2,1)}, u32[]{:S(2)}) copy-start(bf16[72,384]{1,0:T(8,128)(2,1)} %get-tuple-element.21) | copy-start | bytes 165892
  18.9 80.0 %copy-start = (bf16[384,3072]{1,0:T(8,128)(2,1)S(1)}, bf16[384,3072]{1,0:T(8,128)(2,1)}, u32[]{:S(2)}) copy-start(bf16[384,3072]{1,0:T(8,128)(2,1)} %w_ref.1) | copy-start | bytes 7077892
  19.0 44.4 %all-to-all-start = ((bf16[4,64,384]{2,1,0:T(8,128)(2,1)}), bf16[4,64,384]{2,1,0:T(8,128)(2,1)S(1)}, u32[]{:S(2)}, u32[]{:S(2)}) async-start(bf16[4,64,384]{2,1,0:T(8,128)(2,1)} %get-tuple-element.13), calls=%async_computation | async-start | bytes 393216 | tf_op jit(solution)/shard_map/all_to_all | solution.py:305
  81.7 1.3 copy-start.1
  86.2 12.7 %all-to-all-start.1 = ((bf16[4,72,384]{2,1,0:T(8,128)(2,1)}), bf16[4,72,384]{2,1,0:T(8,128)(2,1)S(1)}, u32[]{:S(2)}, u32[]{:S(2)}) async-start(bf16[4,72,384]{2,1,0:T(8,128)(2,1)} %attend.1), calls=%async_computation.1 | async-start | bytes 442368 | tf_op jit(solution)/shard_map/all_to_all | solution.py:330
  93.3 4.9 %collective-permute-start.1 = (bf16[72,384]{1,0:T(8,128)(2,1)S(1)}, bf16[72,384]{1,0:T(8,128)(2,1)S(1)}, u32[]{:S(2)}, u32[]{:S(2)}) collective-permute-start(bf16[72,384]{1,0:T(8,128)(2,1)S(1)} %copy-done.7), channel_id=1, source_target_pairs={{0,256},{256,0},{1,257},{257,1},{2,258},{258,2},{3,259},{259,3},{4... | collective-permute-start | bytes 165896 | tf_op jit(solution)/shard_map/ppermute | solution.py:329
  98.9 10.9 %copy-start.6 = (f32[384]{0:T(512)S(1)}, f32[384]{0:T(512)}, u32[]{:S(2)}) copy-start(f32[384]{0:T(512)} %param.27) | copy-start | bytes 4612
  98.9 10.9 %copy-start.8 = (f32[2]{0:T(128)S(1)}, f32[2]{0:T(128)}, u32[]{:S(2)}) copy-start(f32[2]{0:T(128)} %param.28) | copy-start | bytes 28
  98.9 23.2 %copy-start.2 = (bf16[1,2,64,384]{3,2,1,0:T(8,128)(2,1)S(1)}, bf16[1,2,64,384]{3,2,1,0:T(8,128)(2,1)}, u32[]{:S(2)}) copy-start(bf16[1,2,64,384]{3,2,1,0:T(8,128)(2,1)} %param.17) | copy-start | bytes 294916
  98.9 23.2 %copy-start.3 = (bf16[1,64,384]{2,1,0:T(8,128)(2,1)S(1)}, bf16[1,64,384]{2,1,0:T(8,128)(2,1)}, u32[]{:S(2)}) copy-start(bf16[1,64,384]{2,1,0:T(8,128)(2,1)} %lat_ref.1) | copy-start | bytes 147460
  98.9 23.2 %copy-start.4 = (f32[1,2,384]{2,1,0:T(2,128)S(1)}, f32[1,2,384]{2,1,0:T(2,128)}, u32[]{:S(2)}) copy-start(f32[1,2,384]{2,1,0:T(2,128)} %param.25) | copy-start | bytes 9220
  100.9 21.2 %all-to-all-start.2 = ((bf16[16,64,384]{2,1,0:T(8,128)(2,1)}), bf16[16,64,384]{2,1,0:T(8,128)(2,1)S(1)}, u32[]{:S(2)}, u32[]{:S(2)}) async-start(bf16[16,64,384]{2,1,0:T(8,128)(2,1)} %bitcast.13), calls=%async_computation.2 | async-start | bytes 1572864 | tf_op jit(solution)/shard_map/all_to_all | solution.py:340
Sparse Core Ops, SparseCore 0:
  19.1 62.5 all-gather.1

commit v10 on v8

--- a/solution.py
+++ b/solution.py
@@ -318,10 +318,7 @@
         VMEM(),
         "attend",
     )(xh[None], z0[None], text_len, q, kv)
-    out, side = lax.optimization_barrier((out, side))
-    side = lax.ppermute(side, "g", swap)
     out = lax.all_to_all(out, ("xh", "z0"), 0, 0, tiled=True)
-    out, side = lax.optimization_barrier((out, side))
     part = call(
         project_kernel,
         jax.ShapeDtypeStruct((2, 8, TQ, W), BF),
@@ -330,6 +327,7 @@
         "project",
         [pltpu.VMEM((2 * TQ, W), BF), pltpu.VMEM((2, 8, TQ, W), BF), pltpu.SemaphoreType.DMA((8,))],
     )((z0 & 1)[None], out, proj_weight)
+    side = lax.ppermute(side, "g", swap)
     part = lax.all_to_all(part.reshape(16, TQ, W), ("g", "y", "c"), 0, 0, tiled=True)
     index = step_index[0]
     u_now = 1.0 - index.astype(F32) / STEPS

time: 114 us -> 114 us (level)
  starting transfers between devices: 47.9 us -> 49.2 us
  waiting for transfers between devices: 20.6 us -> 19.3 us
    all_to_all x1, waiting for transfers between devices: 10.9 us -> 0.97 us  [shards(): lax.all_to_all(part.reshape(16, TQ, W), ('g', 'y', 'c'), 0, 0, tiled=True)]
    all_to_all x1, waiting for transfers between devices: 5.76 us -> 11.6 us  [shards(): out = lax.all_to_all(out, ('xh', 'z0'), 0, 0, tiled=True)]
    ppermute x1, waiting for transfers between devices: 3.97 us -> 6.63 us  [shards(): side = lax.ppermute(side, 'g', swap)]
    ppermute x1, starting transfers between devices: 1.92 us -> 3.3 us  [shards(): side = lax.ppermute(side, 'g', swap)]
where the time goes in v10:
time: 114 us; the launch traced here: 113 us
  starting transfers between devices  49.2 us (43%)
  blocking collectives  30.5 us (27%)
  waiting for transfers between devices  19.3 us (17%)
  Pallas kernels  11.2 us (10%)
  between operations  1.51 us (1%)
    all_gather x1, blocking collectives, shards(): kv = lax.all_gather(kv, 'z1', axis=0)  30.5 us
    all_to_all x1, starting transfers between devices, shards(): out = lax.all_to_all(out, ('xh', 'z0'), 0, 0, tiled=True)  25.9 us
    all_to_all x1, waiting for transfers between devices, shards(): out = lax.all_to_all(out, ('xh', 'z0'), 0, 0, tiled=True)  11.6 us
    all_to_all x1, starting transfers between devices, shards(): lax.all_to_all(part.reshape(16, TQ, W), ('g', 'y', 'c'), 0, 0, tiled=True)  8.93 us
    ppermute x1, waiting for transfers between devices, shards(): side = lax.ppermute(side, 'g', swap)  6.63 us
    all_to_all x1, starting transfers between devices, shards(): q = lax.all_to_all(q, ('xh', 'z0'), 0, 0, tiled=True)  5.63 us
    ppermute x1, starting transfers between devices, shards(): got = lax.ppermute(send, 'xh', swap)  5.48 us
    pallas_call x1, Pallas kernels, shards(): call(attend_kernel, pltpu.HBM((NS, TQ + STAT, W), BF), [SMEM()] * 3 + [VM...  3.95 us
  transfers between devices with their start and end apart: 5, of which 3 were waited for; matrix products, arithmetic and copies ran while one was open for 1% of the time, Pallas kernels for 1%

profile of v10, /device:TPU:1, one launch (start us, length us, event | category | flops | bytes accessed | tf_op | source)
XLA Modules:
  0.0 113.0 jit_solution(5836598378719879583)
XLA Ops:
  0.6 3.1 %prepare.1 = (bf16[2,2,80,384]{3,2,1,0:T(8,128)(2,1)}, bf16[2,80,384]{2,1,0:T(8,128)(2,1)}, bf16[8,64,384]{2,1,0:T(8,128)(2,1)}, bf16[72,384]{1,0:T(8,128)(2,1)}) custom-call(s32[1]{0:T(128)} %bitcast.4.seq_id, s32[1]{0:T(128)} %bitcast.2.xh_id, s32[1]{0:T(128)} %bitcast.guide_id.ids, bf16[2,64,384]{2,1,0:T(8,128)(2,1)} %bitcast.20, ...), custom_call_target="tpu_custom_call" | custom-call | tf_op jit(solution)/shard_map/prepare/pallas_call | solution.py:257
  3.8 5.5 %collective-permute-start = (bf16[2,80,384]{2,1,0:T(8,128)(2,1)}, bf16[2,80,384]{2,1,0:T(8,128)(2,1)S(1)}, u32[]{:S(2)}, u32[]{:S(2)}) collective-permute-start(bf16[2,80,384]{2,1,0:T(8,128)(2,1)} %get-tuple-element.8), channel_id=1, source_target_pairs={{0,128},{128,0},{1,129},{129,1},{2,130},{130,2},{3,131},{131,3},{4... | collective-permute-start | bytes 368648 | tf_op jit(solution)/shard_map/ppermute | solution.py:301
  9.3 5.6 %all-to-all-start = ((bf16[8,64,384]{2,1,0:T(8,128)(2,1)}), bf16[8,64,384]{2,1,0:T(8,128)(2,1)}, u32[]{:S(2)}, u32[]{:S(2)}) async-start(bf16[8,64,384]{2,1,0:T(8,128)(2,1)} %get-tuple-element.6), calls=%async_computation | async-start | bytes 786432 | tf_op jit(solution)/shard_map/all_to_all | solution.py:299
  14.9 0.0 collective-permute-done.got_hbm
  14.9 0.0 copy-start.4
  14.9 0.7 join.1
  15.6 0.0 copy-start
  15.6 30.5 %all-gather = bf16[8,2,80,384]{3,2,1,0:T(8,128)(2,1)S(1)} all-gather(bf16[2,2,80,384]{3,2,1,0:T(8,128)(2,1)} %join.1), channel_id=2, replica_groups=mesh['g'=2,'xh'=2,'z1'=4,'z0'=4,'y'=4,'c'=2] {'z1'}, dimensions={0}, use_global_device_ids=true | all-gather | bytes 1228800 | tf_op jit(solution)/shard_map/all_gather | solution.py:312
  46.1 0.0 all-to-all-done.q_ref
  46.1 0.0 copy-done.4
  46.1 4.0 %attend.1 = bf16[8,72,384]{2,1,0:T(8,128)(2,1)} custom-call(s32[1]{0:T(128)} %bitcast.2.xh_id, s32[1]{0:T(128)} %bitcast.3.z0_id, s32[2]{0:T(128)S(1)} %copy-done.4, bf16[8,64,384]{2,1,0:T(8,128)(2,1)} %all-to-all-done.q_ref, bf16[4,2,2,80,384]{4,3,2,1,0:T(8,128)(2,1)S(1)} %bitcast.15), custom_call_target="tpu_custom_call" | custom-call | tf_op jit(solution)/shard_map/attend/pallas_call | solution.py:314
  50.0 25.9 %all-to-all-start.1 = ((bf16[8,72,384]{2,1,0:T(8,128)(2,1)}), bf16[8,72,384]{2,1,0:T(8,128)(2,1)S(1)}, u32[]{:S(2)}, u32[]{:S(2)}) async-start(bf16[8,72,384]{2,1,0:T(8,128)(2,1)} %attend.1), calls=%async_computation.1 | async-start | bytes 884736 | tf_op jit(solution)/shard_map/all_to_all | solution.py:321
  75.9 11.6 %all-to-all-done.1.o_ref = bf16[8,72,384]{2,1,0:T(8,128)(2,1)S(1)} async-done(((bf16[8,72,384]{2,1,0:T(8,128)(2,1)}), bf16[8,72,384]{2,1,0:T(8,128)(2,1)S(1)}, u32[]{:S(2)}, u32[]{:S(2)}) %all-to-all-start.1) | async-done | bytes 442400 | tf_op jit(solution)/shard_map/all_to_all | solution.py:321
  87.6 0.0 copy-done
  87.6 0.0 copy-start.6
  87.6 0.0 copy-start.1
  87.6 0.0 copy-start.2
  87.6 0.0 copy-start.3
  87.6 2.1 %project.1 = bf16[2,8,64,384]{3,2,1,0:T(8,128)(2,1)} custom-call(s32[1]{0:T(128)} %bitcast.1.ids, bf16[8,72,384]{2,1,0:T(8,128)(2,1)S(1)} %all-to-all-done.1.o_ref, bf16[384,3072]{1,0:T(8,128)(2,1)S(1)} %copy-done), custom_call_target="tpu_custom_call" | custom-call | tf_op jit(solution)/shard_map/project/pallas_call | solution.py:322
  89.8 8.9 %all-to-all-start.2 = ((bf16[16,64,384]{2,1,0:T(8,128)(2,1)}), bf16[16,64,384]{2,1,0:T(8,128)(2,1)S(1)}, u32[]{:S(2)}, u32[]{:S(2)}) async-start(bf16[16,64,384]{2,1,0:T(8,128)(2,1)} %bitcast.14), calls=%async_computation.2 | async-start | bytes 1572864 | tf_op jit(solution)/shard_map/all_to_all | solution.py:331
  98.7 0.0 copy-done.6
  98.7 3.3 %collective-permute-start.1 = (bf16[72,384]{1,0:T(8,128)(2,1)S(1)}, bf16[72,384]{1,0:T(8,128)(2,1)S(1)}, u32[]{:S(2)}, u32[]{:S(2)}) collective-permute-start(bf16[72,384]{1,0:T(8,128)(2,1)S(1)} %copy-done.6), channel_id=1, source_target_pairs={{0,256},{256,0},{1,257},{257,1},{2,258},{258,2},{3,259},{259,3},{4... | collective-permute-start | bytes 165896 | tf_op jit(solution)/shard_map/ppermute | solution.py:330
  102.7 0.0 copy-done.7
  102.7 0.6 dynamic_slice.3
  103.4 0.7 pad_maximum_fusion.scal
  104.1 0.0 copy-done.5
  104.1 6.6 %collective-permute-done.1.side_ref = bf16[72,384]{1,0:T(8,128)(2,1)S(1)} collective-permute-done((bf16[72,384]{1,0:T(8,128)(2,1)S(1)}, bf16[72,384]{1,0:T(8,128)(2,1)S(1)}, u32[]{:S(2)}, u32[]{:S(2)}) %collective-permute-start.1) | collective-permute-done | bytes 55328 | tf_op jit(solution)/shard_map/ppermute | solution.py:330
  110.7 1.0 all-to-all-done.2.part_ref
  111.7 0.0 copy-done.1
  111.7 0.0 copy-done.2
  111.7 0.0 copy-done.3
  111.7 1.3 %finish.1 = (bf16[1,64,384]{2,1,0:T(8,128)(2,1)}, bf16[1,64,384]{2,1,0:T(8,128)(2,1)}) custom-call(s32[1]{0:T(128)} %bitcast.guide_id.ids, f32[2]{0:T(128)S(1)} %pad_maximum_fusion.scal, bf16[16,64,384]{2,1,0:T(8,128)(2,1)S(1)} %all-to-all-done.2.part_ref, bf16[2,64,384]{2,1,0:T(8,128)(2,1)S(1)} %bitcast.17, f32[2,384]{1,0:T(2,128)S(1)} %bitcast.19, ...), custom_call_target="tpu_custom_call" | custom-call | tf_op jit(solution)/shard_map/finish/pallas_call | solution.py:337
  (3 shorter events, 0.0 us)
Async XLA Ops:
  3.8 11.1 %collective-permute-start = (bf16[2,80,384]{2,1,0:T(8,128)(2,1)}, bf16[2,80,384]{2,1,0:T(8,128)(2,1)S(1)}, u32[]{:S(2)}, u32[]{:S(2)}) collective-permute-start(bf16[2,80,384]{2,1,0:T(8,128)(2,1)} %get-tuple-element.8), channel_id=1, source_target_pairs={{0,128},{128,0},{1,129},{129,1},{2,130},{130,2},{3,131},{131,3},{4... | collective-permute-start | bytes 368648 | tf_op jit(solution)/shard_map/ppermute | solution.py:301
  9.3 36.8 %all-to-all-start = ((bf16[8,64,384]{2,1,0:T(8,128)(2,1)}), bf16[8,64,384]{2,1,0:T(8,128)(2,1)}, u32[]{:S(2)}, u32[]{:S(2)}) async-start(bf16[8,64,384]{2,1,0:T(8,128)(2,1)} %get-tuple-element.6), calls=%async_computation | async-start | bytes 786432 | tf_op jit(solution)/shard_map/all_to_all | solution.py:299
  14.9 31.2 %copy-start.4 = (s32[2]{0:T(128)S(1)}, s32[2]{0:T(128)}, u32[]{:S(2)}) copy-start(s32[2]{0:T(128)} %len_ref.1) | copy-start | bytes 28
  15.6 72.0 %copy-start = (bf16[384,3072]{1,0:T(8,128)(2,1)S(1)}, bf16[384,3072]{1,0:T(8,128)(2,1)}, u32[]{:S(2)}) copy-start(bf16[384,3072]{1,0:T(8,128)(2,1)} %w_ref.1) | copy-start | bytes 7077892
  50.0 37.5 %all-to-all-start.1 = ((bf16[8,72,384]{2,1,0:T(8,128)(2,1)}), bf16[8,72,384]{2,1,0:T(8,128)(2,1)S(1)}, u32[]{:S(2)}, u32[]{:S(2)}) async-start(bf16[8,72,384]{2,1,0:T(8,128)(2,1)} %attend.1), calls=%async_computation.1 | async-start | bytes 884736 | tf_op jit(solution)/shard_map/all_to_all | solution.py:321
  87.6 11.1 %copy-start.6 = (bf16[72,384]{1,0:T(8,128)(2,1)S(1)}, bf16[72,384]{1,0:T(8,128)(2,1)}, u32[]{:S(2)}) copy-start(bf16[72,384]{1,0:T(8,128)(2,1)} %get-tuple-element.9) | copy-start | bytes 165892
  87.6 15.1 %copy-start.7 = (f32[2]{0:T(128)S(1)}, f32[2]{0:T(128)}, u32[]{:S(2)}) copy-start(f32[2]{0:T(128)} %param.28) | copy-start | bytes 28
  87.6 16.5 %copy-start.5 = (f32[384]{0:T(512)S(1)}, f32[384]{0:T(512)}, u32[]{:S(2)}) copy-start(f32[384]{0:T(512)} %param.27) | copy-start | bytes 4612
  87.6 24.1 %copy-start.1 = (bf16[1,2,64,384]{3,2,1,0:T(8,128)(2,1)S(1)}, bf16[1,2,64,384]{3,2,1,0:T(8,128)(2,1)}, u32[]{:S(2)}) copy-start(bf16[1,2,64,384]{3,2,1,0:T(8,128)(2,1)} %param.17) | copy-start | bytes 294916
  87.6 24.1 %copy-start.2 = (bf16[1,64,384]{2,1,0:T(8,128)(2,1)S(1)}, bf16[1,64,384]{2,1,0:T(8,128)(2,1)}, u32[]{:S(2)}) copy-start(bf16[1,64,384]{2,1,0:T(8,128)(2,1)} %lat_ref.1) | copy-start | bytes 147460
  87.6 24.1 %copy-start.3 = (f32[1,2,384]{2,1,0:T(2,128)S(1)}, f32[1,2,384]{2,1,0:T(2,128)}, u32[]{:S(2)}) copy-start(f32[1,2,384]{2,1,0:T(2,128)} %param.25) | copy-start | bytes 9220
  89.8 21.9 %all-to-all-start.2 = ((bf16[16,64,384]{2,1,0:T(8,128)(2,1)}), bf16[16,64,384]{2,1,0:T(8,128)(2,1)S(1)}, u32[]{:S(2)}, u32[]{:S(2)}) async-start(bf16[16,64,384]{2,1,0:T(8,128)(2,1)} %bitcast.14), calls=%async_computation.2 | async-start | bytes 1572864 | tf_op jit(solution)/shard_map/all_to_all | solution.py:331
  98.7 12.0 %collective-permute-start.1 = (bf16[72,384]{1,0:T(8,128)(2,1)S(1)}, bf16[72,384]{1,0:T(8,128)(2,1)S(1)}, u32[]{:S(2)}, u32[]{:S(2)}) collective-permute-start(bf16[72,384]{1,0:T(8,128)(2,1)S(1)} %copy-done.6), channel_id=1, source_target_pairs={{0,256},{256,0},{1,257},{257,1},{2,258},{258,2},{3,259},{259,3},{4... | collective-permute-start | bytes 165896 | tf_op jit(solution)/shard_map/ppermute | solution.py:330

commit v11 on v10

--- a/solution.py
+++ b/solution.py
@@ -229,6 +229,14 @@
         input_output_aliases=aliases,
         name=name,
     )
+
+
+def exchange(x):
+    groups = []
+    for core in range(2):
+        for first in range(2 * core, 16 + 2 * core, NZ):
+            groups.append([(half * 16 + (first + i) % 16) * 2 + core for half in range(2) for i in range(NZ)])
+    return lax.all_to_all(x, ("xh", "z1", "z0", "c"), 0, 0, tiled=True, axis_index_groups=groups)
 
 
 def shards(
@@ -296,7 +304,7 @@
         jnp.asarray(rows),
         jnp.asarray(cols),
     )
-    q = lax.all_to_all(q, ("xh", "z0"), 0, 0, tiled=True)
+    q = exchange(q)
     swap = [(0, 1), (1, 0)]
     got = lax.ppermute(send, "xh", swap)
     kv = call(
@@ -318,7 +326,7 @@
         VMEM(),
         "attend",
     )(xh[None], z0[None], text_len, q, kv)
-    out = lax.all_to_all(out, ("xh", "z0"), 0, 0, tiled=True)
+    out = exchange(out)
     part = call(
         project_kernel,
         jax.ShapeDtypeStruct((2, 8, TQ, W), BF),

time: 114 us -> 112 us (0.982)
  blocking collectives: 30.5 us -> 35.4 us
  starting transfers between devices: 49.2 us -> 44.4 us
  waiting for transfers between devices: 19.3 us -> 17.2 us
    all_gather x1, blocking collectives: 30.5 us -> 35.4 us  [shards(): kv = lax.all_gather(kv, 'z1', axis=0)]
    all_to_all x1, starting transfers between devices: 8.93 us -> 5.94 us  [shards(): lax.all_to_all(part.reshape(16, TQ, W), ('g', 'y', 'c'), 0, 0, tiled=True)]
    all_to_all x2, waiting for transfers between devices: 11.7 us -> 9.61 us  [exchange(): lax.all_to_all(x, ('xh', 'z1', 'z0', 'c'), 0, 0, tiled=True, axis_index_g...]
    all_to_all x2, starting transfers between devices: 31.5 us -> 29.7 us  [exchange(): lax.all_to_all(x, ('xh', 'z1', 'z0', 'c'), 0, 0, tiled=True, axis_index_g...]
where the time goes in v11:
time: 112 us; the launch traced here: 111 us
  starting transfers between devices  44.4 us (40%)
  blocking collectives  35.4 us (32%)
  waiting for transfers between devices  17.2 us (15%)
  Pallas kernels  11.2 us (10%)
  between operations  1.5 us (1%)
    all_gather x1, blocking collectives, shards(): kv = lax.all_gather(kv, 'z1', axis=0)  35.4 us
    all_to_all x2, starting transfers between devices, exchange(): lax.all_to_all(x, ('xh', 'z1', 'z0', 'c'), 0, 0, tiled=True, axis_index_g...  29.7 us
    all_to_all x2, waiting for transfers between devices, exchange(): lax.all_to_all(x, ('xh', 'z1', 'z0', 'c'), 0, 0, tiled=True, axis_index_g...  9.61 us
    ppermute x1, waiting for transfers between devices, shards(): side = lax.ppermute(side, 'g', swap)  6.63 us
    all_to_all x1, starting transfers between devices, shards(): lax.all_to_all(part.reshape(16, TQ, W), ('g', 'y', 'c'), 0, 0, tiled=True)  5.94 us
    ppermute x1, starting transfers between devices, shards(): got = lax.ppermute(send, 'xh', swap)  5.48 us
    pallas_call x1, Pallas kernels, shards(): call(attend_kernel, pltpu.HBM((NS, TQ + STAT, W), BF), [SMEM()] * 3 + [VM...  3.95 us
    ppermute x1, starting transfers between devices, shards(): side = lax.ppermute(side, 'g', swap)  3.3 us
  transfers between devices with their start and end apart: 5, of which 3 were waited for; matrix products, arithmetic and copies ran while one was open for 1% of the time, Pallas kernels for 1%

profile of v11, /device:TPU:1, one launch (start us, length us, event | category | flops | bytes accessed | tf_op | source)
XLA Modules:
  0.0 111.1 jit_solution(4717366826115144268)
XLA Ops:
  0.6 3.1 %prepare.1 = (bf16[2,2,80,384]{3,2,1,0:T(8,128)(2,1)}, bf16[2,80,384]{2,1,0:T(8,128)(2,1)}, bf16[8,64,384]{2,1,0:T(8,128)(2,1)}, bf16[72,384]{1,0:T(8,128)(2,1)}) custom-call(s32[1]{0:T(128)} %bitcast.4.seq_id, s32[1]{0:T(128)} %bitcast.2.xh_id, s32[1]{0:T(128)} %bitcast.guide_id.ids, bf16[2,64,384]{2,1,0:T(8,128)(2,1)} %bitcast.20, ...), custom_call_target="tpu_custom_call" | custom-call | tf_op jit(solution)/shard_map/prepare/pallas_call | solution.py:265
  3.8 5.5 %collective-permute-start = (bf16[2,80,384]{2,1,0:T(8,128)(2,1)}, bf16[2,80,384]{2,1,0:T(8,128)(2,1)S(1)}, u32[]{:S(2)}, u32[]{:S(2)}) collective-permute-start(bf16[2,80,384]{2,1,0:T(8,128)(2,1)} %get-tuple-element.8), channel_id=1, source_target_pairs={{0,128},{128,0},{1,129},{129,1},{2,130},{130,2},{3,131},{131,3},{4... | collective-permute-start | bytes 368648 | tf_op jit(solution)/shard_map/ppermute | solution.py:309
  9.3 13.7 %all-to-all-start = ((bf16[8,64,384]{2,1,0:T(8,128)(2,1)}), bf16[8,64,384]{2,1,0:T(8,128)(2,1)}, u32[]{:S(2)}, u32[]{:S(2)}) async-start(bf16[8,64,384]{2,1,0:T(8,128)(2,1)} %get-tuple-element.6), calls=%async_computation | async-start | bytes 786432 | tf_op jit(solution)/shard_map/all_to_all | solution.py:239
  22.9 0.0 collective-permute-done.got_hbm
  22.9 0.0 copy-start.4
  22.9 0.7 join.1
  23.6 0.0 copy-start
  23.6 35.4 %all-gather = bf16[8,2,80,384]{3,2,1,0:T(8,128)(2,1)S(1)} all-gather(bf16[2,2,80,384]{3,2,1,0:T(8,128)(2,1)} %join.1), channel_id=2, replica_groups=mesh['g'=2,'xh'=2,'z1'=4,'z0'=4,'y'=4,'c'=2] {'z1'}, dimensions={0}, use_global_device_ids=true | all-gather | bytes 1228800 | tf_op jit(solution)/shard_map/all_gather | solution.py:320
  59.0 0.0 all-to-all-done.q_ref
  59.0 0.0 copy-done.4
  59.0 3.9 %attend.1 = bf16[8,72,384]{2,1,0:T(8,128)(2,1)} custom-call(s32[1]{0:T(128)} %bitcast.2.xh_id, s32[1]{0:T(128)} %bitcast.3.z0_id, s32[2]{0:T(128)S(1)} %copy-done.4, bf16[8,64,384]{2,1,0:T(8,128)(2,1)} %all-to-all-done.q_ref, bf16[4,2,2,80,384]{4,3,2,1,0:T(8,128)(2,1)S(1)} %bitcast.15), custom_call_target="tpu_custom_call" | custom-call | tf_op jit(solution)/shard_map/attend/pallas_call | solution.py:322
  62.9 16.0 %all-to-all-start.1 = ((bf16[8,72,384]{2,1,0:T(8,128)(2,1)}), bf16[8,72,384]{2,1,0:T(8,128)(2,1)S(1)}, u32[]{:S(2)}, u32[]{:S(2)}) async-start(bf16[8,72,384]{2,1,0:T(8,128)(2,1)} %attend.1), calls=%async_computation.1 | async-start | bytes 884736 | tf_op jit(solution)/shard_map/all_to_all | solution.py:239
  79.0 9.6 %all-to-all-done.1.o_ref = bf16[8,72,384]{2,1,0:T(8,128)(2,1)S(1)} async-done(((bf16[8,72,384]{2,1,0:T(8,128)(2,1)}), bf16[8,72,384]{2,1,0:T(8,128)(2,1)S(1)}, u32[]{:S(2)}, u32[]{:S(2)}) %all-to-all-start.1) | async-done | bytes 442400 | tf_op jit(solution)/shard_map/all_to_all | solution.py:239
  88.6 0.0 copy-done
  88.6 0.0 copy-start.6
  88.6 0.0 copy-start.1
  88.6 0.0 copy-start.2
  88.6 0.0 copy-start.3
  88.6 2.1 %project.1 = bf16[2,8,64,384]{3,2,1,0:T(8,128)(2,1)} custom-call(s32[1]{0:T(128)} %bitcast.1.ids, bf16[8,72,384]{2,1,0:T(8,128)(2,1)S(1)} %all-to-all-done.1.o_ref, bf16[384,3072]{1,0:T(8,128)(2,1)S(1)} %copy-done), custom_call_target="tpu_custom_call" | custom-call | tf_op jit(solution)/shard_map/project/pallas_call | solution.py:330
  90.8 5.9 %all-to-all-start.2 = ((bf16[16,64,384]{2,1,0:T(8,128)(2,1)}), bf16[16,64,384]{2,1,0:T(8,128)(2,1)S(1)}, u32[]{:S(2)}, u32[]{:S(2)}) async-start(bf16[16,64,384]{2,1,0:T(8,128)(2,1)} %bitcast.14), calls=%async_computation.2 | async-start | bytes 1572864 | tf_op jit(solution)/shard_map/all_to_all | solution.py:339
  96.7 0.0 copy-done.6
  96.7 3.3 %collective-permute-start.1 = (bf16[72,384]{1,0:T(8,128)(2,1)S(1)}, bf16[72,384]{1,0:T(8,128)(2,1)S(1)}, u32[]{:S(2)}, u32[]{:S(2)}) collective-permute-start(bf16[72,384]{1,0:T(8,128)(2,1)S(1)} %copy-done.6), channel_id=1, source_target_pairs={{0,256},{256,0},{1,257},{257,1},{2,258},{258,2},{3,259},{259,3},{4... | collective-permute-start | bytes 165896 | tf_op jit(solution)/shard_map/ppermute | solution.py:338
  100.7 0.0 copy-done.7
  100.7 0.6 dynamic_slice.3
  101.4 0.7 pad_maximum_fusion.scal
  102.1 0.0 copy-done.5
  102.1 6.6 %collective-permute-done.1.side_ref = bf16[72,384]{1,0:T(8,128)(2,1)S(1)} collective-permute-done((bf16[72,384]{1,0:T(8,128)(2,1)S(1)}, bf16[72,384]{1,0:T(8,128)(2,1)S(1)}, u32[]{:S(2)}, u32[]{:S(2)}) %collective-permute-start.1) | collective-permute-done | bytes 55328 | tf_op jit(solution)/shard_map/ppermute | solution.py:338
  108.7 1.0 all-to-all-done.2.part_ref
  109.7 0.0 copy-done.1
  109.7 0.0 copy-done.2
  109.7 0.0 copy-done.3
  109.7 1.3 %finish.1 = (bf16[1,64,384]{2,1,0:T(8,128)(2,1)}, bf16[1,64,384]{2,1,0:T(8,128)(2,1)}) custom-call(s32[1]{0:T(128)} %bitcast.guide_id.ids, f32[2]{0:T(128)S(1)} %pad_maximum_fusion.scal, bf16[16,64,384]{2,1,0:T(8,128)(2,1)S(1)} %all-to-all-done.2.part_ref, bf16[2,64,384]{2,1,0:T(8,128)(2,1)S(1)} %bitcast.17, f32[2,384]{1,0:T(2,128)S(1)} %bitcast.19, ...), custom_call_target="tpu_custom_call" | custom-call | tf_op jit(solution)/shard_map/finish/pallas_call | solution.py:345
  (3 shorter events, 0.0 us)
Async XLA Ops:
  3.8 19.2 %collective-permute-start = (bf16[2,80,384]{2,1,0:T(8,128)(2,1)}, bf16[2,80,384]{2,1,0:T(8,128)(2,1)S(1)}, u32[]{:S(2)}, u32[]{:S(2)}) collective-permute-start(bf16[2,80,384]{2,1,0:T(8,128)(2,1)} %get-tuple-element.8), channel_id=1, source_target_pairs={{0,128},{128,0},{1,129},{129,1},{2,130},{130,2},{3,131},{131,3},{4... | collective-permute-start | bytes 368648 | tf_op jit(solution)/shard_map/ppermute | solution.py:309
  9.3 49.7 %all-to-all-start = ((bf16[8,64,384]{2,1,0:T(8,128)(2,1)}), bf16[8,64,384]{2,1,0:T(8,128)(2,1)}, u32[]{:S(2)}, u32[]{:S(2)}) async-start(bf16[8,64,384]{2,1,0:T(8,128)(2,1)} %get-tuple-element.6), calls=%async_computation | async-start | bytes 786432 | tf_op jit(solution)/shard_map/all_to_all | solution.py:239
  22.9 36.1 %copy-start.4 = (s32[2]{0:T(128)S(1)}, s32[2]{0:T(128)}, u32[]{:S(2)}) copy-start(s32[2]{0:T(128)} %len_ref.1) | copy-start | bytes 28
  23.6 65.0 %copy-start = (bf16[384,3072]{1,0:T(8,128)(2,1)S(1)}, bf16[384,3072]{1,0:T(8,128)(2,1)}, u32[]{:S(2)}) copy-start(bf16[384,3072]{1,0:T(8,128)(2,1)} %w_ref.1) | copy-start | bytes 7077892
  62.9 25.6 %all-to-all-start.1 = ((bf16[8,72,384]{2,1,0:T(8,128)(2,1)}), bf16[8,72,384]{2,1,0:T(8,128)(2,1)S(1)}, u32[]{:S(2)}, u32[]{:S(2)}) async-start(bf16[8,72,384]{2,1,0:T(8,128)(2,1)} %attend.1), calls=%async_computation.1 | async-start | bytes 884736 | tf_op jit(solution)/shard_map/all_to_all | solution.py:239
  88.6 8.1 %copy-start.6 = (bf16[72,384]{1,0:T(8,128)(2,1)S(1)}, bf16[72,384]{1,0:T(8,128)(2,1)}, u32[]{:S(2)}) copy-start(bf16[72,384]{1,0:T(8,128)(2,1)} %get-tuple-element.9) | copy-start | bytes 165892
  88.6 12.1 %copy-start.7 = (f32[2]{0:T(128)S(1)}, f32[2]{0:T(128)}, u32[]{:S(2)}) copy-start(f32[2]{0:T(128)} %param.28) | copy-start | bytes 28
  88.6 13.5 %copy-start.5 = (f32[384]{0:T(512)S(1)}, f32[384]{0:T(512)}, u32[]{:S(2)}) copy-start(f32[384]{0:T(512)} %param.27) | copy-start | bytes 4612
  88.6 21.1 %copy-start.1 = (bf16[1,2,64,384]{3,2,1,0:T(8,128)(2,1)S(1)}, bf16[1,2,64,384]{3,2,1,0:T(8,128)(2,1)}, u32[]{:S(2)}) copy-start(bf16[1,2,64,384]{3,2,1,0:T(8,128)(2,1)} %param.17) | copy-start | bytes 294916
  88.6 21.1 %copy-start.2 = (bf16[1,64,384]{2,1,0:T(8,128)(2,1)S(1)}, bf16[1,64,384]{2,1,0:T(8,128)(2,1)}, u32[]{:S(2)}) copy-start(bf16[1,64,384]{2,1,0:T(8,128)(2,1)} %lat_ref.1) | copy-start | bytes 147460
  88.6 21.1 %copy-start.3 = (f32[1,2,384]{2,1,0:T(2,128)S(1)}, f32[1,2,384]{2,1,0:T(2,128)}, u32[]{:S(2)}) copy-start(f32[1,2,384]{2,1,0:T(2,128)} %param.25) | copy-start | bytes 9220
  90.8 18.9 %all-to-all-start.2 = ((bf16[16,64,384]{2,1,0:T(8,128)(2,1)}), bf16[16,64,384]{2,1,0:T(8,128)(2,1)S(1)}, u32[]{:S(2)}, u32[]{:S(2)}) async-start(bf16[16,64,384]{2,1,0:T(8,128)(2,1)} %bitcast.14), calls=%async_computation.2 | async-start | bytes 1572864 | tf_op jit(solution)/shard_map/all_to_all | solution.py:339
  96.7 12.0 %collective-permute-start.1 = (bf16[72,384]{1,0:T(8,128)(2,1)S(1)}, bf16[72,384]{1,0:T(8,128)(2,1)S(1)}, u32[]{:S(2)}, u32[]{:S(2)}) collective-permute-start(bf16[72,384]{1,0:T(8,128)(2,1)S(1)} %copy-done.6), channel_id=1, source_target_pairs={{0,256},{256,0},{1,257},{257,1},{2,258},{258,2},{3,259},{259,3},{4... | collective-permute-start | bytes 165896 | tf_op jit(solution)/shard_map/ppermute | solution.py:338

commit v12 on v11

--- a/solution.py
+++ b/solution.py
@@ -75,8 +75,8 @@
 
 def prepare_kernel(
     seq_id, xh_id, guide_id, k_hbm, q_hbm, v_hbm, tk_hbm, tv_hbm, hid_hbm, gate_hbm, qg_hbm, kg_hbm, row_hbm, col_hbm,
-    keep_out, send_out, q_out, side_out,
-    k_ref, q_ref, v_ref, tk_ref, tv_ref, hid_ref, gate_ref, qg_ref, kg_ref, row_ref, col_ref, sems,
+    keep_out, send_out, q_hbm_out, side_out,
+    k_ref, q_ref, v_ref, tk_ref, tv_ref, hid_ref, gate_ref, qg_ref, kg_ref, row_ref, col_ref, q_out, sems, q_sems,
 ):
     other = 1 - guide_id[0]
     rows = row_hbm.at[:, pl.ds(seq_id[0], 1)]
@@ -90,12 +90,13 @@
     for copy in copies[:4]:
         copy.wait()
     table = rope_of(row_ref, col_ref)
+    sent = []
     for p in range(2):
         for h in range(HPD):
             hs = slice(h * HD, (h + 1) * HD)
-            q = rotated(normed(q_ref[p, :, hs], qg_ref[...]), table).astype(BF)
-            for z in range(NZ):
-                q_out[p * NZ + z, :, hs] = q
+            q_out[p, :, hs] = rotated(normed(q_ref[p, :, hs], qg_ref[...]), table).astype(BF)
+        slots = [p * NZ + z for z in range(NZ)]
+        sent += start_all([(q_out.at[p], q_hbm_out.at[d]) for d in slots], q_sems.at[pl.ds(p * NZ, NZ)])
     for copy in copies[4:7]:
         copy.wait()
     own = xh_id[0]
@@ -114,6 +115,8 @@
     rows = lax.broadcasted_iota(jnp.int32, (8, W), 0)
     packed = jnp.where(rows == 0, hi.astype(F32), jnp.where(rows == 1, mid.astype(F32), lo.astype(F32)))
     side_out[TQ : TQ + 8, :] = packed.astype(BF)
+    for copy in sent:
+        copy.wait()
 
 
 def join_kernel(kv_hbm, got_hbm, out_hbm, sem):
@@ -271,7 +274,7 @@
             jax.ShapeDtypeStruct((TQ + 8, W), BF),
         ),
         [SMEM()] * 3 + [HBM()] * 11,
-        (VMEM(),) * 4,
+        (VMEM(), VMEM(), HBM(), VMEM()),
         "prepare",
         [
             pltpu.VMEM((2, TQ, W), BF),
@@ -285,7 +288,9 @@
             pltpu.VMEM((2, HD), F32),
             pltpu.VMEM((2, 1, HD), F32),
             pltpu.VMEM((2, TQ, HD), F32),
+            pltpu.VMEM((2, TQ, W), BF),
             pltpu.SemaphoreType.DMA((11,)),
+            pltpu.SemaphoreType.DMA((NS,)),
         ],
         63 * 1024 * 1024,
     )(

time: 112 us -> 112 us (level)
  no operation moved by 1% of the time
where the time goes in v12:
time: 112 us; the launch traced here: 111 us
  starting transfers between devices  44.4 us (40%)
  blocking collectives  35.4 us (32%)
  waiting for transfers between devices  17.2 us (15%)
  Pallas kernels  11.2 us (10%)
  between operations  1.5 us (1%)
    all_gather x1, blocking collectives, shards(): kv = lax.all_gather(kv, 'z1', axis=0)  35.4 us
    all_to_all x2, starting transfers between devices, exchange(): lax.all_to_all(x, ('xh', 'z1', 'z0', 'c'), 0, 0, tiled=True, axis_index_g...  29.7 us
    all_to_all x2, waiting for transfers between devices, exchange(): lax.all_to_all(x, ('xh', 'z1', 'z0', 'c'), 0, 0, tiled=True, axis_index_g...  9.61 us
    ppermute x1, waiting for transfers between devices, shards(): side = lax.ppermute(side, 'g', swap)  6.63 us
    all_to_all x1, starting transfers between devices, shards(): lax.all_to_all(part.reshape(16, TQ, W), ('g', 'y', 'c'), 0, 0, tiled=True)  5.94 us
    ppermute x1, starting transfers between devices, shards(): got = lax.ppermute(send, 'xh', swap)  5.48 us
    pallas_call x1, Pallas kernels, shards(): call(attend_kernel, pltpu.HBM((NS, TQ + STAT, W), BF), [SMEM()] * 3 + [VM...  3.95 us
    ppermute x1, starting transfers between devices, shards(): side = lax.ppermute(side, 'g', swap)  3.3 us
  transfers between devices with their start and end apart: 5, of which 3 were waited for; matrix products, arithmetic and copies ran while one was open for 1% of the time, Pallas kernels for 1%

profile of v12, /device:TPU:1, one launch (start us, length us, event | category | flops | bytes accessed | tf_op | source)
XLA Modules:
  0.0 111.1 jit_solution(1147488278875752130)
XLA Ops:
  0.6 3.1 %prepare.1 = (bf16[2,2,80,384]{3,2,1,0:T(8,128)(2,1)}, bf16[2,80,384]{2,1,0:T(8,128)(2,1)}, bf16[8,64,384]{2,1,0:T(8,128)(2,1)}, bf16[72,384]{1,0:T(8,128)(2,1)}) custom-call(s32[1]{0:T(128)} %bitcast.4.seq_id, s32[1]{0:T(128)} %bitcast.2.xh_id, s32[1]{0:T(128)} %bitcast.guide_id.ids, bf16[2,64,384]{2,1,0:T(8,128)(2,1)} %bitcast.20, ...), custom_call_target="tpu_custom_call" | custom-call | tf_op jit(solution)/shard_map/prepare/pallas_call | solution.py:268
  3.8 5.5 %collective-permute-start = (bf16[2,80,384]{2,1,0:T(8,128)(2,1)}, bf16[2,80,384]{2,1,0:T(8,128)(2,1)S(1)}, u32[]{:S(2)}, u32[]{:S(2)}) collective-permute-start(bf16[2,80,384]{2,1,0:T(8,128)(2,1)} %get-tuple-element.8), channel_id=1, source_target_pairs={{0,128},{128,0},{1,129},{129,1},{2,130},{130,2},{3,131},{131,3},{4... | collective-permute-start | bytes 368648 | tf_op jit(solution)/shard_map/ppermute | solution.py:314
  9.3 13.7 %all-to-all-start = ((bf16[8,64,384]{2,1,0:T(8,128)(2,1)}), bf16[8,64,384]{2,1,0:T(8,128)(2,1)}, u32[]{:S(2)}, u32[]{:S(2)}) async-start(bf16[8,64,384]{2,1,0:T(8,128)(2,1)} %get-tuple-element.6), calls=%async_computation | async-start | bytes 786432 | tf_op jit(solution)/shard_map/all_to_all | solution.py:242
  22.9 0.0 collective-permute-done.got_hbm
  22.9 0.0 copy-start.4
  22.9 0.7 join.1
  23.6 0.0 copy-start
  23.6 35.4 %all-gather = bf16[8,2,80,384]{3,2,1,0:T(8,128)(2,1)S(1)} all-gather(bf16[2,2,80,384]{3,2,1,0:T(8,128)(2,1)} %join.1), channel_id=2, replica_groups=mesh['g'=2,'xh'=2,'z1'=4,'z0'=4,'y'=4,'c'=2] {'z1'}, dimensions={0}, use_global_device_ids=true | all-gather | bytes 1228800 | tf_op jit(solution)/shard_map/all_gather | solution.py:325
  59.0 0.0 all-to-all-done.q_ref
  59.0 0.0 copy-done.4
  59.0 3.9 %attend.1 = bf16[8,72,384]{2,1,0:T(8,128)(2,1)} custom-call(s32[1]{0:T(128)} %bitcast.2.xh_id, s32[1]{0:T(128)} %bitcast.3.z0_id, s32[2]{0:T(128)S(1)} %copy-done.4, bf16[8,64,384]{2,1,0:T(8,128)(2,1)} %all-to-all-done.q_ref, bf16[4,2,2,80,384]{4,3,2,1,0:T(8,128)(2,1)S(1)} %bitcast.15), custom_call_target="tpu_custom_call" | custom-call | tf_op jit(solution)/shard_map/attend/pallas_call | solution.py:327
  62.9 16.0 %all-to-all-start.1 = ((bf16[8,72,384]{2,1,0:T(8,128)(2,1)}), bf16[8,72,384]{2,1,0:T(8,128)(2,1)S(1)}, u32[]{:S(2)}, u32[]{:S(2)}) async-start(bf16[8,72,384]{2,1,0:T(8,128)(2,1)} %attend.1), calls=%async_computation.1 | async-start | bytes 884736 | tf_op jit(solution)/shard_map/all_to_all | solution.py:242
  79.0 9.6 %all-to-all-done.1.o_ref = bf16[8,72,384]{2,1,0:T(8,128)(2,1)S(1)} async-done(((bf16[8,72,384]{2,1,0:T(8,128)(2,1)}), bf16[8,72,384]{2,1,0:T(8,128)(2,1)S(1)}, u32[]{:S(2)}, u32[]{:S(2)}) %all-to-all-start.1) | async-done | bytes 442400 | tf_op jit(solution)/shard_map/all_to_all | solution.py:242
  88.6 0.0 copy-done
  88.6 0.0 copy-start.6
  88.6 0.0 copy-start.1
  88.6 0.0 copy-start.2
  88.6 0.0 copy-start.3
  88.6 2.1 %project.1 = bf16[2,8,64,384]{3,2,1,0:T(8,128)(2,1)} custom-call(s32[1]{0:T(128)} %bitcast.1.ids, bf16[8,72,384]{2,1,0:T(8,128)(2,1)S(1)} %all-to-all-done.1.o_ref, bf16[384,3072]{1,0:T(8,128)(2,1)S(1)} %copy-done), custom_call_target="tpu_custom_call" | custom-call | tf_op jit(solution)/shard_map/project/pallas_call | solution.py:335
  90.8 5.9 %all-to-all-start.2 = ((bf16[16,64,384]{2,1,0:T(8,128)(2,1)}), bf16[16,64,384]{2,1,0:T(8,128)(2,1)S(1)}, u32[]{:S(2)}, u32[]{:S(2)}) async-start(bf16[16,64,384]{2,1,0:T(8,128)(2,1)} %bitcast.14), calls=%async_computation.2 | async-start | bytes 1572864 | tf_op jit(solution)/shard_map/all_to_all | solution.py:344
  96.7 0.0 copy-done.6
  96.7 3.3 %collective-permute-start.1 = (bf16[72,384]{1,0:T(8,128)(2,1)S(1)}, bf16[72,384]{1,0:T(8,128)(2,1)S(1)}, u32[]{:S(2)}, u32[]{:S(2)}) collective-permute-start(bf16[72,384]{1,0:T(8,128)(2,1)S(1)} %copy-done.6), channel_id=1, source_target_pairs={{0,256},{256,0},{1,257},{257,1},{2,258},{258,2},{3,259},{259,3},{4... | collective-permute-start | bytes 165896 | tf_op jit(solution)/shard_map/ppermute | solution.py:343
  100.7 0.0 copy-done.7
  100.7 0.6 dynamic_slice.3
  101.4 0.7 pad_maximum_fusion.scal
  102.1 0.0 copy-done.5
  102.1 6.6 %collective-permute-done.1.side_ref = bf16[72,384]{1,0:T(8,128)(2,1)S(1)} collective-permute-done((bf16[72,384]{1,0:T(8,128)(2,1)S(1)}, bf16[72,384]{1,0:T(8,128)(2,1)S(1)}, u32[]{:S(2)}, u32[]{:S(2)}) %collective-permute-start.1) | collective-permute-done | bytes 55328 | tf_op jit(solution)/shard_map/ppermute | solution.py:343
  108.7 1.0 all-to-all-done.2.part_ref
  109.7 0.0 copy-done.1
  109.7 0.0 copy-done.2
  109.7 0.0 copy-done.3
  109.7 1.3 %finish.1 = (bf16[1,64,384]{2,1,0:T(8,128)(2,1)}, bf16[1,64,384]{2,1,0:T(8,128)(2,1)}) custom-call(s32[1]{0:T(128)} %bitcast.guide_id.ids, f32[2]{0:T(128)S(1)} %pad_maximum_fusion.scal, bf16[16,64,384]{2,1,0:T(8,128)(2,1)S(1)} %all-to-all-done.2.part_ref, bf16[2,64,384]{2,1,0:T(8,128)(2,1)S(1)} %bitcast.17, f32[2,384]{1,0:T(2,128)S(1)} %bitcast.19, ...), custom_call_target="tpu_custom_call" | custom-call | tf_op jit(solution)/shard_map/finish/pallas_call | solution.py:350
  (3 shorter events, 0.0 us)
Async XLA Ops:
  3.8 19.2 %collective-permute-start = (bf16[2,80,384]{2,1,0:T(8,128)(2,1)}, bf16[2,80,384]{2,1,0:T(8,128)(2,1)S(1)}, u32[]{:S(2)}, u32[]{:S(2)}) collective-permute-start(bf16[2,80,384]{2,1,0:T(8,128)(2,1)} %get-tuple-element.8), channel_id=1, source_target_pairs={{0,128},{128,0},{1,129},{129,1},{2,130},{130,2},{3,131},{131,3},{4... | collective-permute-start | bytes 368648 | tf_op jit(solution)/shard_map/ppermute | solution.py:314
  9.3 49.7 %all-to-all-start = ((bf16[8,64,384]{2,1,0:T(8,128)(2,1)}), bf16[8,64,384]{2,1,0:T(8,128)(2,1)}, u32[]{:S(2)}, u32[]{:S(2)}) async-start(bf16[8,64,384]{2,1,0:T(8,128)(2,1)} %get-tuple-element.6), calls=%async_computation | async-start | bytes 786432 | tf_op jit(solution)/shard_map/all_to_all | solution.py:242
  22.9 36.1 %copy-start.4 = (s32[2]{0:T(128)S(1)}, s32[2]{0:T(128)}, u32[]{:S(2)}) copy-start(s32[2]{0:T(128)} %len_ref.1) | copy-start | bytes 28
  23.6 65.0 %copy-start = (bf16[384,3072]{1,0:T(8,128)(2,1)S(1)}, bf16[384,3072]{1,0:T(8,128)(2,1)}, u32[]{:S(2)}) copy-start(bf16[384,3072]{1,0:T(8,128)(2,1)} %w_ref.1) | copy-start | bytes 7077892
  62.9 25.6 %all-to-all-start.1 = ((bf16[8,72,384]{2,1,0:T(8,128)(2,1)}), bf16[8,72,384]{2,1,0:T(8,128)(2,1)S(1)}, u32[]{:S(2)}, u32[]{:S(2)}) async-start(bf16[8,72,384]{2,1,0:T(8,128)(2,1)} %attend.1), calls=%async_computation.1 | async-start | bytes 884736 | tf_op jit(solution)/shard_map/all_to_all | solution.py:242
  88.6 8.1 %copy-start.6 = (bf16[72,384]{1,0:T(8,128)(2,1)S(1)}, bf16[72,384]{1,0:T(8,128)(2,1)}, u32[]{:S(2)}) copy-start(bf16[72,384]{1,0:T(8,128)(2,1)} %get-tuple-element.9) | copy-start | bytes 165892
  88.6 12.1 %copy-start.7 = (f32[2]{0:T(128)S(1)}, f32[2]{0:T(128)}, u32[]{:S(2)}) copy-start(f32[2]{0:T(128)} %param.28) | copy-start | bytes 28
  88.6 13.5 %copy-start.5 = (f32[384]{0:T(512)S(1)}, f32[384]{0:T(512)}, u32[]{:S(2)}) copy-start(f32[384]{0:T(512)} %param.27) | copy-start | bytes 4612
  88.6 21.1 %copy-start.1 = (bf16[1,2,64,384]{3,2,1,0:T(8,128)(2,1)S(1)}, bf16[1,2,64,384]{3,2,1,0:T(8,128)(2,1)}, u32[]{:S(2)}) copy-start(bf16[1,2,64,384]{3,2,1,0:T(8,128)(2,1)} %param.17) | copy-start | bytes 294916
  88.6 21.1 %copy-start.2 = (bf16[1,64,384]{2,1,0:T(8,128)(2,1)S(1)}, bf16[1,64,384]{2,1,0:T(8,128)(2,1)}, u32[]{:S(2)}) copy-start(bf16[1,64,384]{2,1,0:T(8,128)(2,1)} %lat_ref.1) | copy-start | bytes 147460
  88.6 21.1 %copy-start.3 = (f32[1,2,384]{2,1,0:T(2,128)S(1)}, f32[1,2,384]{2,1,0:T(2,128)}, u32[]{:S(2)}) copy-start(f32[1,2,384]{2,1,0:T(2,128)} %param.25) | copy-start | bytes 9220
  90.8 18.9 %all-to-all-start.2 = ((bf16[16,64,384]{2,1,0:T(8,128)(2,1)}), bf16[16,64,384]{2,1,0:T(8,128)(2,1)S(1)}, u32[]{:S(2)}, u32[]{:S(2)}) async-start(bf16[16,64,384]{2,1,0:T(8,128)(2,1)} %bitcast.14), calls=%async_computation.2 | async-start | bytes 1572864 | tf_op jit(solution)/shard_map/all_to_all | solution.py:344
  96.7 12.0 %collective-permute-start.1 = (bf16[72,384]{1,0:T(8,128)(2,1)S(1)}, bf16[72,384]{1,0:T(8,128)(2,1)S(1)}, u32[]{:S(2)}, u32[]{:S(2)}) collective-permute-start(bf16[72,384]{1,0:T(8,128)(2,1)S(1)} %copy-done.6), channel_id=1, source_target_pairs={{0,256},{256,0},{1,257},{257,1},{2,258},{258,2},{3,259},{259,3},{4... | collective-permute-start | bytes 165896 | tf_op jit(solution)/shard_map/ppermute | solution.py:343
